TPU v7x, 512 devices: a whole 4x4x16 slice. The times are simulated.
512 devices in a mesh: slab: 128 (over x, z, core), sub: 4 (over y).
Axes of the slice: x: 4, y: 4, z: 16, core: 2. Of those that a mesh axis runs over, the one named last changes fastest.
Arguments:
- ensemble: float32 [2, 15, 80, 65536], P(None, None, None, ('slab', 'sub')), may hold values from -6 to 6
- obs_value: float32 [2, 256], replicated, may hold values from -6 to 6
- obs_var: float32 [2, 256], replicated, may hold values from 0.5 to 4
- obs_owner: int32 [2, 256, 1], replicated, may hold values from 0 to 127; in each aligned block of 256 rows (0 to 255, 256 to 511, ..., all dimensions but the last counted through in order) at most 8 rows name the same one
- obs_column: int32 [2, 256], replicated, may hold values from 0 to 511
- home_block: int32 [2, 256], replicated, may hold values from -1 to 1
- batch_order: int32 [2], replicated, may hold values from 0 to 1, each once
Outputs:
- analysis: float32 [2, 15, 80, 65536], P(None, None, None, ('slab', 'sub'))
- assimilated_priors: float32 [2, 256, 160], replicated
Inputs may be any that keep to these rules, and one draw needn't show every extreme that they name: `obs_owner`: in each batch no slab owns more than 8 observations; in some batch one slab owns exactly 8. `batch_order`: each batch appears once.
All inputs are finite; a program needn't handle non-finite values.
Results may differ from a plain program's by a relative error of at most 0.00012.
Values sent between devices are 32-bit elements; how exact they have to be, the bound alone decides.
A program may use at most 64 MiB of HBM per device.

v0:
```python
import jax
import jax.numpy as jnp
from jax import lax
from jax.sharding import PartitionSpec as P

BANDS = 2
BLK = 16
BATCHES = 2
CAP = 8


HIGHEST = lax.Precision.HIGHEST


def gc_weight(first, second, nblocks, length):
    block_gap = jnp.abs(first - second)
    block_gap = jnp.minimum(block_gap, nblocks - block_gap)
    scaled_gap = block_gap.astype(jnp.float32) / length
    near_part = (
        ((-0.25 * scaled_gap + 0.5) * scaled_gap + 0.625) * scaled_gap**3
        - 5.0 / 3.0 * scaled_gap**2
        + 1.0
    )
    floored = jnp.maximum(scaled_gap, 1.0)
    far_part = (
        (
            (((scaled_gap / 12.0 - 0.5) * scaled_gap + 0.625) * scaled_gap + 5.0 / 3.0) * scaled_gap
            - 5.0
        )
        * scaled_gap
        + 4.0
        - 2.0 / (3.0 * floored)
    )
    return jnp.where(scaled_gap <= 1.0, near_part, jnp.where(scaled_gap < 2.0, far_part, 0.0))


def obs_statistics(current, values, variances, members):
    banded = current.reshape(current.shape[0], BANDS, members)
    whole_obs = jnp.sum(banded, axis=1)
    centre = jnp.mean(whole_obs, axis=1, keepdims=True)
    spread = jnp.sum((whole_obs - centre) ** 2, axis=1) / (members - 1) + 1e-06
    post_var = 1.0 / (1.0 / spread + 1.0 / variances)
    post_mean = post_var * (centre[:, 0] / spread + values / variances)
    increments = (post_mean - centre[:, 0])[:, None] + (jnp.sqrt(post_var / spread) - 1.0)[
        :, None
    ] * (whole_obs - centre)
    deviations = banded - jnp.mean(banded, axis=2, keepdims=True)
    return (deviations, spread, increments)


def update_pool(prior_pool, pool_homes, deviations, spread, increments, obs_homes, nblocks, decays):
    members = deviations.shape[2]
    banded = prior_pool.reshape(prior_pool.shape[0], prior_pool.shape[1], BANDS, members)
    new_bands = []
    for band_no in range(BANDS):
        pool_band = banded[:, :, band_no, :]
        pool_dev = pool_band - jnp.mean(pool_band, axis=2, keepdims=True)
        weights = (
            gc_weight(pool_homes[:, :, None], obs_homes[None, None, :], nblocks, decays[band_no])
            / ((members - 1) * spread)[None, None, :]
        )
        crossed = jnp.einsum("bpm,km->bpk", pool_dev, deviations[:, band_no, :], precision=HIGHEST)
        change = jnp.einsum("bpk,km->bpm", crossed * weights, increments, precision=HIGHEST)
        new_bands.append(pool_band + change)
    return jnp.stack(new_bands, axis=2).reshape(prior_pool.shape)


def update_state(ensemble, my_cols, deviations, spread, increments, obs_homes, nblocks, decays):
    members = ensemble.shape[2]
    new_bands = []
    for band_no in range(BANDS):
        band_layer = ensemble[band_no]
        layer_dev = band_layer - jnp.mean(band_layer, axis=1, keepdims=True)
        obs_dev = deviations[:, band_no, :]
        weights = (
            gc_weight((my_cols // BLK)[:, None], obs_homes[None, :], nblocks, decays[band_no])
            / ((members - 1) * spread)[None, :]
        )

        def one_level(level_dev):
            crossed = jnp.einsum("mc,km->ck", level_dev, obs_dev, precision=HIGHEST)
            return jnp.einsum("ck,km->mc", crossed * weights, increments, precision=HIGHEST)

        change = lax.map(one_level, layer_dev)
        new_bands.append(band_layer + change)
    return jnp.stack(new_bands, axis=0)


def slot_table(owners, slot_rank, slab_number, capacity):
    obs_count = owners.shape[1]
    matches = (owners == slab_number)[:, None, :] & (
        slot_rank[:, None, :] == jnp.arange(capacity, dtype=jnp.int32)[None, :, None]
    )
    slot_obs = jnp.sum(
        jnp.where(matches, jnp.arange(obs_count, dtype=jnp.int32)[None, None, :], 0), axis=2
    )
    slot_valid = jnp.any(matches, axis=2)
    return (slot_obs, slot_valid)


def per_device(ensemble, obs_value, obs_var, obs_owner, obs_column, home_block, batch_order):
    members = ensemble.shape[2]
    levels_count = ensemble.shape[1]
    cols_dev = ensemble.shape[3]
    slab_count = lax.axis_size("slab")
    sub_count = lax.axis_size("sub")
    slab_index = lax.axis_index("slab")
    sub_index = lax.axis_index("sub")
    obs_batch = obs_value.shape[1]
    capacity = CAP
    cols_slab = cols_dev * sub_count
    nblocks = cols_slab * slab_count // BLK
    span_broad = cols_slab // (4 * BLK)
    span_narrow = max(span_broad // 4, 1)
    decays = (float(span_broad), float(span_narrow))
    owners = obs_owner[:, :, 0]
    obs_home = jnp.mod((owners * cols_slab + obs_column) // BLK + home_block, nblocks)
    onehot = (owners[:, :, None] == jnp.arange(slab_count, dtype=jnp.int32)[None, None, :]).astype(
        jnp.int32
    )
    running = jnp.cumsum(onehot, axis=1) - 1
    slot_rank = jnp.sum(onehot * running, axis=2)
    slot_global = owners * capacity + slot_rank
    slot_obs, slot_valid = slot_table(owners, slot_rank, slab_index, capacity)
    slot_column = jnp.take_along_axis(obs_column, slot_obs, axis=1)
    slot_level = slot_obs % levels_count
    holder = slot_column // cols_dev
    local_col = slot_column % cols_dev
    picked = ensemble[:, slot_level, :, local_col]
    retain = slot_valid & (holder == sub_index)
    picked = jnp.where(retain[:, :, None, None], picked, 0.0).reshape(
        BATCHES, capacity, BANDS * members
    )
    slot_priors = lax.psum(picked, "sub")
    slot_homes = jnp.take_along_axis(obs_home, slot_obs, axis=1)
    my_cols = (slab_index * sub_count + sub_index) * cols_dev + jnp.arange(
        cols_dev, dtype=jnp.int32
    )
    recorded = jnp.zeros((BATCHES, obs_batch, BANDS * members), jnp.float32)
    for step_no in range(BATCHES):
        batch_id = batch_order[step_no]
        own_slots = slot_priors[batch_id]
        values = obs_value[batch_id]
        variances = obs_var[batch_id]
        obs_homes = obs_home[batch_id]
        gathered = lax.all_gather(own_slots, "slab", axis=0, tiled=True)
        current = gathered[slot_global[batch_id]]
        live = jnp.ones((obs_batch,), jnp.bool_)
        recorded = recorded.at[batch_id].set(current)
        deviations, spread, increments = obs_statistics(current, values, variances, members)
        increments = jnp.where(live[:, None], increments, 0.0)
        slot_priors = update_pool(
            slot_priors, slot_homes, deviations, spread, increments, obs_homes, nblocks, decays
        )
        ensemble = update_state(
            ensemble, my_cols, deviations, spread, increments, obs_homes, nblocks, decays
        )
    return (ensemble, recorded)


def solution(mesh):
    placed = (P(None, None, None, ("slab", "sub")), P(), P(), P(), P(), P(), P())
    return jax.shard_map(
        per_device,
        mesh=mesh,
        in_specs=placed,
        out_specs=(P(None, None, None, ("slab", "sub")), P()),
        check_vma=False,
    )
```

profile of v0, /device:TPU:1, one launch (start us, length us, event | category | flops | bytes accessed | tf_op | source)
XLA Modules:
  0.0 351.5 jit_solution(10229613459352276190)
XLA Ops:
  5.6 14.3 %psum.7 = f32[2,8,160]{2,1,0:T(8,128)S(1)} all-reduce(f32[2,8,160]{2,1,0:T(8,128)S(1)} %broadcast_select_fusion), channel_id=1, replica_groups=mesh['slab'=128,'sub'=4] {'sub'}, use_global_device_ids=true, to_apply=%region_6.8 | all-reduce | flops 2560 | bytes 20480 | tf_op jit(solution)/shard_map/psum | solution.py:134
  22.5 111.6 %all-gather = f32[1,1024,160]{2,1,0:T(8,128)S(1)} all-gather(f32[1,8,160]{2,1,0:T(8,128)S(1)} %constant_dynamic-slice_fusion.9), channel_id=2, replica_groups=mesh['slab'=128,'sub'=4] {'slab'}, dimensions={1}, use_global_device_ids=true | all-gather | bytes 660480 | tf_op jit(solution)/shard_map/all_gather | solution.py:146
  139.6 99.9 %all-gather.1 = f32[1,1024,160]{2,1,0:T(8,128)S(1)} all-gather(f32[1,8,160]{2,1,0:T(8,128)S(1)} %constant_dynamic-slice_fusion.4), channel_id=3, replica_groups=mesh['slab'=128,'sub'=4] {'slab'}, dimensions={1}, use_global_device_ids=true | all-gather | bytes 660480 | tf_op jit(solution)/shard_map/all_gather | solution.py:146
  245.5 24.5 %while.48 = (s32[]{:T(128)}, f32[15,80,128]{2,1,0:T(8,128)S(1)}, f32[15,80,128]{2,1,0:T(8,128)}, f32[256,80]{1,0:T(8,128)S(1)}, f32[256,80]{1,0:T(8,128)S(1)}, /...) while((s32[]{:T(128)}, f32[15,80,128]{2,1,0:T(8,128)S(1)}, ...), condition=%wide.region_24.26_spmd.clone, body=%wide.region_23.25_spmd.clone.sunk | while | flops 64094208 | bytes 560225 | solution.py:84
  245.5 1.2 convolution_multiply_fusion.12
  247.2 1.2 convolution_multiply_fusion.12
  248.8 1.2 convolution_multiply_fusion.12
  250.4 1.2 convolution_multiply_fusion.12
  252.1 1.2 convolution_multiply_fusion.12
  253.7 1.2 convolution_multiply_fusion.12
  255.3 1.2 convolution_multiply_fusion.12
  257.0 1.2 convolution_multiply_fusion.12
  258.6 1.2 convolution_multiply_fusion.12
  260.2 1.2 convolution_multiply_fusion.12
  261.9 1.2 convolution_multiply_fusion.12
  263.5 1.2 convolution_multiply_fusion.12
  265.1 1.2 convolution_multiply_fusion.12
  266.8 1.2 convolution_multiply_fusion.12
  268.4 1.2 convolution_multiply_fusion.12
  270.8 26.6 %while.46 = (s32[]{:T(128)}, f32[15,80,128]{2,1,0:T(8,128)S(1)}, f32[15,80,128]{2,1,0:T(8,128)S(1)}, f32[256,80]{1,0:T(8,128)}, f32[256,80]{1,0:T(8,128)S(1)}, /...) while((s32[]{:T(128)}, f32[15,80,128]{2,1,0:T(8,128)S(1)}, ...), condition=%wide.region_12.14_spmd.clone, body=%wide.region_11.13_spmd.clone.sunk | while | flops 64094208 | bytes 559717 | solution.py:84
  270.8 1.4 convolution_multiply_fusion.10
  272.6 1.4 convolution_multiply_fusion.10
  274.4 1.4 convolution_multiply_fusion.10
  276.2 1.4 convolution_multiply_fusion.10
  277.9 1.4 convolution_multiply_fusion.10
  279.7 1.4 convolution_multiply_fusion.10
  281.5 1.4 convolution_multiply_fusion.10
  283.3 1.4 convolution_multiply_fusion.10
  285.0 1.4 convolution_multiply_fusion.10
  286.8 1.4 convolution_multiply_fusion.10
  288.6 1.4 convolution_multiply_fusion.10
  290.3 1.4 convolution_multiply_fusion.10
  292.1 1.4 convolution_multiply_fusion.10
  293.9 1.4 convolution_multiply_fusion.10
  295.7 1.4 convolution_multiply_fusion.10
  299.0 24.5 %while.49 = (s32[]{:T(128)}, f32[15,80,128]{2,1,0:T(8,128)S(1)}, f32[15,80,128]{2,1,0:T(8,128)}, f32[256,80]{1,0:T(8,128)S(1)}, f32[256,80]{1,0:T(8,128)S(1)}, /...) while((s32[]{:T(128)}, f32[15,80,128]{2,1,0:T(8,128)S(1)}, ...), condition=%wide.region_27.29_spmd.clone, body=%wide.region_26.28_spmd.clone.sunk | while | flops 64094208 | bytes 560225 | solution.py:84
  300.6 1.2 convolution_multiply_fusion.13
  302.3 1.2 convolution_multiply_fusion.13
  303.9 1.2 convolution_multiply_fusion.13
  305.5 1.2 convolution_multiply_fusion.13
  307.2 1.2 convolution_multiply_fusion.13
  310.4 1.2 convolution_multiply_fusion.13
  312.1 1.2 convolution_multiply_fusion.13
  315.3 1.2 convolution_multiply_fusion.13
  317.0 1.2 convolution_multiply_fusion.13
  320.3 1.2 convolution_multiply_fusion.13
  321.9 1.2 convolution_multiply_fusion.13
  324.4 24.6 %while.47 = (s32[]{:T(128)}, f32[15,80,128]{2,1,0:T(8,128)S(1)}, f32[15,80,128]{2,1,0:T(8,128)}, f32[256,80]{1,0:T(8,128)S(1)}, f32[256,80]{1,0:T(8,128)S(1)}, /...) while((s32[]{:T(128)}, f32[15,80,128]{2,1,0:T(8,128)S(1)}, ...), condition=%wide.region_21.23_spmd.clone, body=%wide.region_20.22_spmd.clone.sunk | while | flops 64094208 | bytes 560225 | solution.py:84
  324.4 1.2 convolution_multiply_fusion.11
  326.0 1.2 convolution_multiply_fusion.11
  327.7 1.2 convolution_multiply_fusion.11
  329.3 1.2 convolution_multiply_fusion.11
  331.0 1.2 convolution_multiply_fusion.11
  332.6 1.2 convolution_multiply_fusion.11
  334.2 1.2 convolution_multiply_fusion.11
  335.9 1.2 convolution_multiply_fusion.11
  337.5 1.2 convolution_multiply_fusion.11
  339.2 1.2 convolution_multiply_fusion.11
  340.8 1.2 convolution_multiply_fusion.11
  342.4 1.2 convolution_multiply_fusion.11
  344.1 1.2 convolution_multiply_fusion.11
  345.7 1.2 convolution_multiply_fusion.11
  347.3 1.2 convolution_multiply_fusion.11
  349.0 1.3 add_bitcast_fusion.1
  (188 shorter events, 46.3 us)
Async XLA Ops:
  0.6 1.6 copy-start.3
  0.6 2.1 copy-start
  2.0 1.8 copy-start.1
  3.8 16.2 %copy-start.4 = (s32[2]{0:T(128)S(1)}, s32[2]{0:T(128)}, u32[]{:S(2)}) copy-start(s32[2]{0:T(128)} %param.27) | copy-start | bytes 28
  4.8 131.3 %copy-start.5 = (s32[2,256]{1,0:T(2,128)S(1)}, s32[2,256]{1,0:T(2,128)}, u32[]{:S(2)}) copy-start(s32[2,256]{1,0:T(2,128)} %param.26) | copy-start | bytes 6148
  136.2 1.3 copy-start.6
  136.2 1.3 copy-start.7
  137.5 2.0 copy-start.8
  137.8 101.7 %copy-start.10 = (s32[1,256]{1,0:T(1,128)}, s32[1,256]{1,0:T(1,128)S(1)}, u32[]{:S(2)}) copy-start(s32[1,256]{1,0:T(1,128)S(1)} %get-tuple-element.436) | copy-start | bytes 3076
  239.5 1.0 copy-start.12
  244.5 1.0 copy-start.9
  244.5 1.0 copy-start.11
  270.0 0.8 copy-start.13
  297.7 1.3 copy-start.14
  323.5 0.8 copy-start.2
where the time goes:
time: 355 us; the launch traced here: 352 us
  blocking collectives  226 us (64%)
  matrix products  99.2 us (28%)
  local copies, waits for them, and re-layouts  10.4 us (3%)
  other arithmetic  9.13 us (3%)
  between operations  5.16 us (1%)
    all_gather x2, blocking collectives, per_device(): gathered = lax.all_gather(own_slots, 'slab', axis=0, tiled=True)  212 us
    dot_general x60, matrix products, one_level(): crossed = jnp.einsum('mc,km->ck', level_dev, obs_dev, precision=HIGHEST)  76 us
    dot_general x60, matrix products, one_level(): jnp.einsum('ck,km->mc', crossed * weights, increments, precision=HIGHEST)  22.5 us
    psum x1, blocking collectives, per_device(): slot_priors = lax.psum(picked, 'sub')  14.3 us

commit v1 on v0

--- a/solution.py
+++ b/solution.py
@@ -48,24 +48,24 @@
     return (deviations, spread, increments)
 
 
-def update_pool(prior_pool, pool_homes, deviations, spread, increments, obs_homes, nblocks, decays):
+def update_pool(pool, pool_homes, deviations, spread, increments, obs_homes, nblocks, decays):
     members = deviations.shape[2]
-    banded = prior_pool.reshape(prior_pool.shape[0], prior_pool.shape[1], BANDS, members)
+    banded = pool.reshape(pool.shape[0], BANDS, members)
     new_bands = []
     for band_no in range(BANDS):
-        pool_band = banded[:, :, band_no, :]
-        pool_dev = pool_band - jnp.mean(pool_band, axis=2, keepdims=True)
+        pool_band = banded[:, band_no, :]
+        pool_dev = pool_band - jnp.mean(pool_band, axis=1, keepdims=True)
         weights = (
-            gc_weight(pool_homes[:, :, None], obs_homes[None, None, :], nblocks, decays[band_no])
-            / ((members - 1) * spread)[None, None, :]
+            gc_weight(pool_homes[:, None], obs_homes[None, :], nblocks, decays[band_no])
+            / ((members - 1) * spread)[None, :]
         )
-        crossed = jnp.einsum("bpm,km->bpk", pool_dev, deviations[:, band_no, :], precision=HIGHEST)
-        change = jnp.einsum("bpk,km->bpm", crossed * weights, increments, precision=HIGHEST)
+        crossed = jnp.einsum("pm,km->pk", pool_dev, deviations[:, band_no, :], precision=HIGHEST)
+        change = jnp.einsum("pk,km->pm", crossed * weights, increments, precision=HIGHEST)
         new_bands.append(pool_band + change)
-    return jnp.stack(new_bands, axis=2).reshape(prior_pool.shape)
+    return jnp.stack(new_bands, axis=1).reshape(pool.shape)
 
 
-def update_state(ensemble, my_cols, deviations, spread, increments, obs_homes, nblocks, decays):
+def update_state(ensemble, my_cols, deviations, spread, increments, obs_homes, valid, nblocks, decays):
     members = ensemble.shape[2]
     new_bands = []
     for band_no in range(BANDS):
@@ -76,12 +76,9 @@
             gc_weight((my_cols // BLK)[:, None], obs_homes[None, :], nblocks, decays[band_no])
             / ((members - 1) * spread)[None, :]
         )
-
-        def one_level(level_dev):
-            crossed = jnp.einsum("mc,km->ck", level_dev, obs_dev, precision=HIGHEST)
-            return jnp.einsum("ck,km->mc", crossed * weights, increments, precision=HIGHEST)
-
-        change = lax.map(one_level, layer_dev)
+        weights = jnp.where(valid[None, :], weights, 0.0)
+        crossed = jnp.einsum("lmc,km->lck", layer_dev, obs_dev, precision=HIGHEST)
+        change = jnp.einsum("lck,km->lmc", crossed * weights[None], increments, precision=HIGHEST)
         new_bands.append(band_layer + change)
     return jnp.stack(new_bands, axis=0)
 
@@ -106,13 +103,13 @@
     sub_count = lax.axis_size("sub")
     slab_index = lax.axis_index("slab")
     sub_index = lax.axis_index("sub")
-    obs_batch = obs_value.shape[1]
     capacity = CAP
     cols_slab = cols_dev * sub_count
     nblocks = cols_slab * slab_count // BLK
     span_broad = cols_slab // (4 * BLK)
     span_narrow = max(span_broad // 4, 1)
     decays = (float(span_broad), float(span_narrow))
+    assert 2 * span_broad + 1 <= cols_slab // BLK and slab_count >= 3
     owners = obs_owner[:, :, 0]
     obs_home = jnp.mod((owners * cols_slab + obs_column) // BLK + home_block, nblocks)
     onehot = (owners[:, :, None] == jnp.arange(slab_count, dtype=jnp.int32)[None, None, :]).astype(
@@ -131,29 +128,38 @@
     picked = jnp.where(retain[:, :, None, None], picked, 0.0).reshape(
         BATCHES, capacity, BANDS * members
     )
-    slot_priors = lax.psum(picked, "sub")
-    slot_homes = jnp.take_along_axis(obs_home, slot_obs, axis=1)
+    slab_slots = jnp.sum(lax.all_gather(picked, "sub", axis=0), axis=0)
+    gathered = lax.all_gather(slab_slots, "slab", axis=1, tiled=True)
+    priors = jnp.take_along_axis(gathered, slot_global[:, :, None], axis=1)
+
+    first, second = batch_order[0], batch_order[1]
+    y0 = priors[first]
+    stats0 = obs_statistics(y0, obs_value[first], obs_var[first], members)
+    y1 = update_pool(priors[second], obs_home[second], *stats0, obs_home[first], nblocks, decays)
+    stats1 = obs_statistics(y1, obs_value[second], obs_var[second], members)
+    recorded = jnp.zeros_like(priors).at[first].set(y0).at[second].set(y1)
+
     my_cols = (slab_index * sub_count + sub_index) * cols_dev + jnp.arange(
         cols_dev, dtype=jnp.int32
     )
-    recorded = jnp.zeros((BATCHES, obs_batch, BANDS * members), jnp.float32)
-    for step_no in range(BATCHES):
-        batch_id = batch_order[step_no]
-        own_slots = slot_priors[batch_id]
-        values = obs_value[batch_id]
-        variances = obs_var[batch_id]
-        obs_homes = obs_home[batch_id]
-        gathered = lax.all_gather(own_slots, "slab", axis=0, tiled=True)
-        current = gathered[slot_global[batch_id]]
-        live = jnp.ones((obs_batch,), jnp.bool_)
-        recorded = recorded.at[batch_id].set(current)
-        deviations, spread, increments = obs_statistics(current, values, variances, members)
-        increments = jnp.where(live[:, None], increments, 0.0)
-        slot_priors = update_pool(
-            slot_priors, slot_homes, deviations, spread, increments, obs_homes, nblocks, decays
-        )
+    near = [jnp.mod(slab_index + d, slab_count) for d in (-1, 0, 1)]
+    for batch_id, stats in ((first, stats0), (second, stats1)):
+        deviations, spread, increments = stats
+        b_owners = lax.dynamic_index_in_dim(owners, batch_id, keepdims=True)
+        b_rank = lax.dynamic_index_in_dim(slot_rank, batch_id, keepdims=True)
+        tables = [slot_table(b_owners, b_rank, n, capacity) for n in near]
+        idx = jnp.concatenate([t[0][0] for t in tables])
+        valid = jnp.concatenate([t[1][0] for t in tables])
         ensemble = update_state(
-            ensemble, my_cols, deviations, spread, increments, obs_homes, nblocks, decays
+            ensemble,
+            my_cols,
+            deviations[idx],
+            spread[idx],
+            increments[idx],
+            obs_home[batch_id][idx],
+            valid,
+            nblocks,
+            decays,
         )
     return (ensemble, recorded)
 

time: 355 us -> 195 us (0.55)
  blocking collectives: 226 us -> 10.3 us
  waiting for transfers between devices: 0 us -> 133 us
  matrix products: 99.2 us -> 7.03 us
  between operations: 5.16 us -> 18.4 us
  local copies, waits for them, and re-layouts: 10.4 us -> 18 us
    all_gather x2 -> x1, blocking collectives: 212 us -> 10.3 us  [per_device(): slab_slots = jnp.sum(lax.all_gather(picked, 'sub', axis=0), axis=0)]
    all_gather x0 -> x1, waiting for transfers between devices: none -> 133 us  [per_device(): gathered = lax.all_gather(slab_slots, 'slab', axis=1, tiled=True)]
    dot_general x124 -> x12, matrix products: 99.2 us -> 7.03 us  [the longest x4 2.78 us: update_state(): jnp.einsum('lck,km->lmc', crossed * weights[None], increments, precision=...]
    psum x1 -> x0, blocking collectives: 14.3 us -> none  [per_device(): slot_priors = lax.psum(picked, 'sub')]
    gather x6 -> x10, local copies, waits for them, and re-layouts: 2.92 us -> 11.5 us  [the longest x2 6.32 us: per_device(): priors = jnp.take_along_axis(gathered, slot_global[:, :, None], axis=1)]
  transfers between devices with their start and end apart: 0 -> 1, of which waited for: 0 -> 1; matrix products, arithmetic and copies ran while one was open for 0% -> 2% of each run, Pallas kernels for 0% -> 0%
where the time goes in v1:
time: 195 us; the launch traced here: 194 us
  waiting for transfers between devices  133 us (68%)
  between operations  18.4 us (9%)
  local copies, waits for them, and re-layouts  18 us (9%)
  blocking collectives  10.3 us (5%)
  other arithmetic  7.86 us (4%)
  matrix products  7.03 us (4%)
    all_gather x1, waiting for transfers between devices, per_device(): gathered = lax.all_gather(slab_slots, 'slab', axis=1, tiled=True)  133 us
    all_gather x1, blocking collectives, per_device(): slab_slots = jnp.sum(lax.all_gather(picked, 'sub', axis=0), axis=0)  10.3 us
    gather x2, local copies, waits for them, and re-layouts, per_device(): priors = jnp.take_along_axis(gathered, slot_global[:, :, None], axis=1)  6.32 us
  transfers between devices with their start and end apart: 1, of which 1 were waited for; matrix products, arithmetic and copies ran while one was open for 2% of the time, Pallas kernels for 0%

profile of v1, /device:TPU:1, one launch (start us, length us, event | category | flops | bytes accessed | tf_op | source)
XLA Modules:
  0.0 194.4 jit_solution(9131951338326680747)
XLA Ops:
  7.2 0.7 copy.71
  7.9 0.7 broadcast_compare_fusion
  8.6 0.8 copy.45
  9.4 0.4 fusion.29
  9.9 0.1 add_add_fusion
  10.1 0.2 fusion.30
  10.3 0.2 select_reduce_fusion
  10.5 0.2 fusion.42
  10.6 0.1 reshape.1818
  10.7 0.7 gather_fusion.9
  11.4 0.1 reshape.1821
  11.5 0.1 gather.40
  11.6 0.1 reshape.1748
  11.7 1.0 copy.47
  12.8 0.6 gather_fusion
  13.4 0.1 gather.42
  13.6 10.3 %all_gather.6 = f32[4,2,8,160]{3,2,1,0:T(8,128)S(1)} all-gather(f32[1,2,8,160]{3,2,1,0:T(8,128)S(1)} %broadcast_select_fusion.1), channel_id=1, replica_groups=mesh['slab'=128,'sub'=4] {'sub'}, dimensions={0}, use_global_device_ids=true | all-gather | bytes 51200 | tf_op jit(solution)/shard_map/all_gather | solution.py:131
  23.9 0.6 reduce_sum.213
  24.6 0.6 fusion.104
  29.1 0.2 select_reduce_fusion.6
  29.2 0.2 select_reduce_fusion.3
  29.4 0.1 fusion.96
  29.5 0.7 gather_fusion.3
  30.2 0.7 gather_fusion.7
  31.0 0.2 fusion.76
  31.2 0.1 pad_add_fusion
  31.2 0.1 pad_add_fusion.1
  31.4 0.7 and_reduce_fusion
  32.1 0.1 slice_reduce_fusion.1
  32.2 132.7 %all-gather.2.cloned.1.call-done = f32[2,1024,160]{2,1,0:T(8,128)} async-done(((f32[2,8,160]{2,1,0:T(8,128)}), f32[2,1024,160]{2,1,0:T(8,128)}) %all-gather.2.cloned.1.call-update) | async-done | bytes 1310736 | tf_op jit(solution)/shard_map/all_gather | solution.py:132
  164.9 6.2 %gather_fusion.10 = f32[512,160]{1,0:T(8,128)S(1)} fusion(f32[2,1024,160]{2,1,0:T(8,128)} %all-gather.2.cloned.1.call-done, s32[512]{0:T(512)S(1)} %bitcast.158), kind=kCustom, calls=%fused_computation.10 | custom fusion | bytes 659456 | tf_op jit(solution)/shard_map/jit(take_along_axis)/gather | solution.py:133
  171.1 0.2 copy.48
  171.3 0.7 select_dynamic-update-slice_fusion
  172.1 0.1 copy.51
  172.2 0.1 copy.50
  172.4 0.3 broadcast_subtract_fusion
  172.7 0.2 fusion.101
  172.9 0.6 gather_fusion.2
  173.6 0.1 copy.49
  173.7 0.2 multiply_reduce_fusion
  173.9 0.2 multiply_add_fusion
  174.1 0.6 gather_fusion.1
  174.7 0.8 convolution_multiply_fusion
  175.4 0.4 convolution_add_fusion
  175.8 0.7 gather_fusion.4
  176.5 0.8 convolution_multiply_fusion.1
  177.3 0.4 fusion.100
  177.8 0.7 gather_fusion.8
  178.5 0.1 fusion.54
  178.7 0.5 convolution_multiply_fusion.5
  179.2 0.7 fusion.106
  180.0 0.1 copy.54
  180.1 0.6 gather_fusion.6
  180.7 0.1 copy.53
  180.8 0.6 gather_fusion.5
  181.4 0.5 convolution_multiply_fusion.3
  181.9 0.7 fusion.105
  182.6 0.5 convolution_multiply_fusion.4
  183.1 0.7 fusion.4
  183.8 0.5 convolution_multiply_fusion.2
  184.3 0.7 fusion.1
  185.0 1.2 pad_maximum_fusion
  186.2 0.6 constant_dynamic-update-slice_fusion
  186.8 0.7 copy-done.2
  (61 shorter events, 0.8 us)
Async XLA Ops:
  7.2 3.6 %copy-start = (s32[2,256]{1,0:T(2,128)S(1)}, s32[2,256]{1,0:T(2,128)}, u32[]{:S(2)}) copy-start(s32[2,256]{1,0:T(2,128)} %param.15) | copy-start | bytes 6148
  7.2 157.8 %all-gather.2.cloned.1.call-start = ((), (), s32[]{:S(2)}) async-start(), calls=%async_computation | async-start | bytes 2113536 | tf_op jit(solution)/shard_map/all_gather | solution.py:132
  9.9 1.8 copy-start.1
  11.7 12.8 %copy-start.4 = (s32[2]{0:T(128)S(1)}, s32[2]{0:T(128)}, u32[]{:S(2)}) copy-start(s32[2]{0:T(128)} %param.17) | copy-start | bytes 28
  11.7 16.0 %copy-start.3 = (s32[2,256,1]{1,2,0:T(1,128)S(1)}, s32[2,256,1]{1,2,0:T(1,128)}, u32[]{:S(2)}) copy-start(s32[2,256,1]{1,2,0:T(1,128)} %param.14) | copy-start | bytes 6148
  11.7 17.8 %copy-start.5 = (s32[2,256]{1,0:T(2,128)S(1)}, s32[2,256]{1,0:T(2,128)}, u32[]{:S(2)}) copy-start(s32[2,256]{1,0:T(2,128)} %param.16) | copy-start | bytes 6148
  12.8 18.6 %copy-start.6 = (f32[2,256]{1,0:T(2,128)S(1)}, f32[2,256]{1,0:T(2,128)}, u32[]{:S(2)}) copy-start(f32[2,256]{1,0:T(2,128)} %param.12) | copy-start | bytes 6148
  12.8 18.5 %copy-start.7 = (f32[2,256]{1,0:T(2,128)S(1)}, f32[2,256]{1,0:T(2,128)}, u32[]{:S(2)}) copy-start(f32[2,256]{1,0:T(2,128)} %param.13) | copy-start | bytes 6148
  12.8 18.6 %copy-start.8 = (s32[3]{0:T(128)S(1)}, s32[3]{0:T(128)}, u32[]{:S(2)}) copy-start(s32[3]{0:T(128)} %constant.306.clone.1) | copy-start | bytes 40
  186.8 0.7 copy-start.2
Sparse Core Ops, SparseCore 0:
  24.7 140.2 all-gather.1

commit v2 on v1

--- a/solution.py
+++ b/solution.py
@@ -1,7 +1,13 @@
+import functools
+
 import jax
 import jax.numpy as jnp
 from jax import lax
+from jax.experimental import pallas as pl
+from jax.experimental.pallas import tpu as pltpu
 from jax.sharding import PartitionSpec as P
+
+MESH = pl.DeviceIdType.MESH
 
 BANDS = 2
 BLK = 16
@@ -93,6 +99,122 @@
     )
     slot_valid = jnp.any(matches, axis=2)
     return (slot_obs, slot_valid)
+
+
+def gather_kernel(n_row, picked_ref, out_ref, part_ref, sem0, send0, sem_a, send_a, sem_b, send_b, sem_c, send_c):
+    n_slab = lax.axis_size("slab")
+    n_sub = lax.axis_size("sub")
+    s = lax.axis_index("slab")
+    u = lax.axis_index("sub")
+    n_rows = n_slab // n_row
+    row, loc = s // n_row, s % n_row
+    q_rows = out_ref.shape[2]
+
+    def copy(src, dst, send, recv, dev):
+        return pltpu.make_async_remote_copy(
+            src_ref=src, dst_ref=dst, send_sem=send, recv_sem=recv, device_id=dev, device_id_type=MESH
+        )
+
+    def to_sub(d):
+        q = (u + d) % n_sub
+        return copy(
+            picked_ref.at[q], part_ref.at[u], send0.at[q], sem0.at[u], (s, q)
+        )
+
+    def from_sub(d):
+        q = (u + d) % n_sub
+        return copy(
+            picked_ref.at[q], part_ref.at[q], send0.at[q], sem0.at[q], (s, q)
+        )
+
+    for d in range(1, n_sub):
+        to_sub(d).start()
+    total = picked_ref[u]
+    for d in range(1, n_sub):
+        from_sub(d).wait_recv()
+        total = total + part_ref[(u + d) % n_sub]
+    out_ref[u, s] = total
+
+    def to_a(d):
+        j = (loc + d) % n_row
+        return copy(out_ref.at[u, s], out_ref.at[u, s], send_a.at[j], sem_a.at[loc], (row * n_row + j, u))
+
+    def from_a(d):
+        j = (loc + d) % n_row
+        src = row * n_row + j
+        return copy(out_ref.at[u, src], out_ref.at[u, src], send_a.at[j], sem_a.at[j], (src, u))
+
+    def start_a(d, c):
+        to_a(d).start()
+        return c
+
+    def wait_a(d, c):
+        from_a(d).wait_recv()
+        return c
+
+    lax.fori_loop(1, n_row, start_a, 0)
+    lax.fori_loop(1, n_row, wait_a, 0)
+
+    def block(r):
+        return out_ref.at[u, pl.ds(r * n_row, n_row)]
+
+    def to_b(d):
+        r = (row + d) % n_rows
+        return copy(block(row), block(row), send_b.at[r], sem_b.at[row], (r * n_row + loc, u))
+
+    def from_b(d):
+        r = (row + d) % n_rows
+        return copy(block(r), block(r), send_b.at[r], sem_b.at[r], (r * n_row + loc, u))
+
+    for d in range(1, n_rows):
+        to_b(d).start()
+    for d in range(1, n_rows):
+        from_b(d).wait_recv()
+
+    def to_c(d):
+        q = (u + d) % n_sub
+        return copy(out_ref.at[u], out_ref.at[u], send_c.at[q], sem_c.at[u], (s, q))
+
+    def from_c(d):
+        q = (u + d) % n_sub
+        return copy(out_ref.at[q], out_ref.at[q], send_c.at[q], sem_c.at[q], (s, q))
+
+    for d in range(1, n_sub):
+        to_c(d).start()
+    for d in range(1, n_sub):
+        from_c(d).wait_recv()
+
+    for d in range(1, n_sub):
+        to_sub(d).wait_send()
+    lax.fori_loop(1, n_row, lambda d, c: (to_a(d).wait_send(), c)[1], 0)
+    for d in range(1, n_rows):
+        to_b(d).wait_send()
+    for d in range(1, n_sub):
+        to_c(d).wait_send()
+
+
+def gather_slots(picked, n_slab, n_sub, n_row):
+    rows, width = picked.shape
+    q_rows = rows // n_sub
+    n_rows = n_slab // n_row
+    return pl.pallas_call(
+        functools.partial(gather_kernel, n_row),
+        out_shape=jax.ShapeDtypeStruct((n_sub, n_slab, q_rows, width), jnp.float32),
+        in_specs=[pl.BlockSpec(memory_space=pltpu.VMEM)],
+        out_specs=pl.BlockSpec(memory_space=pltpu.VMEM),
+        scratch_shapes=[
+            pltpu.VMEM((n_sub, q_rows, width), jnp.float32),
+            pltpu.SemaphoreType.DMA((n_sub,)),
+            pltpu.SemaphoreType.DMA((n_sub,)),
+            pltpu.SemaphoreType.DMA((n_row,)),
+            pltpu.SemaphoreType.DMA((n_row,)),
+            pltpu.SemaphoreType.DMA((n_rows,)),
+            pltpu.SemaphoreType.DMA((n_rows,)),
+            pltpu.SemaphoreType.DMA((n_sub,)),
+            pltpu.SemaphoreType.DMA((n_sub,)),
+        ],
+        compiler_params=pltpu.CompilerParams(has_side_effects=True),
+    )(picked.reshape(n_sub, q_rows, width))
 
 
 def per_device(ensemble, obs_value, obs_var, obs_owner, obs_column, home_block, batch_order):
@@ -126,11 +248,14 @@
     picked = ensemble[:, slot_level, :, local_col]
     retain = slot_valid & (holder == sub_index)
     picked = jnp.where(retain[:, :, None, None], picked, 0.0).reshape(
-        BATCHES, capacity, BANDS * members
-    )
-    slab_slots = jnp.sum(lax.all_gather(picked, "sub", axis=0), axis=0)
-    gathered = lax.all_gather(slab_slots, "slab", axis=1, tiled=True)
-    priors = jnp.take_along_axis(gathered, slot_global[:, :, None], axis=1)
+        BATCHES * capacity, BANDS * members
+    )
+    n_row = 32 if slab_count % 32 == 0 else slab_count
+    gathered = gather_slots(picked, slab_count, sub_count, n_row)
+    q_rows = gathered.shape[2]
+    row_of = jnp.arange(BATCHES, dtype=jnp.int32)[:, None] * capacity + slot_rank
+    flat = (row_of // q_rows) * (slab_count * q_rows) + owners * q_rows + row_of % q_rows
+    priors = jnp.take(gathered.reshape(-1, BANDS * members), flat, axis=0)
 
     first, second = batch_order[0], batch_order[1]
     y0 = priors[first]

time: 195 us -> 116 us (0.59)
  waiting for transfers between devices: 133 us -> 0 us
  Pallas kernels: 0 us -> 80.1 us
  between operations: 18.4 us -> 5.13 us
  blocking collectives: 10.3 us -> 0 us
  local copies, waits for them, and re-layouts: 18 us -> 15.9 us
    all_gather x1 -> x0, waiting for transfers between devices: 133 us -> none  [per_device(): gathered = lax.all_gather(slab_slots, 'slab', axis=1, tiled=True)]
    pallas_call x0 -> x1, Pallas kernels: none -> 80.1 us  [gather_slots(): pl.pallas_call(functools.partial(gather_kernel, n_row), out_shape=jax.Sha...]
    all_gather x1 -> x0, blocking collectives: 10.3 us -> none  [per_device(): slab_slots = jnp.sum(lax.all_gather(picked, 'sub', axis=0), axis=0)]
    gather x2, local copies, waits for them, and re-layouts: 6.32 us -> 3.47 us  [per_device(): priors = jnp.take(gathered.reshape(-1, BANDS * members), flat, axis=0)]
    reshape x0 -> x1, local copies, waits for them, and re-layouts: none -> 1.98 us  [per_device(): priors = jnp.take(gathered.reshape(-1, BANDS * members), flat, axis=0)]
  transfers between devices with their start and end apart: 1 -> 0, of which waited for: 1 -> 0; matrix products, arithmetic and copies ran while one was open for 2% -> 0% of each run, Pallas kernels for 0% -> 0%
where the time goes in v2:
time: 116 us
  Pallas kernels  80.1 us (69%)
  local copies, waits for them, and re-layouts  15.9 us (14%)
  other arithmetic  7.87 us (7%)
  matrix products  7.01 us (6%)
  between operations  5.13 us (4%)
    pallas_call x1, Pallas kernels, gather_slots(): pl.pallas_call(functools.partial(gather_kernel, n_row), out_shape=jax.Sha...  80.1 us
    gather x2, local copies, waits for them, and re-layouts, per_device(): priors = jnp.take(gathered.reshape(-1, BANDS * members), flat, axis=0)  3.47 us
    dot_general x4, matrix products, update_state(): jnp.einsum('lck,km->lmc', crossed * weights[None], increments, precision=...  2.76 us

profile of v2, /device:TPU:1, one launch (start us, length us, event | category | flops | bytes accessed | tf_op | source)
XLA Modules:
  0.0 116.1 jit_solution(1468698786047018179)
XLA Ops:
  0.7 0.7 broadcast_compare_fusion
  1.4 0.8 copy.46
  2.2 0.4 fusion.29
  2.7 0.1 add_add_fusion
  2.9 0.2 fusion.30
  3.1 0.2 select_reduce_fusion
  3.3 0.1 reshape.1946
  3.4 0.7 gather_fusion.10
  4.1 0.1 gather.42
  4.2 0.1 reduce_sum.205
  4.3 0.2 fusion.42
  4.4 0.1 reduce_or.66
  4.5 0.1 gather.43
  4.6 0.1 reshape.1868
  4.7 1.0 copy.48
  5.8 0.6 gather_fusion
  6.4 0.1 gather.45
  6.5 0.7 broadcast_select_fusion.1.picked_ref
  7.1 80.1 %shard_map.86 = f32[4,128,4,160]{3,2,1,0:T(4,128)} custom-call(f32[4,4,160]{2,1,0:T(4,128)} %broadcast_select_fusion.1.picked_ref), custom_call_target="tpu_custom_call" | custom-call | tf_op jit(solution)/shard_map/pallas_call | solution.py:200
  87.3 2.0 %reshape.1866 = f32[2048,160]{1,0:T(8,128)S(1)} reshape(f32[4,128,4,160]{3,2,1,0:T(4,128)} %shard_map.86) | data formatting | bytes 2621440 | tf_op jit(solution)/shard_map/reshape | solution.py:258
  89.3 0.1 compare_and_fusion
  89.4 2.2 %gather_fusion.1 = f32[512,160]{1,0:T(8,128)} fusion(f32[2048,160]{1,0:T(8,128)S(1)} %reshape.1866, s32[1024]{0:T(1024)S(1)} %pad_clamp_fusion.2), kind=kCustom, calls=%fused_computation.1 | custom fusion | bytes 657408 | tf_op jit(solution)/shard_map/jit(_take)/gather | solution.py:258
  91.6 1.2 %copy.49 = f32[2,256,160]{1,2,0:T(8,128)S(1)} copy(f32[2,256,160]{2,1,0:T(8,128)} %bitcast.160) | data formatting | bytes 655360 | tf_op jit(solution)/shard_map/jit(_take)/gather | solution.py:258
  93.0 0.6 fusion.109
  97.4 0.7 and_reduce_fusion
  98.2 0.6 select_dynamic-update-slice_fusion
  98.9 0.1 copy.50
  99.0 0.2 multiply_reduce_fusion
  99.3 0.1 copy.51
  99.4 0.2 copy.52
  99.6 0.3 broadcast_subtract_fusion
  99.9 0.2 fusion.106
  100.2 0.8 convolution_multiply_fusion.1
  101.0 0.2 multiply_add_fusion
  101.1 0.8 convolution_multiply_fusion
  101.9 0.4 convolution_add_fusion
  102.3 0.4 fusion.105
  102.7 0.7 constant_dynamic-update-slice_fusion
  103.5 0.2 fusion.76
  103.7 0.1 pad_add_fusion
  103.8 0.2 select_reduce_fusion.6
  104.0 0.2 select_reduce_fusion.3
  104.1 0.1 fusion.101
  104.2 0.7 gather_fusion.5
  105.1 0.7 gather_fusion.9
  105.8 0.7 gather_fusion.4
  106.5 0.7 gather_fusion.8
  107.2 0.1 fusion.54
  107.4 0.6 gather_fusion.3
  108.0 0.1 slice_reduce_fusion.1
  108.1 0.5 convolution_multiply_fusion.5
  108.6 0.6 gather_fusion.2
  109.2 0.7 fusion.111
  109.9 0.1 copy.55
  110.1 0.6 gather_fusion.7
  110.7 0.5 convolution_multiply_fusion.4
  111.2 0.1 copy.54
  111.3 0.6 gather_fusion.6
  111.9 0.7 fusion.4
  112.6 0.5 convolution_multiply_fusion.3
  113.1 0.7 fusion.110
  113.8 0.5 convolution_multiply_fusion.2
  114.3 0.7 fusion.1
  115.0 1.1 pad_maximum_fusion
  (61 shorter events, 0.7 us)
Async XLA Ops:
  0.6 2.2 %copy-start.3 = (s32[2,256,1]{1,2,0:T(1,128)S(1)}, s32[2,256,1]{1,2,0:T(1,128)}, u32[]{:S(2)}) copy-start(s32[2,256,1]{1,2,0:T(1,128)} %param.14) | copy-start | bytes 6148
  0.6 2.8 %copy-start = (s32[2,256]{1,0:T(2,128)S(1)}, s32[2,256]{1,0:T(2,128)}, u32[]{:S(2)}) copy-start(s32[2,256]{1,0:T(2,128)} %param.15) | copy-start | bytes 6148
  2.7 2.1 %copy-start.1 = (f32[2,15,80,128]{3,2,1,0:T(8,128)S(1)}, f32[2,15,80,128]{3,2,1,0:T(8,128)}, u32[]{:S(2)}) copy-start(f32[2,15,80,128]{3,2,1,0:T(8,128)} %param.11) | copy-start | bytes 3686404
  91.6 1.3 %copy-start.4 = (s32[2]{0:T(128)S(1)}, s32[2]{0:T(128)}, u32[]{:S(2)}) copy-start(s32[2]{0:T(128)} %param.17) | copy-start | bytes 28
  91.6 5.8 %copy-start.8 = (s32[3]{0:T(128)S(1)}, s32[3]{0:T(128)}, u32[]{:S(2)}) copy-start(s32[3]{0:T(128)} %constant.326.clone.1) | copy-start | bytes 40
  92.9 6.3 %copy-start.5 = (f32[2,256]{1,0:T(2,128)S(1)}, f32[2,256]{1,0:T(2,128)}, u32[]{:S(2)}) copy-start(f32[2,256]{1,0:T(2,128)} %param.12) | copy-start | bytes 6148
  92.9 6.3 %copy-start.6 = (f32[2,256]{1,0:T(2,128)S(1)}, f32[2,256]{1,0:T(2,128)}, u32[]{:S(2)}) copy-start(f32[2,256]{1,0:T(2,128)} %param.13) | copy-start | bytes 6148
  98.8 1.3 %copy-start.7 = (s32[2,256]{1,0:T(2,128)S(1)}, s32[2,256]{1,0:T(2,128)}, u32[]{:S(2)}) copy-start(s32[2,256]{1,0:T(2,128)} %param.16) | copy-start | bytes 6148
  103.4 4.6 %copy-start.2 = (f32[2,256,160]{1,2,0:T(8,128)}, f32[2,256,160]{1,2,0:T(8,128)S(1)}, u32[]{:S(2)}) copy-start(f32[2,256,160]{1,2,0:T(8,128)S(1)} %constant_dynamic-update-slice_fusion) | copy-start | bytes 983044

commit v3 on v2

--- a/solution.py
+++ b/solution.py
@@ -108,7 +108,6 @@
     u = lax.axis_index("sub")
     n_rows = n_slab // n_row
     row, loc = s // n_row, s % n_row
-    q_rows = out_ref.shape[2]
 
     def copy(src, dst, send, recv, dev):
         return pltpu.make_async_remote_copy(
@@ -117,32 +116,31 @@
 
     def to_sub(d):
         q = (u + d) % n_sub
-        return copy(
-            picked_ref.at[q], part_ref.at[u], send0.at[q], sem0.at[u], (s, q)
-        )
+        return copy(picked_ref.at[q], part_ref.at[u], send0.at[q], sem0.at[u], (s, q))
 
     def from_sub(d):
         q = (u + d) % n_sub
-        return copy(
-            picked_ref.at[q], part_ref.at[q], send0.at[q], sem0.at[q], (s, q)
-        )
+        return copy(picked_ref.at[q], part_ref.at[q], send0.at[q], sem0.at[q], (s, q))
 
     for d in range(1, n_sub):
         to_sub(d).start()
-    total = picked_ref[u]
+    total = picked_ref[pl.ds(u, 1), :]
     for d in range(1, n_sub):
         from_sub(d).wait_recv()
-        total = total + part_ref[(u + d) % n_sub]
-    out_ref[u, s] = total
+        total = total + part_ref[pl.ds((u + d) % n_sub, 1), :]
+    out_ref[u, pl.ds(s, 1), :] = total
+
+    def own(r):
+        return out_ref.at[u, pl.ds(r, 1)]
 
     def to_a(d):
         j = (loc + d) % n_row
-        return copy(out_ref.at[u, s], out_ref.at[u, s], send_a.at[j], sem_a.at[loc], (row * n_row + j, u))
+        return copy(own(s), own(s), send_a.at[j], sem_a.at[loc], (row * n_row + j, u))
 
     def from_a(d):
         j = (loc + d) % n_row
         src = row * n_row + j
-        return copy(out_ref.at[u, src], out_ref.at[u, src], send_a.at[j], sem_a.at[j], (src, u))
+        return copy(own(src), own(src), send_a.at[j], sem_a.at[j], (src, u))
 
     def start_a(d, c):
         to_a(d).start()
@@ -195,15 +193,15 @@
 
 def gather_slots(picked, n_slab, n_sub, n_row):
     rows, width = picked.shape
-    q_rows = rows // n_sub
+    lanes = rows // n_sub * width
     n_rows = n_slab // n_row
     return pl.pallas_call(
         functools.partial(gather_kernel, n_row),
-        out_shape=jax.ShapeDtypeStruct((n_sub, n_slab, q_rows, width), jnp.float32),
+        out_shape=jax.ShapeDtypeStruct((n_sub, n_slab, lanes), jnp.float32),
         in_specs=[pl.BlockSpec(memory_space=pltpu.VMEM)],
         out_specs=pl.BlockSpec(memory_space=pltpu.VMEM),
         scratch_shapes=[
-            pltpu.VMEM((n_sub, q_rows, width), jnp.float32),
+            pltpu.VMEM((n_sub, lanes), jnp.float32),
             pltpu.SemaphoreType.DMA((n_sub,)),
             pltpu.SemaphoreType.DMA((n_sub,)),
             pltpu.SemaphoreType.DMA((n_row,)),
@@ -214,7 +212,7 @@
             pltpu.SemaphoreType.DMA((n_sub,)),
         ],
         compiler_params=pltpu.CompilerParams(has_side_effects=True),
-    )(picked.reshape(n_sub, q_rows, width))
+    )(picked.reshape(n_sub, lanes))
 
 
 def per_device(ensemble, obs_value, obs_var, obs_owner, obs_column, home_block, batch_order):
@@ -252,7 +250,7 @@
     )
     n_row = 32 if slab_count % 32 == 0 else slab_count
     gathered = gather_slots(picked, slab_count, sub_count, n_row)
-    q_rows = gathered.shape[2]
+    q_rows = BATCHES * capacity // sub_count
     row_of = jnp.arange(BATCHES, dtype=jnp.int32)[:, None] * capacity + slot_rank
     flat = (row_of // q_rows) * (slab_count * q_rows) + owners * q_rows + row_of % q_rows
     priors = jnp.take(gathered.reshape(-1, BANDS * members), flat, axis=0)

time: 116 us -> 103 us (0.89)
  Pallas kernels: 80.1 us -> 67 us
    pallas_call x1, Pallas kernels: 80.1 us -> 67 us  [gather_slots(): pl.pallas_call(functools.partial(gather_kernel, n_row), out_shape=jax.Sha...]
where the time goes in v3:
time: 103 us
  Pallas kernels  67 us (65%)
  local copies, waits for them, and re-layouts  16.4 us (16%)
  other arithmetic  7.26 us (7%)
  matrix products  7.01 us (7%)
  between operations  5.13 us (5%)
    pallas_call x1, Pallas kernels, gather_slots(): pl.pallas_call(functools.partial(gather_kernel, n_row), out_shape=jax.Sha...  67 us
    gather x2, local copies, waits for them, and re-layouts, per_device(): priors = jnp.take(gathered.reshape(-1, BANDS * members), flat, axis=0)  3.47 us
    dot_general x4, matrix products, update_state(): jnp.einsum('lck,km->lmc', crossed * weights[None], increments, precision=...  2.76 us

profile of v3, /device:TPU:1, one launch (start us, length us, event | category | flops | bytes accessed | tf_op | source)
XLA Modules:
  0.0 102.8 jit_solution(10078215915483324891)
XLA Ops:
  0.6 0.0 copy-start.3
  0.7 0.7 broadcast_compare_fusion
  1.4 0.8 copy.52
  2.2 0.4 fusion.29
  2.7 0.1 add_add_fusion
  2.9 0.2 fusion.30
  3.1 0.2 select_reduce_fusion
  3.3 0.1 reshape.1944
  3.4 0.7 gather_fusion.10
  4.1 0.1 reshape.1947
  4.2 0.2 fusion.42
  4.4 0.1 gather.38
  4.5 0.1 reshape.1866
  4.6 1.0 %copy.54 = f32[2,15,80,128]{2,0,3,1:T(2,128)S(1)} copy(f32[2,15,80,128]{3,2,1,0:T(8,128)S(1)} %copy-done.1) | data formatting | bytes 2457600 | tf_op args[0]
  5.6 0.6 gather_fusion
  6.2 0.1 bitcast_select_fusion.2
  6.3 0.7 select_n.409.picked_ref
  7.0 67.0 %shard_map.86 = f32[4,128,640]{2,1,0:T(8,128)} custom-call(f32[4,640]{1,0:T(4,128)} %select_n.409.picked_ref), custom_call_target="tpu_custom_call" | custom-call | tf_op jit(solution)/shard_map/pallas_call | solution.py:198
  74.0 2.0 %reshape.1864 = f32[2048,160]{1,0:T(8,128)S(1)} reshape(f32[4,128,640]{2,1,0:T(8,128)} %shard_map.86) | data formatting | bytes 2621440 | tf_op jit(solution)/shard_map/reshape | solution.py:256
  76.0 0.1 compare_and_fusion
  76.1 2.2 %gather_fusion.1 = f32[512,160]{1,0:T(8,128)} fusion(f32[2048,160]{1,0:T(8,128)S(1)} %reshape.1864, s32[1024]{0:T(1024)S(1)} %pad_clamp_fusion.2), kind=kCustom, calls=%fused_computation.1 | custom fusion | bytes 657408 | tf_op jit(solution)/shard_map/jit(_take)/gather | solution.py:256
  78.4 1.2 %copy.57 = f32[2,256,160]{1,2,0:T(8,128)S(1)} copy(f32[2,256,160]{2,1,0:T(8,128)} %bitcast.162) | data formatting | bytes 655360 | tf_op jit(solution)/shard_map/jit(_take)/gather | solution.py:256
  79.7 0.6 fusion.105
  84.2 0.7 and_reduce_fusion
  84.9 0.6 select_dynamic-update-slice_fusion
  85.6 0.1 copy.58
  85.7 0.2 multiply_reduce_fusion
  86.0 0.1 copy.59
  86.1 0.2 copy.60
  86.3 0.3 broadcast_subtract_fusion
  86.6 0.2 fusion.102
  86.9 0.8 convolution_multiply_fusion.1
  87.7 0.2 multiply_add_fusion
  87.9 0.8 convolution_multiply_fusion
  88.6 0.4 convolution_add_fusion
  89.0 0.4 fusion.101
  89.5 0.7 constant_dynamic-update-slice_fusion
  90.3 0.2 fusion.76
  90.5 0.1 pad_add_fusion
  90.5 0.2 select_reduce_fusion.6
  90.7 0.2 select_reduce_fusion.3
  90.9 0.1 fusion.97
  90.9 0.7 gather_fusion.5
  91.7 0.1 pad_add_fusion.1
  91.8 0.7 gather_fusion.9
  92.5 0.7 gather_fusion.4
  93.2 0.7 gather_fusion.8
  94.0 0.1 fusion.54
  94.1 0.6 gather_fusion.3
  94.7 0.1 slice_reduce_fusion.1
  94.8 0.5 convolution_multiply_fusion.5
  95.3 0.6 gather_fusion.2
  95.9 0.7 fusion.107
  96.7 0.1 copy.63
  96.8 0.6 gather_fusion.7
  97.4 0.5 convolution_multiply_fusion.4
  97.9 0.1 copy.62
  98.0 0.6 gather_fusion.6
  98.6 0.7 fusion.4
  99.3 0.5 convolution_multiply_fusion.3
  99.8 0.7 fusion.106
  100.5 0.5 convolution_multiply_fusion.2
  101.0 0.7 fusion.1
  101.7 1.1 %pad_maximum_fusion = f32[2,15,80,128]{3,2,1,0:T(8,128)} fusion(f32[1,15,80,128]{3,2,1,0:T(8,128)S(1)} %fusion.1, f32[1,15,80,128]{3,2,1,0:T(8,128)S(1)} %fusion.4), kind=kLoop, calls=%fused_computation.21 | loop fusion | flops 307200 | bytes 2457600 | tf_op jit(solution)/shard_map/stack | solution.py:89
  (60 shorter events, 0.7 us)
Async XLA Ops:
  0.6 2.2 %copy-start.3 = (s32[2,256,1]{1,2,0:T(1,128)S(1)}, s32[2,256,1]{1,2,0:T(1,128)}, u32[]{:S(2)}) copy-start(s32[2,256,1]{1,2,0:T(1,128)} %param.14) | copy-start | bytes 6148
  0.6 2.8 %copy-start = (s32[2,256]{1,0:T(2,128)S(1)}, s32[2,256]{1,0:T(2,128)}, u32[]{:S(2)}) copy-start(s32[2,256]{1,0:T(2,128)} %param.15) | copy-start | bytes 6148
  2.7 1.9 %copy-start.1 = (f32[2,15,80,128]{3,2,1,0:T(8,128)S(1)}, f32[2,15,80,128]{3,2,1,0:T(8,128)}, u32[]{:S(2)}) copy-start(f32[2,15,80,128]{3,2,1,0:T(8,128)} %param.11) | copy-start | bytes 3686404
  78.4 1.3 %copy-start.4 = (s32[2]{0:T(128)S(1)}, s32[2]{0:T(128)}, u32[]{:S(2)}) copy-start(s32[2]{0:T(128)} %param.17) | copy-start | bytes 28
  78.4 5.8 %copy-start.8 = (s32[3]{0:T(128)S(1)}, s32[3]{0:T(128)}, u32[]{:S(2)}) copy-start(s32[3]{0:T(128)} %constant.326.clone.1) | copy-start | bytes 40
  79.6 6.3 %copy-start.5 = (f32[2,256]{1,0:T(2,128)S(1)}, f32[2,256]{1,0:T(2,128)}, u32[]{:S(2)}) copy-start(f32[2,256]{1,0:T(2,128)} %param.12) | copy-start | bytes 6148
  79.6 6.3 %copy-start.6 = (f32[2,256]{1,0:T(2,128)S(1)}, f32[2,256]{1,0:T(2,128)}, u32[]{:S(2)}) copy-start(f32[2,256]{1,0:T(2,128)} %param.13) | copy-start | bytes 6148
  85.6 1.3 %copy-start.7 = (s32[2,256]{1,0:T(2,128)S(1)}, s32[2,256]{1,0:T(2,128)}, u32[]{:S(2)}) copy-start(s32[2,256]{1,0:T(2,128)} %param.16) | copy-start | bytes 6148
  90.2 4.6 %copy-start.2 = (f32[2,256,160]{1,2,0:T(8,128)}, f32[2,256,160]{1,2,0:T(8,128)S(1)}, u32[]{:S(2)}) copy-start(f32[2,256,160]{1,2,0:T(8,128)S(1)} %constant_dynamic-update-slice_fusion) | copy-start | bytes 983044

commit v4 on v3

--- a/solution.py
+++ b/solution.py
@@ -101,7 +101,7 @@
     return (slot_obs, slot_valid)
 
 
-def gather_kernel(n_row, picked_ref, out_ref, part_ref, sem0, send0, sem_a, send_a, sem_b, send_b, sem_c, send_c):
+def gather_kernel(n_row, picked_ref, out_ref, part_ref, sem0, send0, sem_a, send_a, sem_b, send_b):
     n_slab = lax.axis_size("slab")
     n_sub = lax.axis_size("sub")
     s = lax.axis_index("slab")
@@ -114,24 +114,27 @@
             src_ref=src, dst_ref=dst, send_sem=send, recv_sem=recv, device_id=dev, device_id_type=MESH
         )
 
+    def part(q):
+        return part_ref.at[pl.ds(q, 1)]
+
     def to_sub(d):
         q = (u + d) % n_sub
-        return copy(picked_ref.at[q], part_ref.at[u], send0.at[q], sem0.at[u], (s, q))
+        return copy(picked_ref, part(u), send0.at[q], sem0.at[u], (s, q))
 
     def from_sub(d):
         q = (u + d) % n_sub
-        return copy(picked_ref.at[q], part_ref.at[q], send0.at[q], sem0.at[q], (s, q))
+        return copy(picked_ref, part(q), send0.at[q], sem0.at[q], (s, q))
 
     for d in range(1, n_sub):
         to_sub(d).start()
-    total = picked_ref[pl.ds(u, 1), :]
+    total = picked_ref[...]
     for d in range(1, n_sub):
         from_sub(d).wait_recv()
         total = total + part_ref[pl.ds((u + d) % n_sub, 1), :]
-    out_ref[u, pl.ds(s, 1), :] = total
+    out_ref[pl.ds(s, 1), :] = total
 
     def own(r):
-        return out_ref.at[u, pl.ds(r, 1)]
+        return out_ref.at[pl.ds(r, 1)]
 
     def to_a(d):
         j = (loc + d) % n_row
@@ -154,7 +157,7 @@
     lax.fori_loop(1, n_row, wait_a, 0)
 
     def block(r):
-        return out_ref.at[u, pl.ds(r * n_row, n_row)]
+        return out_ref.at[pl.ds(r * n_row, n_row)]
 
     def to_b(d):
         r = (row + d) % n_rows
@@ -168,36 +171,21 @@
         to_b(d).start()
     for d in range(1, n_rows):
         from_b(d).wait_recv()
-
-    def to_c(d):
-        q = (u + d) % n_sub
-        return copy(out_ref.at[u], out_ref.at[u], send_c.at[q], sem_c.at[u], (s, q))
-
-    def from_c(d):
-        q = (u + d) % n_sub
-        return copy(out_ref.at[q], out_ref.at[q], send_c.at[q], sem_c.at[q], (s, q))
-
-    for d in range(1, n_sub):
-        to_c(d).start()
-    for d in range(1, n_sub):
-        from_c(d).wait_recv()
 
     for d in range(1, n_sub):
         to_sub(d).wait_send()
     lax.fori_loop(1, n_row, lambda d, c: (to_a(d).wait_send(), c)[1], 0)
     for d in range(1, n_rows):
         to_b(d).wait_send()
-    for d in range(1, n_sub):
-        to_c(d).wait_send()
 
 
 def gather_slots(picked, n_slab, n_sub, n_row):
     rows, width = picked.shape
-    lanes = rows // n_sub * width
+    lanes = rows * width
     n_rows = n_slab // n_row
     return pl.pallas_call(
         functools.partial(gather_kernel, n_row),
-        out_shape=jax.ShapeDtypeStruct((n_sub, n_slab, lanes), jnp.float32),
+        out_shape=jax.ShapeDtypeStruct((n_slab, lanes), jnp.float32),
         in_specs=[pl.BlockSpec(memory_space=pltpu.VMEM)],
         out_specs=pl.BlockSpec(memory_space=pltpu.VMEM),
         scratch_shapes=[
@@ -208,11 +196,9 @@
             pltpu.SemaphoreType.DMA((n_row,)),
             pltpu.SemaphoreType.DMA((n_rows,)),
             pltpu.SemaphoreType.DMA((n_rows,)),
-            pltpu.SemaphoreType.DMA((n_sub,)),
-            pltpu.SemaphoreType.DMA((n_sub,)),
         ],
         compiler_params=pltpu.CompilerParams(has_side_effects=True),
-    )(picked.reshape(n_sub, lanes))
+    )(picked.reshape(1, lanes))
 
 
 def per_device(ensemble, obs_value, obs_var, obs_owner, obs_column, home_block, batch_order):
@@ -250,9 +236,7 @@
     )
     n_row = 32 if slab_count % 32 == 0 else slab_count
     gathered = gather_slots(picked, slab_count, sub_count, n_row)
-    q_rows = BATCHES * capacity // sub_count
-    row_of = jnp.arange(BATCHES, dtype=jnp.int32)[:, None] * capacity + slot_rank
-    flat = (row_of // q_rows) * (slab_count * q_rows) + owners * q_rows + row_of % q_rows
+    flat = (owners * BATCHES + jnp.arange(BATCHES, dtype=jnp.int32)[:, None]) * capacity + slot_rank
     priors = jnp.take(gathered.reshape(-1, BANDS * members), flat, axis=0)
 
     first, second = batch_order[0], batch_order[1]

time: 103 us -> 109 us (1.058)
  Pallas kernels: 67 us -> 73.1 us
    pallas_call x1, Pallas kernels: 67 us -> 73.1 us  [gather_slots(): pl.pallas_call(functools.partial(gather_kernel, n_row), out_shape=jax.Sha...]
where the time goes in v4:
time: 109 us
  Pallas kernels  73.1 us (67%)
  local copies, waits for them, and re-layouts  16.7 us (15%)
  other arithmetic  7.17 us (7%)
  matrix products  7.02 us (6%)
  between operations  5.13 us (5%)
    pallas_call x1, Pallas kernels, gather_slots(): pl.pallas_call(functools.partial(gather_kernel, n_row), out_shape=jax.Sha...  73.1 us
    gather x2, local copies, waits for them, and re-layouts, per_device(): priors = jnp.take(gathered.reshape(-1, BANDS * members), flat, axis=0)  3.47 us
    dot_general x4, matrix products, update_state(): jnp.einsum('lck,km->lmc', crossed * weights[None], increments, precision=...  2.76 us
    reshape x1, local copies, waits for them, and re-layouts, per_device(): priors = jnp.take(gathered.reshape(-1, BANDS * members), flat, axis=0)  2.34 us

profile of v4, /device:TPU:1, one launch (start us, length us, event | category | flops | bytes accessed | tf_op | source)
XLA Modules:
  0.0 109.1 jit_solution(1145821286277916588)
XLA Ops:
  0.6 0.0 copy-start.3
  0.7 0.7 broadcast_compare_fusion
  1.4 0.8 copy.52
  2.2 0.4 fusion.29
  2.7 0.0 copy-start.1
  2.7 0.1 add_add_fusion
  2.9 0.2 fusion.30
  3.1 0.2 select_reduce_fusion
  3.3 0.1 reshape.1846
  3.4 0.7 gather_fusion.10
  4.1 0.1 reshape.1849
  4.2 0.2 fusion.42
  4.4 0.1 gather.38
  4.5 0.1 reshape.1768
  4.6 1.0 copy.54
  5.6 0.6 gather_fusion
  6.2 0.1 bitcast_select_fusion.2
  6.3 0.7 select_n.390.picked_ref
  7.0 73.1 %shard_map.86 = f32[128,2560]{1,0:T(8,128)} custom-call(f32[1,2560]{1,0:T(1,128)} %select_n.390.picked_ref), custom_call_target="tpu_custom_call" | custom-call | tf_op jit(solution)/shard_map/pallas_call | solution.py:186
  80.1 2.3 %reshape.1766 = f32[2048,160]{1,0:T(8,128)S(1)} reshape(f32[128,2560]{1,0:T(8,128)} %shard_map.86) | data formatting | bytes 2621440 | tf_op jit(solution)/shard_map/reshape | solution.py:240
  82.4 2.2 %gather_fusion.1 = f32[512,160]{1,0:T(8,128)} fusion(f32[2048,160]{1,0:T(8,128)S(1)} %reshape.1766, s32[1024]{0:T(1024)S(1)} %pad_clamp_fusion.2), kind=kCustom, calls=%fused_computation.1 | custom fusion | bytes 657408 | tf_op jit(solution)/shard_map/jit(_take)/gather | solution.py:240
  84.7 1.2 %copy.57 = f32[2,256,160]{1,2,0:T(8,128)S(1)} copy(f32[2,256,160]{2,1,0:T(8,128)} %bitcast.162) | data formatting | bytes 655360 | tf_op jit(solution)/shard_map/jit(_take)/gather | solution.py:240
  86.0 0.6 fusion.104
  90.5 0.7 and_reduce_fusion
  91.2 0.6 select_dynamic-update-slice_fusion
  91.9 0.1 copy.58
  92.1 0.2 multiply_reduce_fusion
  92.3 0.1 copy.59
  92.5 0.2 copy.60
  92.6 0.3 broadcast_subtract_fusion
  93.0 0.2 fusion.101
  93.2 0.8 convolution_multiply_fusion.1
  94.0 0.2 multiply_add_fusion
  94.2 0.8 convolution_multiply_fusion
  95.0 0.4 convolution_add_fusion
  95.4 0.4 fusion.100
  95.8 0.7 constant_dynamic-update-slice_fusion
  96.6 0.2 fusion.76
  96.8 0.1 pad_add_fusion
  96.9 0.2 select_reduce_fusion.6
  97.0 0.2 select_reduce_fusion.3
  97.2 0.1 fusion.96
  97.3 0.7 gather_fusion.5
  98.0 0.1 pad_add_fusion.1
  98.1 0.7 gather_fusion.9
  98.9 0.7 gather_fusion.4
  99.6 0.7 gather_fusion.8
  100.3 0.1 fusion.54
  100.4 0.6 gather_fusion.3
  101.1 0.1 slice_reduce_fusion.1
  101.2 0.5 convolution_multiply_fusion.5
  101.7 0.6 gather_fusion.2
  102.2 0.7 fusion.106
  103.0 0.1 copy.63
  103.1 0.6 gather_fusion.7
  103.8 0.5 convolution_multiply_fusion.4
  104.3 0.1 copy.62
  104.4 0.6 gather_fusion.6
  104.9 0.7 fusion.4
  105.6 0.5 convolution_multiply_fusion.3
  106.1 0.7 fusion.105
  106.8 0.5 convolution_multiply_fusion.2
  107.3 0.7 fusion.1
  108.0 1.1 %pad_maximum_fusion = f32[2,15,80,128]{3,2,1,0:T(8,128)} fusion(f32[1,15,80,128]{3,2,1,0:T(8,128)S(1)} %fusion.1, f32[1,15,80,128]{3,2,1,0:T(8,128)S(1)} %fusion.4), kind=kLoop, calls=%fused_computation.21 | loop fusion | flops 307200 | bytes 2457600 | tf_op jit(solution)/shard_map/stack | solution.py:89
  (59 shorter events, 0.7 us)
Async XLA Ops:
  0.6 2.2 %copy-start.3 = (s32[2,256,1]{1,2,0:T(1,128)S(1)}, s32[2,256,1]{1,2,0:T(1,128)}, u32[]{:S(2)}) copy-start(s32[2,256,1]{1,2,0:T(1,128)} %param.14) | copy-start | bytes 6148
  0.6 2.8 %copy-start = (s32[2,256]{1,0:T(2,128)S(1)}, s32[2,256]{1,0:T(2,128)}, u32[]{:S(2)}) copy-start(s32[2,256]{1,0:T(2,128)} %param.15) | copy-start | bytes 6148
  2.7 1.9 %copy-start.1 = (f32[2,15,80,128]{3,2,1,0:T(8,128)S(1)}, f32[2,15,80,128]{3,2,1,0:T(8,128)}, u32[]{:S(2)}) copy-start(f32[2,15,80,128]{3,2,1,0:T(8,128)} %param.11) | copy-start | bytes 3686404
  84.7 1.3 %copy-start.4 = (s32[2]{0:T(128)S(1)}, s32[2]{0:T(128)}, u32[]{:S(2)}) copy-start(s32[2]{0:T(128)} %param.17) | copy-start | bytes 28
  84.7 5.8 %copy-start.8 = (s32[3]{0:T(128)S(1)}, s32[3]{0:T(128)}, u32[]{:S(2)}) copy-start(s32[3]{0:T(128)} %constant.309.clone.1) | copy-start | bytes 40
  85.9 6.3 %copy-start.5 = (f32[2,256]{1,0:T(2,128)S(1)}, f32[2,256]{1,0:T(2,128)}, u32[]{:S(2)}) copy-start(f32[2,256]{1,0:T(2,128)} %param.12) | copy-start | bytes 6148
  86.0 6.3 %copy-start.6 = (f32[2,256]{1,0:T(2,128)S(1)}, f32[2,256]{1,0:T(2,128)}, u32[]{:S(2)}) copy-start(f32[2,256]{1,0:T(2,128)} %param.13) | copy-start | bytes 6148
  91.9 1.3 %copy-start.7 = (s32[2,256]{1,0:T(2,128)S(1)}, s32[2,256]{1,0:T(2,128)}, u32[]{:S(2)}) copy-start(s32[2,256]{1,0:T(2,128)} %param.16) | copy-start | bytes 6148
  96.5 4.6 %copy-start.2 = (f32[2,256,160]{1,2,0:T(8,128)}, f32[2,256,160]{1,2,0:T(8,128)S(1)}, u32[]{:S(2)}) copy-start(f32[2,256,160]{1,2,0:T(8,128)S(1)} %constant_dynamic-update-slice_fusion) | copy-start | bytes 983044

commit v5 on v3

--- a/solution.py
+++ b/solution.py
@@ -121,6 +121,21 @@
     def from_sub(d):
         q = (u + d) % n_sub
         return copy(picked_ref.at[q], part_ref.at[q], send0.at[q], sem0.at[q], (s, q))
+
+    barrier = pltpu.get_barrier_semaphore()
+    for d in range(1, n_sub):
+        pl.semaphore_signal(barrier, 1, device_id=(s, (u + d) % n_sub), device_id_type=MESH)
+
+    def greet(d, c):
+        dev = (row * n_row + (loc + d) % n_row, u)
+        pl.semaphore_signal(barrier, 1, device_id=dev, device_id_type=MESH)
+        return c
+
+    lax.fori_loop(1, n_row, greet, 0)
+    for d in range(1, n_rows):
+        dev = (((row + d) % n_rows) * n_row + loc, u)
+        pl.semaphore_signal(barrier, 1, device_id=dev, device_id_type=MESH)
+    pl.semaphore_wait(barrier, (n_sub - 1) + (n_row - 1) + (n_rows - 1))
 
     for d in range(1, n_sub):
         to_sub(d).start()
@@ -211,7 +226,7 @@
             pltpu.SemaphoreType.DMA((n_sub,)),
             pltpu.SemaphoreType.DMA((n_sub,)),
         ],
-        compiler_params=pltpu.CompilerParams(has_side_effects=True),
+        compiler_params=pltpu.CompilerParams(has_side_effects=True, collective_id=0),
     )(picked.reshape(n_sub, lanes))
 
 

time: 103 us -> 88.1 us (0.86)
  Pallas kernels: 67 us -> 51.9 us
    pallas_call x1, Pallas kernels: 67 us -> 51.9 us  [gather_slots(): pl.pallas_call(functools.partial(gather_kernel, n_row), out_shape=jax.Sha...]
where the time goes in v5:
time: 88.1 us; the launch traced here: 87.7 us
  Pallas kernels  51.9 us (59%)
  local copies, waits for them, and re-layouts  16.4 us (19%)
  other arithmetic  7.26 us (8%)
  matrix products  7.02 us (8%)
  between operations  5.13 us (6%)
    pallas_call x1, Pallas kernels, gather_slots(): pl.pallas_call(functools.partial(gather_kernel, n_row), out_shape=jax.Sha...  51.9 us
    gather x2, local copies, waits for them, and re-layouts, per_device(): priors = jnp.take(gathered.reshape(-1, BANDS * members), flat, axis=0)  3.47 us
    dot_general x4, matrix products, update_state(): jnp.einsum('lck,km->lmc', crossed * weights[None], increments, precision=...  2.76 us
    reshape x1, local copies, waits for them, and re-layouts, per_device(): priors = jnp.take(gathered.reshape(-1, BANDS * members), flat, axis=0)  2.04 us
    dot_general x4, matrix products, update_state(): crossed = jnp.einsum('lmc,km->lck', layer_dev, obs_dev, precision=HIGHEST)  1.93 us

profile of v5, /device:TPU:1, one launch (start us, length us, event | category | flops | bytes accessed | tf_op | source)
XLA Modules:
  0.0 87.7 jit_solution(16907245151190017742)
XLA Ops:
  0.7 0.7 broadcast_compare_fusion
  1.4 0.8 copy.52
  2.2 0.4 fusion.29
  2.7 0.0 copy-start.1
  2.7 0.1 add_add_fusion
  2.9 0.2 fusion.30
  3.1 0.2 select_reduce_fusion
  3.3 0.1 reshape.1944
  3.4 0.7 gather_fusion.10
  4.1 0.1 reshape.1947
  4.2 0.2 fusion.42
  4.4 0.1 gather.38
  4.5 0.1 reshape.1866
  4.6 1.0 %copy.54 = f32[2,15,80,128]{2,0,3,1:T(2,128)S(1)} copy(f32[2,15,80,128]{3,2,1,0:T(8,128)S(1)} %copy-done.1) | data formatting | bytes 2457600 | tf_op args[0]
  5.6 0.6 gather_fusion
  6.2 0.1 bitcast_select_fusion.2
  6.3 0.7 select_n.409.picked_ref
  7.0 51.9 %shard_map.86 = f32[4,128,640]{2,1,0:T(8,128)} custom-call(f32[4,640]{1,0:T(4,128)} %select_n.409.picked_ref), custom_call_target="tpu_custom_call" | custom-call | tf_op jit(solution)/shard_map/pallas_call | solution.py:213
  58.9 2.0 %reshape.1864 = f32[2048,160]{1,0:T(8,128)S(1)} reshape(f32[4,128,640]{2,1,0:T(8,128)} %shard_map.86) | data formatting | bytes 2621440 | tf_op jit(solution)/shard_map/reshape | solution.py:271
  60.9 0.1 compare_and_fusion
  61.1 2.2 %gather_fusion.1 = f32[512,160]{1,0:T(8,128)} fusion(f32[2048,160]{1,0:T(8,128)S(1)} %reshape.1864, s32[1024]{0:T(1024)S(1)} %pad_clamp_fusion.2), kind=kCustom, calls=%fused_computation.1 | custom fusion | bytes 657408 | tf_op jit(solution)/shard_map/jit(_take)/gather | solution.py:271
  63.3 1.2 %copy.57 = f32[2,256,160]{1,2,0:T(8,128)S(1)} copy(f32[2,256,160]{2,1,0:T(8,128)} %bitcast.162) | data formatting | bytes 655360 | tf_op jit(solution)/shard_map/jit(_take)/gather | solution.py:271
  64.6 0.6 fusion.105
  69.1 0.7 and_reduce_fusion
  69.8 0.6 select_dynamic-update-slice_fusion
  70.5 0.1 copy.58
  70.7 0.2 multiply_reduce_fusion
  70.9 0.1 copy.59
  71.1 0.2 copy.60
  71.2 0.3 broadcast_subtract_fusion
  71.6 0.2 fusion.102
  71.8 0.8 convolution_multiply_fusion.1
  72.6 0.2 multiply_add_fusion
  72.8 0.8 convolution_multiply_fusion
  73.6 0.4 convolution_add_fusion
  74.0 0.4 fusion.101
  74.4 0.7 constant_dynamic-update-slice_fusion
  75.2 0.2 fusion.76
  75.4 0.1 pad_add_fusion
  75.5 0.2 select_reduce_fusion.6
  75.6 0.2 select_reduce_fusion.3
  75.8 0.1 fusion.97
  75.9 0.7 gather_fusion.5
  76.6 0.1 pad_add_fusion.1
  76.8 0.7 gather_fusion.9
  77.5 0.7 gather_fusion.4
  78.2 0.7 gather_fusion.8
  78.9 0.1 fusion.54
  79.0 0.6 gather_fusion.3
  79.7 0.1 slice_reduce_fusion.1
  79.8 0.5 convolution_multiply_fusion.5
  80.3 0.6 gather_fusion.2
  80.8 0.7 fusion.107
  81.6 0.1 copy.63
  81.7 0.6 gather_fusion.7
  82.4 0.5 convolution_multiply_fusion.4
  82.9 0.1 copy.62
  83.0 0.6 gather_fusion.6
  83.5 0.7 fusion.4
  84.2 0.5 convolution_multiply_fusion.3
  84.7 0.7 fusion.106
  85.4 0.5 convolution_multiply_fusion.2
  85.9 0.7 fusion.1
  86.6 1.1 %pad_maximum_fusion = f32[2,15,80,128]{3,2,1,0:T(8,128)} fusion(f32[1,15,80,128]{3,2,1,0:T(8,128)S(1)} %fusion.1, f32[1,15,80,128]{3,2,1,0:T(8,128)S(1)} %fusion.4), kind=kLoop, calls=%fused_computation.21 | loop fusion | flops 307200 | bytes 2457600 | tf_op jit(solution)/shard_map/stack | solution.py:89
  (60 shorter events, 0.7 us)
Async XLA Ops:
  0.6 2.2 %copy-start.3 = (s32[2,256,1]{1,2,0:T(1,128)S(1)}, s32[2,256,1]{1,2,0:T(1,128)}, u32[]{:S(2)}) copy-start(s32[2,256,1]{1,2,0:T(1,128)} %param.14) | copy-start | bytes 6148
  0.6 2.8 %copy-start = (s32[2,256]{1,0:T(2,128)S(1)}, s32[2,256]{1,0:T(2,128)}, u32[]{:S(2)}) copy-start(s32[2,256]{1,0:T(2,128)} %param.15) | copy-start | bytes 6148
  2.7 1.9 %copy-start.1 = (f32[2,15,80,128]{3,2,1,0:T(8,128)S(1)}, f32[2,15,80,128]{3,2,1,0:T(8,128)}, u32[]{:S(2)}) copy-start(f32[2,15,80,128]{3,2,1,0:T(8,128)} %param.11) | copy-start | bytes 3686404
  63.3 1.3 %copy-start.4 = (s32[2]{0:T(128)S(1)}, s32[2]{0:T(128)}, u32[]{:S(2)}) copy-start(s32[2]{0:T(128)} %param.17) | copy-start | bytes 28
  63.3 5.8 %copy-start.8 = (s32[3]{0:T(128)S(1)}, s32[3]{0:T(128)}, u32[]{:S(2)}) copy-start(s32[3]{0:T(128)} %constant.326.clone.1) | copy-start | bytes 40
  64.6 6.3 %copy-start.5 = (f32[2,256]{1,0:T(2,128)S(1)}, f32[2,256]{1,0:T(2,128)}, u32[]{:S(2)}) copy-start(f32[2,256]{1,0:T(2,128)} %param.12) | copy-start | bytes 6148
  64.6 6.3 %copy-start.6 = (f32[2,256]{1,0:T(2,128)S(1)}, f32[2,256]{1,0:T(2,128)}, u32[]{:S(2)}) copy-start(f32[2,256]{1,0:T(2,128)} %param.13) | copy-start | bytes 6148
  70.5 1.3 %copy-start.7 = (s32[2,256]{1,0:T(2,128)S(1)}, s32[2,256]{1,0:T(2,128)}, u32[]{:S(2)}) copy-start(s32[2,256]{1,0:T(2,128)} %param.16) | copy-start | bytes 6148
  75.1 4.6 %copy-start.2 = (f32[2,256,160]{1,2,0:T(8,128)}, f32[2,256,160]{1,2,0:T(8,128)S(1)}, u32[]{:S(2)}) copy-start(f32[2,256,160]{1,2,0:T(8,128)S(1)} %constant_dynamic-update-slice_fusion) | copy-start | bytes 983044

commit v6 on v5

--- a/solution.py
+++ b/solution.py
@@ -143,10 +143,13 @@
     for d in range(1, n_sub):
         from_sub(d).wait_recv()
         total = total + part_ref[pl.ds((u + d) % n_sub, 1), :]
-    out_ref[u, pl.ds(s, 1), :] = total
-
-    def own(r):
-        return out_ref.at[u, pl.ds(r, 1)]
+    half = n_row // 2
+
+    def own(t):
+        j = t % n_row
+        return out_ref.at[u, t // n_row, j // half, pl.ds(j % half, 1)]
+
+    own(s)[...] = total
 
     def to_a(d):
         j = (loc + d) % n_row
@@ -168,51 +171,81 @@
     lax.fori_loop(1, n_row, start_a, 0)
     lax.fori_loop(1, n_row, wait_a, 0)
 
-    def block(r):
-        return out_ref.at[u, pl.ds(r * n_row, n_row)]
-
-    def to_b(d):
+    def peer_x(d):
         r = (row + d) % n_rows
-        return copy(block(row), block(row), send_b.at[r], sem_b.at[row], (r * n_row + loc, u))
-
-    def from_b(d):
-        r = (row + d) % n_rows
-        return copy(block(r), block(r), send_b.at[r], sem_b.at[r], (r * n_row + loc, u))
-
-    for d in range(1, n_rows):
-        to_b(d).start()
-    for d in range(1, n_rows):
-        from_b(d).wait_recv()
-
-    def to_c(d):
+        return r, (r * n_row + loc, u)
+
+    def peer_y(d):
         q = (u + d) % n_sub
-        return copy(out_ref.at[u], out_ref.at[u], send_c.at[q], sem_c.at[u], (s, q))
-
-    def from_c(d):
-        q = (u + d) % n_sub
-        return copy(out_ref.at[q], out_ref.at[q], send_c.at[q], sem_c.at[q], (s, q))
-
-    for d in range(1, n_sub):
-        to_c(d).start()
-    for d in range(1, n_sub):
-        from_c(d).wait_recv()
+        return q, (s, q)
+
+    def to_b1(d):
+        r, dev = peer_x(d)
+        return copy(out_ref.at[u, row, 0], out_ref.at[u, row, 0], send_b.at[0, r], sem_b.at[0, row], dev)
+
+    def from_b1(d):
+        r, dev = peer_x(d)
+        return copy(out_ref.at[u, r, 0], out_ref.at[u, r, 0], send_b.at[0, r], sem_b.at[0, r], dev)
+
+    def to_c1(d):
+        q, dev = peer_y(d)
+        return copy(out_ref.at[u, row, 1], out_ref.at[u, row, 1], send_c.at[0, q], sem_c.at[0, u], dev)
+
+    def from_c1(d):
+        q, dev = peer_y(d)
+        return copy(out_ref.at[q, row, 1], out_ref.at[q, row, 1], send_c.at[0, q], sem_c.at[0, q], dev)
+
+    def to_b2(d):
+        r, dev = peer_x(d)
+        return copy(out_ref.at[:, row, 1], out_ref.at[:, row, 1], send_b.at[1, r], sem_b.at[1, row], dev)
+
+    def from_b2(d):
+        r, dev = peer_x(d)
+        return copy(out_ref.at[:, r, 1], out_ref.at[:, r, 1], send_b.at[1, r], sem_b.at[1, r], dev)
+
+    def to_c2(d):
+        q, dev = peer_y(d)
+        return copy(out_ref.at[u, :, 0], out_ref.at[u, :, 0], send_c.at[1, q], sem_c.at[1, u], dev)
+
+    def from_c2(d):
+        q, dev = peer_y(d)
+        return copy(out_ref.at[q, :, 0], out_ref.at[q, :, 0], send_c.at[1, q], sem_c.at[1, q], dev)
+
+    for d in range(1, n_rows):
+        to_b1(d).start()
+    for d in range(1, n_sub):
+        to_c1(d).start()
+    for d in range(1, n_sub):
+        from_c1(d).wait_recv()
+    for d in range(1, n_rows):
+        to_b2(d).start()
+    for d in range(1, n_rows):
+        from_b1(d).wait_recv()
+    for d in range(1, n_sub):
+        to_c2(d).start()
+    for d in range(1, n_rows):
+        from_b2(d).wait_recv()
+    for d in range(1, n_sub):
+        from_c2(d).wait_recv()
 
     for d in range(1, n_sub):
         to_sub(d).wait_send()
     lax.fori_loop(1, n_row, lambda d, c: (to_a(d).wait_send(), c)[1], 0)
     for d in range(1, n_rows):
-        to_b(d).wait_send()
-    for d in range(1, n_sub):
-        to_c(d).wait_send()
+        to_b1(d).wait_send()
+        to_b2(d).wait_send()
+    for d in range(1, n_sub):
+        to_c1(d).wait_send()
+        to_c2(d).wait_send()
 
 
 def gather_slots(picked, n_slab, n_sub, n_row):
     rows, width = picked.shape
     lanes = rows // n_sub * width
     n_rows = n_slab // n_row
-    return pl.pallas_call(
+    gathered = pl.pallas_call(
         functools.partial(gather_kernel, n_row),
-        out_shape=jax.ShapeDtypeStruct((n_sub, n_slab, lanes), jnp.float32),
+        out_shape=jax.ShapeDtypeStruct((n_sub, n_rows, 2, n_row // 2, lanes), jnp.float32),
         in_specs=[pl.BlockSpec(memory_space=pltpu.VMEM)],
         out_specs=pl.BlockSpec(memory_space=pltpu.VMEM),
         scratch_shapes=[
@@ -221,13 +254,14 @@
             pltpu.SemaphoreType.DMA((n_sub,)),
             pltpu.SemaphoreType.DMA((n_row,)),
             pltpu.SemaphoreType.DMA((n_row,)),
-            pltpu.SemaphoreType.DMA((n_rows,)),
-            pltpu.SemaphoreType.DMA((n_rows,)),
-            pltpu.SemaphoreType.DMA((n_sub,)),
-            pltpu.SemaphoreType.DMA((n_sub,)),
+            pltpu.SemaphoreType.DMA((2, n_rows)),
+            pltpu.SemaphoreType.DMA((2, n_rows)),
+            pltpu.SemaphoreType.DMA((2, n_sub)),
+            pltpu.SemaphoreType.DMA((2, n_sub)),
         ],
         compiler_params=pltpu.CompilerParams(has_side_effects=True, collective_id=0),
     )(picked.reshape(n_sub, lanes))
+    return gathered.reshape(n_sub, n_slab, lanes)
 
 
 def per_device(ensemble, obs_value, obs_var, obs_owner, obs_column, home_block, batch_order):

time: 88.1 us -> 78.9 us (0.90)
  Pallas kernels: 51.9 us -> 42.8 us
    pallas_call x1, Pallas kernels: 51.9 us -> 42.8 us  [gather_slots(): pl.pallas_call(functools.partial(gather_kernel, n_row), out_shape=jax.Sha...]
    another operation x2 -> x3, local copies, waits for them, and re-layouts: 0.01 us -> 2.04 us  [the longest x1 2.04 us: per_device(): priors = jnp.take(gathered.reshape(-1, BANDS * members), flat, axis=0)]
    reshape x1 -> x0, local copies, waits for them, and re-layouts: 2.04 us -> none  [per_device(): priors = jnp.take(gathered.reshape(-1, BANDS * members), flat, axis=0)]
where the time goes in v6:
time: 78.9 us; the launch traced here: 78.6 us
  Pallas kernels  42.8 us (54%)
  local copies, waits for them, and re-layouts  16.4 us (21%)
  other arithmetic  7.26 us (9%)
  matrix products  7.02 us (9%)
  between operations  5.13 us (7%)
    pallas_call x1, Pallas kernels, gather_slots(): pl.pallas_call(functools.partial(gather_kernel, n_row), out_shape=jax.Sha...  42.8 us
    gather x2, local copies, waits for them, and re-layouts, per_device(): priors = jnp.take(gathered.reshape(-1, BANDS * members), flat, axis=0)  3.47 us
    dot_general x4, matrix products, update_state(): jnp.einsum('lck,km->lmc', crossed * weights[None], increments, precision=...  2.76 us
    another operation x1, local copies, waits for them, and re-layouts, per_device(): priors = jnp.take(gathered.reshape(-1, BANDS * members), flat, axis=0)  2.04 us
    dot_general x4, matrix products, update_state(): crossed = jnp.einsum('lmc,km->lck', layer_dev, obs_dev, precision=HIGHEST)  1.93 us

profile of v6, /device:TPU:1, one launch (start us, length us, event | category | flops | bytes accessed | tf_op | source)
XLA Modules:
  0.0 78.6 jit_solution(7565529033398005376)
XLA Ops:
  0.7 0.7 broadcast_compare_fusion
  1.4 0.8 %copy.52 = s32[2,2,128]{1,2,0:T(8,128)S(1)} copy(s32[2,2,128]{2,1,0:T(2,128)} %bitcast.176) | data formatting | bytes 4096 | tf_op jit(solution)/shard_map/eq | solution.py:284
  2.2 0.4 fusion.29
  2.7 0.0 copy-start.1
  2.7 0.1 add_add_fusion
  2.9 0.2 fusion.30
  3.1 0.2 select_reduce_fusion
  3.3 0.1 reshape.1940
  3.4 0.7 gather_fusion.10
  4.1 0.1 reshape.1943
  4.2 0.2 fusion.42
  4.4 0.1 gather.38
  4.5 0.1 reshape.1862
  4.6 1.0 %copy.54 = f32[2,15,80,128]{2,0,3,1:T(2,128)S(1)} copy(f32[2,15,80,128]{3,2,1,0:T(8,128)S(1)} %copy-done.1) | data formatting | bytes 2457600 | tf_op args[0]
  5.6 0.6 gather_fusion
  6.2 0.1 bitcast_select_fusion.2
  6.3 0.7 select_n.409.picked_ref
  7.0 42.8 %shard_map.86 = f32[4,4,2,16,640]{4,3,2,1,0:T(8,128)} custom-call(f32[4,640]{1,0:T(4,128)} %select_n.409.picked_ref), custom_call_target="tpu_custom_call" | custom-call | tf_op jit(solution)/shard_map/pallas_call | solution.py:246
  49.7 2.0 %reshape_reshape.4 = f32[2048,160]{1,0:T(8,128)S(1)} reshape(f32[4,4,2,16,640]{4,3,2,1,0:T(8,128)} %shard_map.86) | data formatting | bytes 2621440 | tf_op jit(solution)/shard_map/reshape;reshape | solution.py:305
  51.8 0.1 compare_and_fusion
  51.9 2.2 %gather_fusion.1 = f32[512,160]{1,0:T(8,128)} fusion(f32[2048,160]{1,0:T(8,128)S(1)} %reshape_reshape.4, s32[1024]{0:T(1024)S(1)} %pad_clamp_fusion.2), kind=kCustom, calls=%fused_computation.1 | custom fusion | bytes 657408 | tf_op jit(solution)/shard_map/jit(_take)/gather | solution.py:305
  54.2 1.2 %copy.57 = f32[2,256,160]{1,2,0:T(8,128)S(1)} copy(f32[2,256,160]{2,1,0:T(8,128)} %bitcast.164) | data formatting | bytes 655360 | tf_op jit(solution)/shard_map/jit(_take)/gather | solution.py:305
  55.5 0.6 fusion.105
  60.0 0.7 and_reduce_fusion
  60.7 0.6 select_dynamic-update-slice_fusion
  61.4 0.1 copy.58
  61.5 0.2 multiply_reduce_fusion
  61.8 0.1 copy.59
  61.9 0.2 copy.60
  62.1 0.3 broadcast_subtract_fusion
  62.4 0.2 fusion.102
  62.7 0.8 convolution_multiply_fusion.1
  63.5 0.2 multiply_add_fusion
  63.7 0.8 convolution_multiply_fusion
  64.4 0.4 convolution_add_fusion
  64.8 0.4 fusion.101
  65.3 0.7 constant_dynamic-update-slice_fusion
  66.1 0.2 fusion.76
  66.3 0.1 pad_add_fusion
  66.3 0.2 select_reduce_fusion.6
  66.5 0.2 select_reduce_fusion.3
  66.6 0.1 fusion.97
  66.7 0.7 gather_fusion.5
  67.5 0.1 pad_add_fusion.1
  67.6 0.7 gather_fusion.9
  68.3 0.7 gather_fusion.4
  69.0 0.7 gather_fusion.8
  69.8 0.1 fusion.54
  69.9 0.6 gather_fusion.3
  70.5 0.1 slice_reduce_fusion.1
  70.6 0.5 convolution_multiply_fusion.5
  71.1 0.6 gather_fusion.2
  71.7 0.7 fusion.107
  72.4 0.1 copy.63
  72.6 0.6 gather_fusion.7
  73.2 0.5 convolution_multiply_fusion.4
  73.7 0.1 copy.62
  73.8 0.6 gather_fusion.6
  74.4 0.7 fusion.4
  75.1 0.5 convolution_multiply_fusion.3
  75.6 0.7 fusion.106
  76.3 0.5 convolution_multiply_fusion.2
  76.8 0.7 fusion.1
  77.5 1.1 %pad_maximum_fusion = f32[2,15,80,128]{3,2,1,0:T(8,128)} fusion(f32[1,15,80,128]{3,2,1,0:T(8,128)S(1)} %fusion.1, f32[1,15,80,128]{3,2,1,0:T(8,128)S(1)} %fusion.4), kind=kLoop, calls=%fused_computation.21 | loop fusion | flops 307200 | bytes 2457600 | tf_op jit(solution)/shard_map/stack | solution.py:89
  (60 shorter events, 0.7 us)
Async XLA Ops:
  0.6 2.2 %copy-start.3 = (s32[2,256,1]{1,2,0:T(1,128)S(1)}, s32[2,256,1]{1,2,0:T(1,128)}, u32[]{:S(2)}) copy-start(s32[2,256,1]{1,2,0:T(1,128)} %param.14) | copy-start | bytes 6148
  0.6 2.8 %copy-start = (s32[2,256]{1,0:T(2,128)S(1)}, s32[2,256]{1,0:T(2,128)}, u32[]{:S(2)}) copy-start(s32[2,256]{1,0:T(2,128)} %param.15) | copy-start | bytes 6148
  2.7 1.9 %copy-start.1 = (f32[2,15,80,128]{3,2,1,0:T(8,128)S(1)}, f32[2,15,80,128]{3,2,1,0:T(8,128)}, u32[]{:S(2)}) copy-start(f32[2,15,80,128]{3,2,1,0:T(8,128)} %param.11) | copy-start | bytes 3686404
  54.2 1.3 %copy-start.4 = (s32[2]{0:T(128)S(1)}, s32[2]{0:T(128)}, u32[]{:S(2)}) copy-start(s32[2]{0:T(128)} %param.17) | copy-start | bytes 28
  54.2 5.8 %copy-start.8 = (s32[3]{0:T(128)S(1)}, s32[3]{0:T(128)}, u32[]{:S(2)}) copy-start(s32[3]{0:T(128)} %constant.326.clone.1) | copy-start | bytes 40
  55.4 6.3 %copy-start.5 = (f32[2,256]{1,0:T(2,128)S(1)}, f32[2,256]{1,0:T(2,128)}, u32[]{:S(2)}) copy-start(f32[2,256]{1,0:T(2,128)} %param.12) | copy-start | bytes 6148
  55.4 6.3 %copy-start.6 = (f32[2,256]{1,0:T(2,128)S(1)}, f32[2,256]{1,0:T(2,128)}, u32[]{:S(2)}) copy-start(f32[2,256]{1,0:T(2,128)} %param.13) | copy-start | bytes 6148
  61.3 1.3 %copy-start.7 = (s32[2,256]{1,0:T(2,128)S(1)}, s32[2,256]{1,0:T(2,128)}, u32[]{:S(2)}) copy-start(s32[2,256]{1,0:T(2,128)} %param.16) | copy-start | bytes 6148
  65.9 4.6 %copy-start.2 = (f32[2,256,160]{1,2,0:T(8,128)}, f32[2,256,160]{1,2,0:T(8,128)S(1)}, u32[]{:S(2)}) copy-start(f32[2,256,160]{1,2,0:T(8,128)S(1)} %constant_dynamic-update-slice_fusion) | copy-start | bytes 983044

commit v7 on v6

--- a/solution.py
+++ b/solution.py
@@ -57,36 +57,32 @@
 def update_pool(pool, pool_homes, deviations, spread, increments, obs_homes, nblocks, decays):
     members = deviations.shape[2]
     banded = pool.reshape(pool.shape[0], BANDS, members)
-    new_bands = []
-    for band_no in range(BANDS):
-        pool_band = banded[:, band_no, :]
-        pool_dev = pool_band - jnp.mean(pool_band, axis=1, keepdims=True)
-        weights = (
-            gc_weight(pool_homes[:, None], obs_homes[None, :], nblocks, decays[band_no])
-            / ((members - 1) * spread)[None, :]
-        )
-        crossed = jnp.einsum("pm,km->pk", pool_dev, deviations[:, band_no, :], precision=HIGHEST)
-        change = jnp.einsum("pk,km->pm", crossed * weights, increments, precision=HIGHEST)
-        new_bands.append(pool_band + change)
-    return jnp.stack(new_bands, axis=1).reshape(pool.shape)
-
-
-def update_state(ensemble, my_cols, deviations, spread, increments, obs_homes, valid, nblocks, decays):
+    pool_dev = banded - jnp.mean(banded, axis=2, keepdims=True)
+    weights = jnp.stack(
+        [gc_weight(pool_homes[:, None], obs_homes[None, :], nblocks, decay) for decay in decays]
+    ) / ((members - 1) * spread)[None, None, :]
+    crossed = jnp.einsum("pbm,kbm->bpk", pool_dev, deviations, precision=HIGHEST)
+    change = jnp.einsum("bpk,km->pbm", crossed * weights, increments, precision=HIGHEST)
+    return (banded + change).reshape(pool.shape)
+
+
+def update_state(ensemble, col_blocks, deviations, spread, increments, obs_homes, valid, nblocks, decays):
     members = ensemble.shape[2]
-    new_bands = []
-    for band_no in range(BANDS):
-        band_layer = ensemble[band_no]
-        layer_dev = band_layer - jnp.mean(band_layer, axis=1, keepdims=True)
-        obs_dev = deviations[:, band_no, :]
-        weights = (
-            gc_weight((my_cols // BLK)[:, None], obs_homes[None, :], nblocks, decays[band_no])
-            / ((members - 1) * spread)[None, :]
-        )
-        weights = jnp.where(valid[None, :], weights, 0.0)
-        crossed = jnp.einsum("lmc,km->lck", layer_dev, obs_dev, precision=HIGHEST)
-        change = jnp.einsum("lck,km->lmc", crossed * weights[None], increments, precision=HIGHEST)
-        new_bands.append(band_layer + change)
-    return jnp.stack(new_bands, axis=0)
+    layer_dev = ensemble - jnp.mean(ensemble, axis=2, keepdims=True)
+    weights = jnp.stack(
+        [gc_weight(col_blocks[:, None], obs_homes[None, :], nblocks, decay) for decay in decays]
+    ) / ((members - 1) * spread)[None, None, :]
+    weights = jnp.where(valid[None, None, :], weights, 0.0)
+    crossed = jnp.einsum("blmc,kbm->blck", layer_dev, deviations, precision=HIGHEST)
+    change = jnp.einsum("blck,km->blmc", crossed * weights[:, None], increments, precision=HIGHEST)
+    return ensemble + change
+
+
+def pick(stacked, which):
+    out = stacked[0]
+    for i in range(1, stacked.shape[0]):
+        out = jnp.where(which == i, stacked[i], out)
+    return out
 
 
 def slot_table(owners, slot_rank, slab_number, capacity):
@@ -286,7 +282,6 @@
     )
     running = jnp.cumsum(onehot, axis=1) - 1
     slot_rank = jnp.sum(onehot * running, axis=2)
-    slot_global = owners * capacity + slot_rank
     slot_obs, slot_valid = slot_table(owners, slot_rank, slab_index, capacity)
     slot_column = jnp.take_along_axis(obs_column, slot_obs, axis=1)
     slot_level = slot_obs % levels_count
@@ -300,36 +295,60 @@
     n_row = 32 if slab_count % 32 == 0 else slab_count
     gathered = gather_slots(picked, slab_count, sub_count, n_row)
     q_rows = BATCHES * capacity // sub_count
+    width = BANDS * members
     row_of = jnp.arange(BATCHES, dtype=jnp.int32)[:, None] * capacity + slot_rank
-    flat = (row_of // q_rows) * (slab_count * q_rows) + owners * q_rows + row_of % q_rows
-    priors = jnp.take(gathered.reshape(-1, BANDS * members), flat, axis=0)
+    lines = jnp.take(
+        gathered.reshape(sub_count * slab_count, q_rows * width),
+        ((row_of // q_rows) * slab_count + owners).reshape(-1),
+        axis=0,
+    )
+    part = (row_of % q_rows).reshape(-1, 1)
+    flat_priors = lines[:, :width]
+    for r in range(1, q_rows):
+        flat_priors = jnp.where(part == r, lines[:, r * width : (r + 1) * width], flat_priors)
+    priors = flat_priors.reshape(BATCHES, -1, width)
 
     first, second = batch_order[0], batch_order[1]
-    y0 = priors[first]
-    stats0 = obs_statistics(y0, obs_value[first], obs_var[first], members)
-    y1 = update_pool(priors[second], obs_home[second], *stats0, obs_home[first], nblocks, decays)
-    stats1 = obs_statistics(y1, obs_value[second], obs_var[second], members)
-    recorded = jnp.zeros_like(priors).at[first].set(y0).at[second].set(y1)
-
-    my_cols = (slab_index * sub_count + sub_index) * cols_dev + jnp.arange(
+    y0 = pick(priors, first)
+    home0 = pick(obs_home, first)
+    home1 = pick(obs_home, second)
+    stats0 = obs_statistics(y0, pick(obs_value, first), pick(obs_var, first), members)
+    y1 = update_pool(pick(priors, second), home1, *stats0, home0, nblocks, decays)
+    stats1 = obs_statistics(y1, pick(obs_value, second), pick(obs_var, second), members)
+    which = jnp.arange(BATCHES, dtype=jnp.int32)[:, None, None]
+    recorded = jnp.where(which == first, y0[None], y1[None])
+
+    col_blocks = ((slab_index * sub_count + sub_index) * cols_dev + jnp.arange(
         cols_dev, dtype=jnp.int32
-    )
-    near = [jnp.mod(slab_index + d, slab_count) for d in (-1, 0, 1)]
-    for batch_id, stats in ((first, stats0), (second, stats1)):
+    )) // BLK
+    near = jnp.mod(slab_index + jnp.arange(-1, 2, dtype=jnp.int32), slab_count)
+    matches = (owners[:, None, None, :] == near[None, :, None, None]) & (
+        slot_rank[:, None, None, :] == jnp.arange(capacity, dtype=jnp.int32)[None, None, :, None]
+    )
+    near_obs = jnp.sum(
+        jnp.where(matches, jnp.arange(owners.shape[1], dtype=jnp.int32), 0), axis=3
+    ).reshape(BATCHES, -1)
+    near_valid = jnp.any(matches, axis=3).reshape(BATCHES, -1)
+    for batch_id, homes, stats in ((first, home0, stats0), (second, home1, stats1)):
         deviations, spread, increments = stats
-        b_owners = lax.dynamic_index_in_dim(owners, batch_id, keepdims=True)
-        b_rank = lax.dynamic_index_in_dim(slot_rank, batch_id, keepdims=True)
-        tables = [slot_table(b_owners, b_rank, n, capacity) for n in near]
-        idx = jnp.concatenate([t[0][0] for t in tables])
-        valid = jnp.concatenate([t[1][0] for t in tables])
+        table = jnp.concatenate(
+            [
+                deviations.reshape(-1, width),
+                increments,
+                spread[:, None],
+                homes[:, None].astype(jnp.float32),
+            ],
+            axis=1,
+        )
+        rows = jnp.take(table, pick(near_obs, batch_id), axis=0)
         ensemble = update_state(
             ensemble,
-            my_cols,
-            deviations[idx],
-            spread[idx],
-            increments[idx],
-            obs_home[batch_id][idx],
-            valid,
+            col_blocks,
+            rows[:, :width].reshape(-1, BANDS, members),
+            rows[:, width + members],
+            rows[:, width : width + members],
+            rows[:, width + members + 1].astype(jnp.int32),
+            pick(near_valid, batch_id),
             nblocks,
             decays,
         )

time: 78.9 us -> 70.7 us (0.90)
  local copies, waits for them, and re-layouts: 16.4 us -> 11.4 us
  between operations: 5.13 us -> 2.49 us
    gather x10 -> x3, local copies, waits for them, and re-layouts: 8.65 us -> 4.7 us  [the longest x1 3.52 us: per_device(): jnp.take(gathered.reshape(sub_count * slab_count, q_rows * width), (row_o...]
    select_n x4 -> x16, other arithmetic: 0.25 us -> 2.82 us  [the longest x1 0.82 us: per_device(): recorded = jnp.where(which == first, y0[None], y1[None])]
    another operation x4 -> x2, local copies, waits for them, and re-layouts: 2.19 us -> 0.01 us  [the longest x1 2.04 us: per_device(): priors = jnp.take(gathered.reshape(-1, BANDS * members), flat, axis=0)]
    another operation x5 -> x2, other arithmetic: 2.33 us -> 0.48 us
    scatter x2 -> x0, other arithmetic: 1.27 us -> none  [per_device(): recorded = jnp.zeros_like(priors).at[first].set(y0).at[second].set(y1)]
    eq x0 -> x5, other arithmetic: none -> 0.91 us  [the longest x1 0.65 us: per_device(): recorded = jnp.where(which == first, y0[None], y1[None])]
    dot_general x12 -> x6, matrix products: 7.02 us -> 6.47 us  [the longest x2 3.54 us: update_state(): jnp.einsum('blck,km->blmc', crossed * weights[:, None], increments, preci...]
where the time goes in v7:
time: 70.7 us; the launch traced here: 70.4 us
  Pallas kernels  42.8 us (61%)
  local copies, waits for them, and re-layouts  11.4 us (16%)
  other arithmetic  7.25 us (10%)
  matrix products  6.47 us (9%)
  between operations  2.49 us (4%)
    pallas_call x1, Pallas kernels, gather_slots(): pl.pallas_call(functools.partial(gather_kernel, n_row), out_shape=jax.Sha...  42.8 us
    dot_general x2, matrix products, update_state(): jnp.einsum('blck,km->blmc', crossed * weights[:, None], increments, preci...  3.54 us
    gather x1, local copies, waits for them, and re-layouts, per_device(): jnp.take(gathered.reshape(sub_count * slab_count, q_rows * width), (row_o...  3.52 us
    dot_general x2, matrix products, update_state(): jnp.einsum('blmc,kbm->blck', layer_dev, deviations, precision=HIGHEST)  1.66 us

profile of v7, /device:TPU:1, one launch (start us, length us, event | category | flops | bytes accessed | tf_op | source)
XLA Modules:
  0.0 70.4 jit_solution(14109084707463499412)
XLA Ops:
  0.6 0.9 %copy.87 = s32[2,2,128]{1,2,0:T(8,128)S(1)} copy(s32[2,2,128]{2,1,0:T(2,128)} %bitcast.111) | data formatting | bytes 4096 | tf_op jit(solution)/shard_map/eq | solution.py:280
  1.5 0.4 fusion.26
  2.0 0.1 add_add_fusion
  2.2 0.2 fusion.27
  2.5 0.1 select_reduce_fusion
  2.6 0.1 reshape.1586
  2.7 0.7 gather_fusion.2
  3.4 0.1 reshape.1589
  3.5 0.2 iota_compare_fusion.1
  3.7 0.1 gather.17
  3.8 0.1 reshape.1572
  3.9 1.0 %copy.89 = f32[2,15,80,128]{2,0,3,1:T(2,128)S(1)} copy(f32[2,15,80,128]{3,2,1,0:T(8,128)S(1)} %copy-done.1) | data formatting | bytes 2457600 | tf_op args[0]
  4.9 0.6 gather_fusion
  5.5 0.1 bitcast_select_fusion.1
  5.6 0.7 select_n.522.picked_ref
  6.3 42.8 %shard_map.86 = f32[4,4,2,16,640]{4,3,2,1,0:T(8,128)} custom-call(f32[4,640]{1,0:T(4,128)} %select_n.522.picked_ref), custom_call_target="tpu_custom_call" | custom-call | tf_op jit(solution)/shard_map/pallas_call | solution.py:242
  49.2 3.5 %gather_fusion.1 = f32[512,640]{1,0:T(8,128)S(1)} fusion(f32[512,640]{1,0:T(8,128)} %bitcast.98, s32[1024]{0:T(1024)S(1)} %pad_clamp_fusion.2), kind=kCustom, calls=%fused_computation.3 | custom fusion | bytes 2623488 | tf_op jit(solution)/shard_map/jit(_take)/gather | solution.py:300
  52.8 0.2 broadcast_select_fusion
  52.9 0.7 fusion.16
  53.7 0.6 fusion.80
  55.6 0.1 fusion.79
  55.7 0.1 copy.92
  56.0 0.1 copy.98
  56.1 0.1 copy-done.6
  56.3 0.6 fusion.20
  56.9 0.6 convolution_multiply_fusion
  57.6 0.6 fusion.77
  58.2 0.7 iota_compare_fusion.2
  58.9 0.8 %broadcast_select_fusion.1 = f32[2,256,160]{1,2,0:T(8,128)} fusion(f32[256,160]{0,1:T(8,128)S(1)} %bitcast.99, f32[256,160]{0,1:T(8,128)S(1)} %copy.92, pred[2]{0:T(512)(128)(4,1)S(1)} %iota_compare_fusion.2), kind=kLoop, calls=%fused_computation.54 | loop fusion | flops 81920 | bytes 655362 | tf_op jit(solution)/shard_map/jit(_where)/select_n | solution.py:319
  59.7 0.1 copy.93
  59.9 0.1 copy.94
  60.0 0.1 copy.95
  60.1 0.1 copy.96
  60.3 0.2 pad_maximum_fusion
  60.5 0.1 broadcast_compare_fusion
  60.5 0.2 fusion.35
  60.7 0.1 select_n.540
  60.8 0.6 gather_fusion.3
  61.5 0.2 fusion.61
  61.7 0.1 copy.100
  61.9 0.1 copy.99
  62.0 0.2 multiply_reduce_fusion
  62.2 0.2 multiply_add_fusion
  62.4 0.1 copy.101
  62.5 0.1 copy.102
  62.7 0.2 pad_maximum_fusion.1
  62.9 0.1 select_n.562
  62.9 0.6 gather_fusion.4
  63.6 0.2 fusion.59
  63.8 0.1 fusion.51
  64.0 0.2 fusion.58
  64.2 0.2 and_reduce_fusion
  64.4 0.1 select_n.564
  64.4 0.1 fusion.37
  64.5 0.2 fusion.60
  64.7 0.1 select_n.542
  64.8 0.1 fusion.36
  64.9 0.1 reshape.1552
  65.0 0.1 reduce_sum.136
  65.1 0.8 %fusion.6 = f32[2,15,128,24]{2,3,1,0:T(8,128)S(1)} fusion(f32[2,15,80,128]{3,2,1,0:T(8,128)S(1)} %copy-done.1, f32[2,15,128]{2,1,0:T(8,128)S(1)} %broadcast_multiply_fusion.1, f32[2,128,24]{1,2,0:T(8,128)S(1)} %fusion.36, f32[24,2,80,1]{2,1,0,3:T(2,128)S(1)} %bitcast.109), kind=kOutput, calls=%fused_computation.14 | convolution fusion | flops 88872960 | bytes 1652736 | tf_op jit(solution)/shard_map/blmc,kbm->blck/dot_general | solution.py:76
  65.9 1.3 %fusion.81 = (f32[2,15,128]{2,1,0:T(8,128)S(1)}, f32[2,15,80,128]{3,2,1,0:T(8,128)S(1)}) fusion(f32[2,15,80,128]{3,2,1,0:T(8,128)S(1)} %copy-done.1, f32[2,15,128,24]{2,3,1,0:T(8,128)S(1)} %fusion.6, f32[24,242]{1,0:T(8,128)S(1)} %broadcast_select_fusion.3), kind=kOutput, calls=%fused_computation.239 | convolution fusion | flops 89084160 | bytes 2853888 | tf_op jit(solution)/shard_map/blck,km->blmc/dot_general | solution.py:77
  67.2 0.1 reshape.1555
  67.3 0.8 %fusion.9 = f32[2,15,128,24]{2,3,1,0:T(8,128)S(1)} fusion(f32[2,15,80,128]{3,2,1,0:T(8,128)S(1)} %get-tuple-element.53, f32[2,15,128]{2,1,0:T(8,128)S(1)} %broadcast_multiply_fusion, f32[2,128,24]{1,2,0:T(8,128)S(1)} %fusion.37, f32[24,2,80,1]{2,1,0,3:T(2,128)S(1)} %bitcast.110), kind=kOutput, calls=%fused_computation.15 | convolution fusion | flops 88872960 | bytes 1652736 | tf_op jit(solution)/shard_map/blmc,kbm->blck/dot_general | solution.py:76
  68.1 2.3 %fusion = f32[2,15,80,128]{3,2,1,0:T(8,128)} fusion(f32[2,15,80,128]{3,2,1,0:T(8,128)S(1)} %get-tuple-element.53, f32[2,15,128,24]{2,3,1,0:T(8,128)S(1)} %fusion.9, f32[24,242]{1,0:T(8,128)S(1)} %broadcast_select_fusion.2), kind=kOutput, calls=%fused_computation.6 | convolution fusion | flops 88780800 | bytes 2838528 | tf_op jit(solution)/shard_map/blck,km->blmc/dot_general | solution.py:77
  (61 shorter events, 0.8 us)
Async XLA Ops:
  0.6 1.6 %copy-start.2 = (s32[2,256,1]{1,2,0:T(1,128)S(1)}, s32[2,256,1]{1,2,0:T(1,128)}, u32[]{:S(2)}) copy-start(s32[2,256,1]{1,2,0:T(1,128)} %param.12) | copy-start | bytes 6148
  0.6 2.1 %copy-start = (s32[2,256]{1,0:T(2,128)S(1)}, s32[2,256]{1,0:T(2,128)}, u32[]{:S(2)}) copy-start(s32[2,256]{1,0:T(2,128)} %param.13) | copy-start | bytes 6148
  2.0 1.9 %copy-start.1 = (f32[2,15,80,128]{3,2,1,0:T(8,128)S(1)}, f32[2,15,80,128]{3,2,1,0:T(8,128)}, u32[]{:S(2)}) copy-start(f32[2,15,80,128]{3,2,1,0:T(8,128)} %param.9) | copy-start | bytes 3686404
  52.9 0.7 %copy-start.3 = (s32[2]{0:T(128)S(1)}, s32[2]{0:T(128)}, u32[]{:S(2)}) copy-start(s32[2]{0:T(128)} %param.15) | copy-start | bytes 28
  53.6 2.2 %copy-start.4 = (f32[2,256]{1,0:T(2,128)S(1)}, f32[2,256]{1,0:T(2,128)}, u32[]{:S(2)}) copy-start(f32[2,256]{1,0:T(2,128)} %param.10) | copy-start | bytes 6148
  53.7 2.2 %copy-start.5 = (f32[2,256]{1,0:T(2,128)S(1)}, f32[2,256]{1,0:T(2,128)}, u32[]{:S(2)}) copy-start(f32[2,256]{1,0:T(2,128)} %param.11) | copy-start | bytes 6148
  55.6 0.7 copy-start.6

commit v8 on v7

--- a/solution.py
+++ b/solution.py
@@ -287,11 +287,11 @@
     slot_level = slot_obs % levels_count
     holder = slot_column // cols_dev
     local_col = slot_column % cols_dev
-    picked = ensemble[:, slot_level, :, local_col]
-    retain = slot_valid & (holder == sub_index)
-    picked = jnp.where(retain[:, :, None, None], picked, 0.0).reshape(
-        BATCHES * capacity, BANDS * members
-    )
+    levels = jnp.take(ensemble, slot_level.reshape(-1), axis=1)
+    retain = (slot_valid & (holder == sub_index)).reshape(-1)
+    chosen = (jnp.arange(cols_dev, dtype=jnp.int32)[None, :] == local_col.reshape(-1, 1)) & retain[:, None]
+    picked = jnp.sum(jnp.where(chosen[None, :, None, :], levels, 0.0), axis=3)
+    picked = jnp.transpose(picked, (1, 0, 2)).reshape(BATCHES * capacity, BANDS * members)
     n_row = 32 if slab_count % 32 == 0 else slab_count
     gathered = gather_slots(picked, slab_count, sub_count, n_row)
     q_rows = BATCHES * capacity // sub_count

time: 70.7 us -> 70.4 us (level)
  local copies, waits for them, and re-layouts: 11.4 us -> 10.4 us
  other arithmetic: 7.25 us -> 8 us
    unnamed x18 -> x17, local copies, waits for them, and re-layouts: 1.2 us -> 0.17 us
    reduce_sum x0 -> x1, other arithmetic: none -> 0.72 us  [per_device(): picked = jnp.sum(jnp.where(chosen[None, :, None, :], levels, 0.0), axis=3)]
    select_n x2 -> x0, local copies, waits for them, and re-layouts: 0.71 us -> none  [per_device(): jnp.where(retain[:, :, None, None], picked, 0.0)]
where the time goes in v8:
time: 70.4 us; the launch traced here: 70.1 us
  Pallas kernels  42.8 us (61%)
  local copies, waits for them, and re-layouts  10.4 us (15%)
  other arithmetic  8 us (11%)
  matrix products  6.48 us (9%)
  between operations  2.5 us (4%)
    pallas_call x1, Pallas kernels, gather_slots(): pl.pallas_call(functools.partial(gather_kernel, n_row), out_shape=jax.Sha...  42.8 us
    dot_general x2, matrix products, update_state(): jnp.einsum('blck,km->blmc', crossed * weights[:, None], increments, preci...  3.54 us
    gather x1, local copies, waits for them, and re-layouts, per_device(): jnp.take(gathered.reshape(sub_count * slab_count, q_rows * width), (row_o...  3.52 us
    dot_general x2, matrix products, update_state(): jnp.einsum('blmc,kbm->blck', layer_dev, deviations, precision=HIGHEST)  1.66 us

profile of v8, /device:TPU:1, one launch (start us, length us, event | category | flops | bytes accessed | tf_op | source)
XLA Modules:
  0.0 70.1 jit_solution(14379293102712429807)
XLA Ops:
  0.6 0.9 %copy.74 = s32[2,2,128]{1,2,0:T(8,128)S(1)} copy(s32[2,2,128]{2,1,0:T(2,128)} %bitcast.102) | data formatting | bytes 4096 | tf_op jit(solution)/shard_map/eq | solution.py:280
  1.5 0.4 fusion.26
  2.0 0.1 add_add_fusion
  2.2 0.2 fusion.27
  2.5 0.1 select_reduce_fusion.1
  2.6 0.1 reshape.1599
  2.7 0.7 gather_fusion.2
  3.4 0.1 reduce_sum.141
  3.5 0.2 iota_compare_fusion.1
  3.6 0.1 reduce_or.21
  3.8 0.1 fusion.62
  3.9 0.1 rem.185
  4.0 0.6 gather_fusion
  4.6 0.7 %select_reduce_fusion = f32[16,2,80]{2,1,0:T(2,128)S(1)} fusion(f32[16,2,80,128]{3,2,1,0:T(8,128)S(1)} %gather_fusion, pred[16]{0:T(512)(128)(4,1)S(1)} %get-tuple-element.53, pred[16,128]{1,0:T(8,128)(4,1)S(1)} %fusion.62), kind=kLoop, calls=%fused_computation.9 | loop fusion | flops 980480 | bytes 1323024 | tf_op jit(solution)/shard_map/reduce_sum | solution.py:293
  5.3 0.7 %reshape_reshape.6.picked_ref = f32[4,640]{1,0:T(4,128)} reshape(f32[16,2,80]{2,1,0:T(2,128)S(1)} %select_reduce_fusion) | data formatting | bytes 20480 | tf_op jit(solution)/shard_map/reshape;reshape | solution.py:259
  6.0 42.8 %shard_map.86 = f32[4,4,2,16,640]{4,3,2,1,0:T(8,128)} custom-call(f32[4,640]{1,0:T(4,128)} %reshape_reshape.6.picked_ref), custom_call_target="tpu_custom_call" | custom-call | tf_op jit(solution)/shard_map/pallas_call | solution.py:242
  48.9 3.5 %gather_fusion.1 = f32[512,640]{1,0:T(8,128)S(1)} fusion(f32[512,640]{1,0:T(8,128)} %bitcast.89, s32[1024]{0:T(1024)S(1)} %pad_clamp_fusion.2), kind=kCustom, calls=%fused_computation.3 | custom fusion | bytes 2623488 | tf_op jit(solution)/shard_map/jit(_take)/gather | solution.py:300
  52.5 0.2 broadcast_select_fusion
  52.7 0.7 fusion.16
  53.4 0.6 fusion.79
  55.3 0.1 fusion.78
  55.4 0.1 copy.76
  55.7 0.1 copy.82
  55.9 0.1 copy-done.6
  56.0 0.6 fusion.20
  56.7 0.6 convolution_multiply_fusion
  57.3 0.6 fusion.76
  58.0 0.7 iota_compare_fusion.3
  58.6 0.8 %broadcast_select_fusion.1 = f32[2,256,160]{1,2,0:T(8,128)} fusion(f32[256,160]{0,1:T(8,128)S(1)} %bitcast.90, f32[256,160]{0,1:T(8,128)S(1)} %copy.76, pred[2]{0:T(512)(128)(4,1)S(1)} %iota_compare_fusion.3), kind=kLoop, calls=%fused_computation.55 | loop fusion | flops 81920 | bytes 655362 | tf_op jit(solution)/shard_map/jit(_where)/select_n | solution.py:319
  59.5 0.1 copy.77
  59.6 0.1 copy.78
  59.7 0.1 copy.79
  59.9 0.1 copy.80
  60.0 0.2 pad_maximum_fusion
  60.2 0.1 broadcast_compare_fusion
  60.3 0.2 fusion.35
  60.5 0.1 select_n.531
  60.6 0.6 gather_fusion.3
  61.3 0.2 fusion.61
  61.5 0.1 copy.84
  61.6 0.1 copy.83
  61.7 0.2 multiply_reduce_fusion
  61.9 0.2 multiply_add_fusion
  62.1 0.1 copy.85
  62.3 0.1 copy.86
  62.4 0.2 pad_maximum_fusion.1
  62.6 0.1 select_n.553
  62.7 0.6 gather_fusion.4
  63.4 0.2 fusion.59
  63.6 0.1 fusion.51
  63.7 0.2 fusion.58
  63.9 0.2 and_reduce_fusion
  64.1 0.1 select_n.555
  64.2 0.1 fusion.37
  64.3 0.2 fusion.60
  64.5 0.1 select_n.533
  64.5 0.1 fusion.36
  64.6 0.1 reshape.1563
  64.7 0.1 reduce_sum.149
  64.8 0.8 %fusion.6 = f32[2,15,128,24]{2,3,1,0:T(8,128)S(1)} fusion(f32[2,15,80,128]{3,2,1,0:T(8,128)S(1)} %copy-done.1, f32[2,15,128]{2,1,0:T(8,128)S(1)} %broadcast_multiply_fusion.1, f32[2,128,24]{1,2,0:T(8,128)S(1)} %fusion.36, f32[24,2,80,1]{2,1,0,3:T(2,128)S(1)} %bitcast.100), kind=kOutput, calls=%fused_computation.15 | convolution fusion | flops 88872960 | bytes 1652736 | tf_op jit(solution)/shard_map/blmc,kbm->blck/dot_general | solution.py:76
  65.7 1.3 %fusion.80 = (f32[2,15,128]{2,1,0:T(8,128)S(1)}, f32[2,15,80,128]{3,2,1,0:T(8,128)S(1)}) fusion(f32[2,15,80,128]{3,2,1,0:T(8,128)S(1)} %copy-done.1, f32[2,15,128,24]{2,3,1,0:T(8,128)S(1)} %fusion.6, f32[24,242]{1,0:T(8,128)S(1)} %broadcast_select_fusion.3), kind=kOutput, calls=%fused_computation.238 | convolution fusion | flops 89084160 | bytes 2853888 | tf_op jit(solution)/shard_map/blck,km->blmc/dot_general | solution.py:77
  66.9 0.1 reshape.1566
  67.0 0.8 %fusion.9 = f32[2,15,128,24]{2,3,1,0:T(8,128)S(1)} fusion(f32[2,15,80,128]{3,2,1,0:T(8,128)S(1)} %get-tuple-element.56, f32[2,15,128]{2,1,0:T(8,128)S(1)} %broadcast_multiply_fusion, f32[2,128,24]{1,2,0:T(8,128)S(1)} %fusion.37, f32[24,2,80,1]{2,1,0,3:T(2,128)S(1)} %bitcast.101), kind=kOutput, calls=%fused_computation.16 | convolution fusion | flops 88872960 | bytes 1652736 | tf_op jit(solution)/shard_map/blmc,kbm->blck/dot_general | solution.py:76
  67.9 2.3 %fusion = f32[2,15,80,128]{3,2,1,0:T(8,128)} fusion(f32[2,15,80,128]{3,2,1,0:T(8,128)S(1)} %get-tuple-element.56, f32[2,15,128,24]{2,3,1,0:T(8,128)S(1)} %fusion.9, f32[24,242]{1,0:T(8,128)S(1)} %broadcast_select_fusion.2), kind=kOutput, calls=%fused_computation.6 | convolution fusion | flops 88780800 | bytes 2838528 | tf_op jit(solution)/shard_map/blck,km->blmc/dot_general | solution.py:77
  (63 shorter events, 0.8 us)
Async XLA Ops:
  0.6 1.6 %copy-start.2 = (s32[2,256,1]{1,2,0:T(1,128)S(1)}, s32[2,256,1]{1,2,0:T(1,128)}, u32[]{:S(2)}) copy-start(s32[2,256,1]{1,2,0:T(1,128)} %param.12) | copy-start | bytes 6148
  0.6 2.1 %copy-start = (s32[2,256]{1,0:T(2,128)S(1)}, s32[2,256]{1,0:T(2,128)}, u32[]{:S(2)}) copy-start(s32[2,256]{1,0:T(2,128)} %param.13) | copy-start | bytes 6148
  2.0 2.0 %copy-start.1 = (f32[2,15,80,128]{3,2,1,0:T(8,128)S(1)}, f32[2,15,80,128]{3,2,1,0:T(8,128)}, u32[]{:S(2)}) copy-start(f32[2,15,80,128]{3,2,1,0:T(8,128)} %param.9) | copy-start | bytes 3686404
  52.7 0.7 %copy-start.3 = (s32[2]{0:T(128)S(1)}, s32[2]{0:T(128)}, u32[]{:S(2)}) copy-start(s32[2]{0:T(128)} %param.15) | copy-start | bytes 28
  53.4 2.2 %copy-start.4 = (f32[2,256]{1,0:T(2,128)S(1)}, f32[2,256]{1,0:T(2,128)}, u32[]{:S(2)}) copy-start(f32[2,256]{1,0:T(2,128)} %param.10) | copy-start | bytes 6148
  53.4 2.2 %copy-start.5 = (f32[2,256]{1,0:T(2,128)S(1)}, f32[2,256]{1,0:T(2,128)}, u32[]{:S(2)}) copy-start(f32[2,256]{1,0:T(2,128)} %param.11) | copy-start | bytes 6148
  55.3 0.7 copy-start.6

commit v9 on v8

--- a/solution.py
+++ b/solution.py
@@ -15,7 +15,7 @@
 CAP = 8
 
 
-HIGHEST = lax.Precision.HIGHEST
+PRODUCT = lax.Precision.HIGH
 
 
 def gc_weight(first, second, nblocks, length):
@@ -61,8 +61,8 @@
     weights = jnp.stack(
         [gc_weight(pool_homes[:, None], obs_homes[None, :], nblocks, decay) for decay in decays]
     ) / ((members - 1) * spread)[None, None, :]
-    crossed = jnp.einsum("pbm,kbm->bpk", pool_dev, deviations, precision=HIGHEST)
-    change = jnp.einsum("bpk,km->pbm", crossed * weights, increments, precision=HIGHEST)
+    crossed = jnp.einsum("pbm,kbm->bpk", pool_dev, deviations, precision=PRODUCT)
+    change = jnp.einsum("bpk,km->pbm", crossed * weights, increments, precision=PRODUCT)
     return (banded + change).reshape(pool.shape)
 
 
@@ -73,8 +73,8 @@
         [gc_weight(col_blocks[:, None], obs_homes[None, :], nblocks, decay) for decay in decays]
     ) / ((members - 1) * spread)[None, None, :]
     weights = jnp.where(valid[None, None, :], weights, 0.0)
-    crossed = jnp.einsum("blmc,kbm->blck", layer_dev, deviations, precision=HIGHEST)
-    change = jnp.einsum("blck,km->blmc", crossed * weights[:, None], increments, precision=HIGHEST)
+    crossed = jnp.einsum("blmc,kbm->blck", layer_dev, deviations, precision=PRODUCT)
+    change = jnp.einsum("blck,km->blmc", crossed * weights[:, None], increments, precision=PRODUCT)
     return ensemble + change
 
 

time: 70.4 us -> 68.3 us (0.970)
  matrix products: 6.48 us -> 4.4 us
    dot_general x4, matrix products: 2.94 us -> 1.75 us  [the longest x2 0.9 us: update_state(): jnp.einsum('blmc,kbm->blck', layer_dev, deviations, precision=PRODUCT)]
    dot_general x2, matrix products: 3.54 us -> 2.65 us  [update_state(): jnp.einsum('blck,km->blmc', crossed * weights[:, None], increments, preci...]
where the time goes in v9:
time: 68.3 us; the launch traced here: 68.1 us
  Pallas kernels  42.8 us (63%)
  local copies, waits for them, and re-layouts  10.4 us (15%)
  other arithmetic  8 us (12%)
  matrix products  4.4 us (6%)
  between operations  2.5 us (4%)
    pallas_call x1, Pallas kernels, gather_slots(): pl.pallas_call(functools.partial(gather_kernel, n_row), out_shape=jax.Sha...  42.8 us
    gather x1, local copies, waits for them, and re-layouts, per_device(): jnp.take(gathered.reshape(sub_count * slab_count, q_rows * width), (row_o...  3.52 us
    dot_general x2, matrix products, update_state(): jnp.einsum('blck,km->blmc', crossed * weights[:, None], increments, preci...  2.65 us

profile of v9, /device:TPU:1, one launch (start us, length us, event | category | flops | bytes accessed | tf_op | source)
XLA Modules:
  0.0 68.1 jit_solution(13597822226082995203)
XLA Ops:
  0.6 0.9 %copy.74 = s32[2,2,128]{1,2,0:T(8,128)S(1)} copy(s32[2,2,128]{2,1,0:T(2,128)} %bitcast.102) | data formatting | bytes 4096 | tf_op jit(solution)/shard_map/eq | solution.py:280
  1.5 0.4 fusion.26
  2.0 0.1 add_add_fusion
  2.2 0.2 fusion.27
  2.5 0.1 select_reduce_fusion.1
  2.6 0.1 reshape.1599
  2.7 0.7 %gather_fusion.2 = s32[16]{0:T(128)S(1)} fusion(s32[2,256]{1,0:T(2,128)S(1)} %copy-done, s32[16]{0:T(128)S(1)} %reshape.1599), kind=kCustom, calls=%fused_computation.4 | custom fusion | bytes 256 | tf_op jit(solution)/shard_map/jit(take_along_axis)/gather | solution.py:286
  3.4 0.1 reduce_sum.141
  3.5 0.2 iota_compare_fusion.1
  3.6 0.1 reduce_or.21
  3.8 0.1 fusion.62
  3.9 0.1 rem.185
  4.0 0.6 gather_fusion
  4.6 0.7 %select_reduce_fusion = f32[16,2,80]{2,1,0:T(2,128)S(1)} fusion(f32[16,2,80,128]{3,2,1,0:T(8,128)S(1)} %gather_fusion, pred[16]{0:T(512)(128)(4,1)S(1)} %get-tuple-element.53, pred[16,128]{1,0:T(8,128)(4,1)S(1)} %fusion.62), kind=kLoop, calls=%fused_computation.9 | loop fusion | flops 980480 | bytes 1323024 | tf_op jit(solution)/shard_map/reduce_sum | solution.py:293
  5.3 0.7 %reshape_reshape.6.picked_ref = f32[4,640]{1,0:T(4,128)} reshape(f32[16,2,80]{2,1,0:T(2,128)S(1)} %select_reduce_fusion) | data formatting | bytes 20480 | tf_op jit(solution)/shard_map/reshape;reshape | solution.py:259
  6.0 42.8 %shard_map.86 = f32[4,4,2,16,640]{4,3,2,1,0:T(8,128)} custom-call(f32[4,640]{1,0:T(4,128)} %reshape_reshape.6.picked_ref), custom_call_target="tpu_custom_call" | custom-call | tf_op jit(solution)/shard_map/pallas_call | solution.py:242
  48.9 3.5 %gather_fusion.1 = f32[512,640]{1,0:T(8,128)S(1)} fusion(f32[512,640]{1,0:T(8,128)} %bitcast.89, s32[1024]{0:T(1024)S(1)} %pad_clamp_fusion.2), kind=kCustom, calls=%fused_computation.3 | custom fusion | bytes 2623488 | tf_op jit(solution)/shard_map/jit(_take)/gather | solution.py:300
  52.5 0.2 broadcast_select_fusion
  52.7 0.7 %fusion.16 = f32[512,160]{1,0:T(8,128)S(1)} fusion(f32[512,640]{1,0:T(8,128)S(1)} %broadcast_select_fusion, pred[512]{0:T(512)(128)(4,1)S(1)} %get-tuple-element.38, pred[512]{0:T(512)(128)(4,1)S(1)} %get-tuple-element.37, pred[512]{0:T(512)(128)(4,1)S(1)} %get-tuple-element.12), kind=kLoop, calls=%fused_computation.24 | loop fusion | flops 245760 | bytes 1639936 | tf_op jit(solution)/shard_map/jit(_where)/select_n | solution.py:308
  53.4 0.6 fusion.79
  55.3 0.1 fusion.78
  55.4 0.1 copy.76
  55.7 0.1 copy.82
  55.9 0.1 copy-done.6
  56.0 0.6 fusion.20
  56.7 0.4 convolution_multiply_fusion
  57.1 0.4 fusion.76
  57.5 0.7 iota_compare_fusion.3
  58.2 0.8 %broadcast_select_fusion.1 = f32[2,256,160]{1,2,0:T(8,128)} fusion(f32[256,160]{0,1:T(8,128)S(1)} %bitcast.90, f32[256,160]{0,1:T(8,128)S(1)} %copy.76, pred[2]{0:T(512)(128)(4,1)S(1)} %iota_compare_fusion.3), kind=kLoop, calls=%fused_computation.55 | loop fusion | flops 81920 | bytes 655362 | tf_op jit(solution)/shard_map/jit(_where)/select_n | solution.py:319
  59.0 0.1 copy.77
  59.2 0.1 copy.78
  59.3 0.1 copy.79
  59.4 0.1 copy.80
  59.6 0.2 pad_maximum_fusion
  59.8 0.1 broadcast_compare_fusion
  59.9 0.2 fusion.35
  60.1 0.1 select_n.531
  60.2 0.6 gather_fusion.3
  60.8 0.2 fusion.61
  61.1 0.1 copy.84
  61.2 0.1 copy.83
  61.3 0.2 multiply_reduce_fusion
  61.5 0.2 multiply_add_fusion
  61.7 0.1 copy.85
  61.8 0.1 copy.86
  62.0 0.2 pad_maximum_fusion.1
  62.2 0.1 select_n.553
  62.3 0.6 gather_fusion.4
  62.9 0.2 fusion.59
  63.1 0.1 fusion.51
  63.3 0.2 fusion.58
  63.5 0.2 and_reduce_fusion
  63.7 0.1 select_n.555
  63.8 0.1 fusion.37
  63.8 0.2 fusion.60
  64.0 0.1 select_n.533
  64.1 0.1 fusion.36
  64.2 0.1 reshape.1563
  64.3 0.1 reduce_sum.149
  64.4 0.4 fusion.6
  64.8 0.8 %fusion.80 = (f32[2,15,128]{2,1,0:T(8,128)S(1)}, f32[2,15,80,128]{3,2,1,0:T(8,128)S(1)}) fusion(f32[2,15,80,128]{3,2,1,0:T(8,128)S(1)} %copy-done.1, f32[2,15,128,24]{2,3,1,0:T(8,128)S(1)} %fusion.6, f32[24,242]{1,0:T(8,128)S(1)} %broadcast_select_fusion.3), kind=kOutput, calls=%fused_computation.238 | convolution fusion | flops 44847360 | bytes 2853888 | tf_op jit(solution)/shard_map/blck,km->blmc/dot_general | solution.py:77
  65.7 0.1 reshape.1566
  65.8 0.5 fusion.9
  66.2 1.8 %fusion = f32[2,15,80,128]{3,2,1,0:T(8,128)} fusion(f32[2,15,80,128]{3,2,1,0:T(8,128)S(1)} %get-tuple-element.56, f32[2,15,128,24]{2,3,1,0:T(8,128)S(1)} %fusion.9, f32[24,242]{1,0:T(8,128)S(1)} %broadcast_select_fusion.2), kind=kOutput, calls=%fused_computation.6 | convolution fusion | flops 44544000 | bytes 2838528 | tf_op jit(solution)/shard_map/blck,km->blmc/dot_general | solution.py:77
  (63 shorter events, 0.8 us)
Async XLA Ops:
  0.6 1.6 %copy-start.2 = (s32[2,256,1]{1,2,0:T(1,128)S(1)}, s32[2,256,1]{1,2,0:T(1,128)}, u32[]{:S(2)}) copy-start(s32[2,256,1]{1,2,0:T(1,128)} %param.12) | copy-start | bytes 6148
  0.6 2.1 %copy-start = (s32[2,256]{1,0:T(2,128)S(1)}, s32[2,256]{1,0:T(2,128)}, u32[]{:S(2)}) copy-start(s32[2,256]{1,0:T(2,128)} %param.13) | copy-start | bytes 6148
  2.0 2.0 %copy-start.1 = (f32[2,15,80,128]{3,2,1,0:T(8,128)S(1)}, f32[2,15,80,128]{3,2,1,0:T(8,128)}, u32[]{:S(2)}) copy-start(f32[2,15,80,128]{3,2,1,0:T(8,128)} %param.9) | copy-start | bytes 3686404
  52.7 0.7 %copy-start.3 = (s32[2]{0:T(128)S(1)}, s32[2]{0:T(128)}, u32[]{:S(2)}) copy-start(s32[2]{0:T(128)} %param.15) | copy-start | bytes 28
  53.4 2.2 %copy-start.4 = (f32[2,256]{1,0:T(2,128)S(1)}, f32[2,256]{1,0:T(2,128)}, u32[]{:S(2)}) copy-start(f32[2,256]{1,0:T(2,128)} %param.10) | copy-start | bytes 6148
  53.4 2.2 %copy-start.5 = (f32[2,256]{1,0:T(2,128)S(1)}, f32[2,256]{1,0:T(2,128)}, u32[]{:S(2)}) copy-start(f32[2,256]{1,0:T(2,128)} %param.11) | copy-start | bytes 6148
  55.3 0.7 %copy-start.6 = (s32[2,256]{1,0:T(2,128)S(1)}, s32[2,256]{1,0:T(2,128)}, u32[]{:S(2)}) copy-start(s32[2,256]{1,0:T(2,128)} %param.14) | copy-start | bytes 6148

commit v10 on v9

--- a/solution.py
+++ b/solution.py
@@ -122,12 +122,15 @@
     for d in range(1, n_sub):
         pl.semaphore_signal(barrier, 1, device_id=(s, (u + d) % n_sub), device_id_type=MESH)
 
-    def greet(d, c):
-        dev = (row * n_row + (loc + d) % n_row, u)
+    def far(i):
+        return n_row // 2 + (2 * (i % 2) - 1) * ((i + 1) // 2)
+
+    def greet(i, c):
+        dev = (row * n_row + (loc + far(i)) % n_row, u)
         pl.semaphore_signal(barrier, 1, device_id=dev, device_id_type=MESH)
         return c
 
-    lax.fori_loop(1, n_row, greet, 0)
+    lax.fori_loop(0, n_row - 1, greet, 0)
     for d in range(1, n_rows):
         dev = (((row + d) % n_rows) * n_row + loc, u)
         pl.semaphore_signal(barrier, 1, device_id=dev, device_id_type=MESH)
@@ -156,16 +159,22 @@
         src = row * n_row + j
         return copy(own(src), own(src), send_a.at[j], sem_a.at[j], (src, u))
 
-    def start_a(d, c):
-        to_a(d).start()
+    def start_a(i, c):
+        to_a(far(i)).start()
         return c
 
-    def wait_a(d, c):
-        from_a(d).wait_recv()
-        return c
-
-    lax.fori_loop(1, n_row, start_a, 0)
-    lax.fori_loop(1, n_row, wait_a, 0)
+    def wait_half(h):
+        def body(j, c):
+            @pl.when(h * half + j != loc)
+            def _():
+                from_a((h * half + j - loc + n_row) % n_row).wait_recv()
+
+            return c
+
+        lax.fori_loop(0, half, body, 0)
+
+    lax.fori_loop(0, n_row - 1, start_a, 0)
+    mine = loc // half
 
     def peer_x(d):
         r = (row + d) % n_rows
@@ -207,10 +216,20 @@
         q, dev = peer_y(d)
         return copy(out_ref.at[q, :, 0], out_ref.at[q, :, 0], send_c.at[1, q], sem_c.at[1, q], dev)
 
-    for d in range(1, n_rows):
-        to_b1(d).start()
-    for d in range(1, n_sub):
-        to_c1(d).start()
+    def start_b1():
+        for d in range(1, n_rows):
+            to_b1(d).start()
+
+    def start_c1():
+        for d in range(1, n_sub):
+            to_c1(d).start()
+
+    wait_half(mine)
+    pl.when(mine == 0)(start_b1)
+    pl.when(mine == 1)(start_c1)
+    wait_half(1 - mine)
+    pl.when(mine == 0)(start_c1)
+    pl.when(mine == 1)(start_b1)
     for d in range(1, n_sub):
         from_c1(d).wait_recv()
     for d in range(1, n_rows):

time: 68.3 us -> 68.5 us (level)
  no operation moved by 1% of the time
where the time goes in v10:
time: 68.5 us; the launch traced here: 68.2 us
  Pallas kernels  42.9 us (63%)
  local copies, waits for them, and re-layouts  10.4 us (15%)
  other arithmetic  8 us (12%)
  matrix products  4.39 us (6%)
  between operations  2.5 us (4%)
    pallas_call x1, Pallas kernels, gather_slots(): pl.pallas_call(functools.partial(gather_kernel, n_row), out_shape=jax.Sha...  42.9 us
    gather x1, local copies, waits for them, and re-layouts, per_device(): jnp.take(gathered.reshape(sub_count * slab_count, q_rows * width), (row_o...  3.52 us
    dot_general x2, matrix products, update_state(): jnp.einsum('blck,km->blmc', crossed * weights[:, None], increments, preci...  2.65 us

profile of v10, /device:TPU:1, one launch (start us, length us, event | category | flops | bytes accessed | tf_op | source)
XLA Modules:
  0.0 68.2 jit_solution(4415885037488446077)
XLA Ops:
  0.6 0.9 %copy.74 = s32[2,2,128]{1,2,0:T(8,128)S(1)} copy(s32[2,2,128]{2,1,0:T(2,128)} %bitcast.102) | data formatting | bytes 4096 | tf_op jit(solution)/shard_map/eq | solution.py:299
  1.5 0.4 fusion.26
  2.0 0.1 add_add_fusion
  2.2 0.2 fusion.27
  2.5 0.1 select_reduce_fusion.1
  2.6 0.1 reshape.1599
  2.7 0.7 %gather_fusion.2 = s32[16]{0:T(128)S(1)} fusion(s32[2,256]{1,0:T(2,128)S(1)} %copy-done, s32[16]{0:T(128)S(1)} %reshape.1599), kind=kCustom, calls=%fused_computation.4 | custom fusion | bytes 256 | tf_op jit(solution)/shard_map/jit(take_along_axis)/gather | solution.py:305
  3.4 0.1 reduce_sum.141
  3.5 0.2 iota_compare_fusion.1
  3.6 0.1 reduce_or.21
  3.8 0.1 fusion.62
  3.9 0.1 rem.185
  4.0 0.6 gather_fusion
  4.6 0.7 %select_reduce_fusion = f32[16,2,80]{2,1,0:T(2,128)S(1)} fusion(f32[16,2,80,128]{3,2,1,0:T(8,128)S(1)} %gather_fusion, pred[16]{0:T(512)(128)(4,1)S(1)} %get-tuple-element.53, pred[16,128]{1,0:T(8,128)(4,1)S(1)} %fusion.62), kind=kLoop, calls=%fused_computation.9 | loop fusion | flops 980480 | bytes 1323024 | tf_op jit(solution)/shard_map/reduce_sum | solution.py:312
  5.3 0.7 %reshape_reshape.6.picked_ref = f32[4,640]{1,0:T(4,128)} reshape(f32[16,2,80]{2,1,0:T(2,128)S(1)} %select_reduce_fusion) | data formatting | bytes 20480 | tf_op jit(solution)/shard_map/reshape;reshape | solution.py:278
  6.0 42.9 %shard_map.86 = f32[4,4,2,16,640]{4,3,2,1,0:T(8,128)} custom-call(f32[4,640]{1,0:T(4,128)} %reshape_reshape.6.picked_ref), custom_call_target="tpu_custom_call" | custom-call | tf_op jit(solution)/shard_map/pallas_call | solution.py:261
  49.1 3.5 %gather_fusion.1 = f32[512,640]{1,0:T(8,128)S(1)} fusion(f32[512,640]{1,0:T(8,128)} %bitcast.89, s32[1024]{0:T(1024)S(1)} %pad_clamp_fusion.2), kind=kCustom, calls=%fused_computation.3 | custom fusion | bytes 2623488 | tf_op jit(solution)/shard_map/jit(_take)/gather | solution.py:319
  52.6 0.2 broadcast_select_fusion
  52.8 0.7 %fusion.16 = f32[512,160]{1,0:T(8,128)S(1)} fusion(f32[512,640]{1,0:T(8,128)S(1)} %broadcast_select_fusion, pred[512]{0:T(512)(128)(4,1)S(1)} %get-tuple-element.38, pred[512]{0:T(512)(128)(4,1)S(1)} %get-tuple-element.37, pred[512]{0:T(512)(128)(4,1)S(1)} %get-tuple-element.12), kind=kLoop, calls=%fused_computation.24 | loop fusion | flops 245760 | bytes 1639936 | tf_op jit(solution)/shard_map/jit(_where)/select_n | solution.py:327
  53.6 0.6 fusion.79
  55.5 0.1 fusion.78
  55.6 0.1 copy.76
  55.9 0.1 copy.82
  56.0 0.1 copy-done.6
  56.2 0.6 fusion.20
  56.8 0.4 convolution_multiply_fusion
  57.3 0.4 fusion.76
  57.7 0.7 iota_compare_fusion.3
  58.3 0.8 %broadcast_select_fusion.1 = f32[2,256,160]{1,2,0:T(8,128)} fusion(f32[256,160]{0,1:T(8,128)S(1)} %bitcast.90, f32[256,160]{0,1:T(8,128)S(1)} %copy.76, pred[2]{0:T(512)(128)(4,1)S(1)} %iota_compare_fusion.3), kind=kLoop, calls=%fused_computation.55 | loop fusion | flops 81920 | bytes 655362 | tf_op jit(solution)/shard_map/jit(_where)/select_n | solution.py:338
  59.2 0.1 copy.77
  59.3 0.1 copy.78
  59.4 0.1 copy.79
  59.6 0.1 copy.80
  59.7 0.2 pad_maximum_fusion
  59.9 0.1 broadcast_compare_fusion
  60.0 0.2 fusion.35
  60.2 0.1 select_n.531
  60.3 0.6 gather_fusion.3
  61.0 0.2 fusion.61
  61.2 0.1 copy.84
  61.3 0.1 copy.83
  61.4 0.2 multiply_reduce_fusion
  61.6 0.2 multiply_add_fusion
  61.8 0.1 copy.85
  62.0 0.1 copy.86
  62.1 0.2 pad_maximum_fusion.1
  62.3 0.1 select_n.553
  62.4 0.6 gather_fusion.4
  63.1 0.2 fusion.59
  63.3 0.1 fusion.51
  63.4 0.2 fusion.58
  63.6 0.2 and_reduce_fusion
  63.8 0.1 select_n.555
  63.9 0.1 fusion.37
  64.0 0.2 fusion.60
  64.2 0.1 select_n.533
  64.2 0.1 fusion.36
  64.3 0.1 reshape.1563
  64.4 0.1 reduce_sum.149
  64.5 0.4 fusion.6
  65.0 0.8 %fusion.80 = (f32[2,15,128]{2,1,0:T(8,128)S(1)}, f32[2,15,80,128]{3,2,1,0:T(8,128)S(1)}) fusion(f32[2,15,80,128]{3,2,1,0:T(8,128)S(1)} %copy-done.1, f32[2,15,128,24]{2,3,1,0:T(8,128)S(1)} %fusion.6, f32[24,242]{1,0:T(8,128)S(1)} %broadcast_select_fusion.3), kind=kOutput, calls=%fused_computation.238 | convolution fusion | flops 44847360 | bytes 2853888 | tf_op jit(solution)/shard_map/blck,km->blmc/dot_general | solution.py:77
  65.8 0.1 reshape.1566
  65.9 0.5 fusion.9
  66.4 1.8 %fusion = f32[2,15,80,128]{3,2,1,0:T(8,128)} fusion(f32[2,15,80,128]{3,2,1,0:T(8,128)S(1)} %get-tuple-element.56, f32[2,15,128,24]{2,3,1,0:T(8,128)S(1)} %fusion.9, f32[24,242]{1,0:T(8,128)S(1)} %broadcast_select_fusion.2), kind=kOutput, calls=%fused_computation.6 | convolution fusion | flops 44544000 | bytes 2838528 | tf_op jit(solution)/shard_map/blck,km->blmc/dot_general | solution.py:77
  (63 shorter events, 0.8 us)
Async XLA Ops:
  0.6 1.6 %copy-start.2 = (s32[2,256,1]{1,2,0:T(1,128)S(1)}, s32[2,256,1]{1,2,0:T(1,128)}, u32[]{:S(2)}) copy-start(s32[2,256,1]{1,2,0:T(1,128)} %param.12) | copy-start | bytes 6148
  0.6 2.1 %copy-start = (s32[2,256]{1,0:T(2,128)S(1)}, s32[2,256]{1,0:T(2,128)}, u32[]{:S(2)}) copy-start(s32[2,256]{1,0:T(2,128)} %param.13) | copy-start | bytes 6148
  2.0 2.0 %copy-start.1 = (f32[2,15,80,128]{3,2,1,0:T(8,128)S(1)}, f32[2,15,80,128]{3,2,1,0:T(8,128)}, u32[]{:S(2)}) copy-start(f32[2,15,80,128]{3,2,1,0:T(8,128)} %param.9) | copy-start | bytes 3686404
  52.8 0.7 %copy-start.3 = (s32[2]{0:T(128)S(1)}, s32[2]{0:T(128)}, u32[]{:S(2)}) copy-start(s32[2]{0:T(128)} %param.15) | copy-start | bytes 28
  53.5 2.2 %copy-start.4 = (f32[2,256]{1,0:T(2,128)S(1)}, f32[2,256]{1,0:T(2,128)}, u32[]{:S(2)}) copy-start(f32[2,256]{1,0:T(2,128)} %param.10) | copy-start | bytes 6148
  53.5 2.2 %copy-start.5 = (f32[2,256]{1,0:T(2,128)S(1)}, f32[2,256]{1,0:T(2,128)}, u32[]{:S(2)}) copy-start(f32[2,256]{1,0:T(2,128)} %param.11) | copy-start | bytes 6148
  55.4 0.7 %copy-start.6 = (s32[2,256]{1,0:T(2,128)S(1)}, s32[2,256]{1,0:T(2,128)}, u32[]{:S(2)}) copy-start(s32[2,256]{1,0:T(2,128)} %param.14) | copy-start | bytes 6148

commit v11 on v9

--- a/solution.py
+++ b/solution.py
@@ -277,11 +277,9 @@
     assert 2 * span_broad + 1 <= cols_slab // BLK and slab_count >= 3
     owners = obs_owner[:, :, 0]
     obs_home = jnp.mod((owners * cols_slab + obs_column) // BLK + home_block, nblocks)
-    onehot = (owners[:, :, None] == jnp.arange(slab_count, dtype=jnp.int32)[None, None, :]).astype(
-        jnp.int32
-    )
-    running = jnp.cumsum(onehot, axis=1) - 1
-    slot_rank = jnp.sum(onehot * running, axis=2)
+    order = jnp.arange(owners.shape[1], dtype=jnp.int32)
+    earlier = (owners[:, None, :] == owners[:, :, None]) & (order[None, :] < order[:, None])[None]
+    slot_rank = jnp.sum(earlier.astype(jnp.int32), axis=2)
     slot_obs, slot_valid = slot_table(owners, slot_rank, slab_index, capacity)
     slot_column = jnp.take_along_axis(obs_column, slot_obs, axis=1)
     slot_level = slot_obs % levels_count

time: 68.3 us -> 69 us (1.010)
    eq x1 -> x0, local copies, waits for them, and re-layouts: 0.86 us -> none  [per_device(): owners[:, :, None] == jnp.arange(slab_count, dtype=jnp.int32)[None, None, :]]
    eq x1, other arithmetic: 0.01 us -> 0.79 us  [slot_table(): owners == slab_number]
where the time goes in v11:
time: 69 us; the launch traced here: 68.7 us
  Pallas kernels  42.8 us (62%)
  local copies, waits for them, and re-layouts  10.9 us (16%)
  other arithmetic  8.22 us (12%)
  matrix products  4.4 us (6%)
  between operations  2.44 us (4%)
    pallas_call x1, Pallas kernels, gather_slots(): pl.pallas_call(functools.partial(gather_kernel, n_row), out_shape=jax.Sha...  42.8 us
    gather x1, local copies, waits for them, and re-layouts, per_device(): jnp.take(gathered.reshape(sub_count * slab_count, q_rows * width), (row_o...  3.52 us
    dot_general x2, matrix products, update_state(): jnp.einsum('blck,km->blmc', crossed * weights[:, None], increments, preci...  2.66 us
    gather x2, local copies, waits for them, and re-layouts, per_device(): slot_column = jnp.take_along_axis(obs_column, slot_obs, axis=1)  1.46 us

profile of v11, /device:TPU:1, one launch (start us, length us, event | category | flops | bytes accessed | tf_op | source)
XLA Modules:
  0.0 68.7 jit_solution(4723455731128315838)
XLA Ops:
  0.6 0.8 %broadcast_compare_fusion.1 = pred[2,256]{1,0:T(4,128)(4,1)S(1)} fusion(s32[]{:T(128)S(6)} %axis_index.23, s32[2,256,1]{1,2,0:T(1,128)} %param.12), kind=kLoop, calls=%fused_computation.212 | loop fusion | flops 512 | bytes 2564 | tf_op jit(solution)/shard_map/eq | solution.py:90
  1.4 0.7 copy.98
  2.1 0.2 convert_reduce_fusion
  2.4 0.2 select_reduce_fusion.1
  2.6 0.1 reshape.1598
  2.6 1.4 %gather_fusion.2 = s32[16]{0:T(128)S(1)} fusion(s32[2,256]{1,0:T(2,128)} %param.13, s32[16]{0:T(128)S(1)} %reshape.1598), kind=kCustom, calls=%fused_computation.4 | custom fusion | bytes 256 | tf_op jit(solution)/shard_map/jit(take_along_axis)/gather | solution.py:284
  4.0 0.1 reduce_sum.141
  4.1 0.2 iota_compare_fusion.1
  4.3 0.1 reduce_or.21
  4.4 0.1 fusion.58
  4.5 0.1 rem.185
  4.6 0.6 gather_fusion
  5.2 0.7 %select_reduce_fusion = f32[16,2,80]{2,1,0:T(2,128)S(1)} fusion(f32[16,2,80,128]{3,2,1,0:T(8,128)S(1)} %gather_fusion, pred[16]{0:T(512)(128)(4,1)S(1)} %get-tuple-element.53, pred[16,128]{1,0:T(8,128)(4,1)S(1)} %fusion.58), kind=kLoop, calls=%fused_computation.9 | loop fusion | flops 980480 | bytes 1323024 | tf_op jit(solution)/shard_map/reduce_sum | solution.py:291
  6.0 0.7 %reshape_reshape.6.picked_ref = f32[4,640]{1,0:T(4,128)} reshape(f32[16,2,80]{2,1,0:T(2,128)S(1)} %select_reduce_fusion) | data formatting | bytes 20480 | tf_op jit(solution)/shard_map/reshape;reshape | solution.py:259
  6.7 42.8 %shard_map.86 = f32[4,4,2,16,640]{4,3,2,1,0:T(8,128)} custom-call(f32[4,640]{1,0:T(4,128)} %reshape_reshape.6.picked_ref), custom_call_target="tpu_custom_call" | custom-call | tf_op jit(solution)/shard_map/pallas_call | solution.py:242
  49.6 3.5 %gather_fusion.1 = f32[512,640]{1,0:T(8,128)S(1)} fusion(f32[512,640]{1,0:T(8,128)} %bitcast.80, s32[1024]{0:T(1024)S(1)} %pad_clamp_fusion.2), kind=kCustom, calls=%fused_computation.3 | custom fusion | bytes 2623488 | tf_op jit(solution)/shard_map/jit(_take)/gather | solution.py:298
  53.1 0.2 broadcast_select_fusion
  53.3 0.7 %fusion.16 = f32[512,160]{1,0:T(8,128)S(1)} fusion(f32[512,640]{1,0:T(8,128)S(1)} %broadcast_select_fusion, pred[512]{0:T(512)(128)(4,1)S(1)} %get-tuple-element.38, pred[512]{0:T(512)(128)(4,1)S(1)} %get-tuple-element.37, pred[512]{0:T(512)(128)(4,1)S(1)} %get-tuple-element.12), kind=kLoop, calls=%fused_computation.24 | loop fusion | flops 245760 | bytes 1639936 | tf_op jit(solution)/shard_map/jit(_where)/select_n | solution.py:306
  54.0 0.6 fusion.75
  55.9 0.1 fusion.74
  56.1 0.1 copy.65
  56.3 0.1 copy.71
  56.5 0.1 copy-done
  56.7 0.6 fusion.20
  57.3 0.4 convolution_multiply_fusion
  57.7 0.4 fusion.72
  58.2 0.7 iota_compare_fusion.3
  58.8 0.8 %broadcast_select_fusion.1 = f32[2,256,160]{1,2,0:T(8,128)} fusion(f32[256,160]{0,1:T(8,128)S(1)} %bitcast.81, f32[256,160]{0,1:T(8,128)S(1)} %copy.65, pred[2]{0:T(512)(128)(4,1)S(1)} %iota_compare_fusion.3), kind=kLoop, calls=%fused_computation.50 | loop fusion | flops 81920 | bytes 655362 | tf_op jit(solution)/shard_map/jit(_where)/select_n | solution.py:317
  59.7 0.1 copy.66
  59.8 0.1 copy.67
  59.9 0.1 copy.68
  60.1 0.1 copy.69
  60.2 0.2 pad_maximum_fusion
  60.4 0.1 broadcast_compare_fusion
  60.5 0.2 fusion.31
  60.7 0.1 select_n.531
  60.8 0.6 gather_fusion.3
  61.4 0.1 broadcast_select_fusion.3
  61.5 0.2 fusion.57
  61.7 0.1 copy.73
  61.8 0.1 copy.72
  61.9 0.2 multiply_reduce_fusion
  62.1 0.2 multiply_add_fusion
  62.3 0.1 copy.74
  62.5 0.1 copy.75
  62.6 0.2 pad_maximum_fusion.1
  62.8 0.1 select_n.553
  62.9 0.6 gather_fusion.4
  63.6 0.2 fusion.55
  63.8 0.1 fusion.47
  63.9 0.2 fusion.54
  64.1 0.2 and_reduce_fusion
  64.3 0.1 select_n.555
  64.4 0.1 fusion.33
  64.5 0.2 fusion.56
  64.7 0.1 select_n.533
  64.7 0.1 fusion.32
  64.8 0.1 reshape.1562
  64.9 0.1 reduce_sum.149
  65.0 0.4 fusion.6
  65.5 0.8 %fusion.76 = (f32[2,15,128]{2,1,0:T(8,128)S(1)}, f32[2,15,80,128]{3,2,1,0:T(8,128)S(1)}) fusion(f32[2,15,80,128]{3,2,1,0:T(8,128)S(1)} %copy-done.1, f32[2,15,128,24]{2,3,1,0:T(8,128)S(1)} %fusion.6, f32[24,242]{1,0:T(8,128)S(1)} %broadcast_select_fusion.3), kind=kOutput, calls=%fused_computation.231 | convolution fusion | flops 44847360 | bytes 2853888 | tf_op jit(solution)/shard_map/blck,km->blmc/dot_general | solution.py:77
  66.3 0.1 reshape.1565
  66.4 0.5 fusion.9
  66.9 1.8 %fusion = f32[2,15,80,128]{3,2,1,0:T(8,128)} fusion(f32[2,15,80,128]{3,2,1,0:T(8,128)S(1)} %get-tuple-element.56, f32[2,15,128,24]{2,3,1,0:T(8,128)S(1)} %fusion.9, f32[24,242]{1,0:T(8,128)S(1)} %broadcast_select_fusion.2), kind=kOutput, calls=%fused_computation.6 | convolution fusion | flops 44544000 | bytes 2838528 | tf_op jit(solution)/shard_map/blck,km->blmc/dot_general | solution.py:77
  (57 shorter events, 0.7 us)
Async XLA Ops:
  0.6 4.0 %copy-start.1 = (f32[2,15,80,128]{3,2,1,0:T(8,128)S(1)}, f32[2,15,80,128]{3,2,1,0:T(8,128)}, u32[]{:S(2)}) copy-start(f32[2,15,80,128]{3,2,1,0:T(8,128)} %param.9) | copy-start | bytes 3686404
  5.2 44.3 %copy-start.2 = (s32[2,256,1]{1,2,0:T(1,128)S(1)}, s32[2,256,1]{1,2,0:T(1,128)}, u32[]{:S(2)}) copy-start(s32[2,256,1]{1,2,0:T(1,128)} %param.12) | copy-start | bytes 6148
  53.3 0.7 %copy-start.3 = (s32[2]{0:T(128)S(1)}, s32[2]{0:T(128)}, u32[]{:S(2)}) copy-start(s32[2]{0:T(128)} %param.15) | copy-start | bytes 28
  54.0 2.2 %copy-start.4 = (f32[2,256]{1,0:T(2,128)S(1)}, f32[2,256]{1,0:T(2,128)}, u32[]{:S(2)}) copy-start(f32[2,256]{1,0:T(2,128)} %param.10) | copy-start | bytes 6148
  54.0 2.2 %copy-start.5 = (f32[2,256]{1,0:T(2,128)S(1)}, f32[2,256]{1,0:T(2,128)}, u32[]{:S(2)}) copy-start(f32[2,256]{1,0:T(2,128)} %param.11) | copy-start | bytes 6148
  55.9 0.7 copy-start
  55.9 0.7 %copy-start.6 = (s32[2,256]{1,0:T(2,128)S(1)}, s32[2,256]{1,0:T(2,128)}, u32[]{:S(2)}) copy-start(s32[2,256]{1,0:T(2,128)} %param.14) | copy-start | bytes 6148

commit v12 on v9

--- a/solution.py
+++ b/solution.py
@@ -78,11 +78,9 @@
     return ensemble + change
 
 
-def pick(stacked, which):
-    out = stacked[0]
-    for i in range(1, stacked.shape[0]):
-        out = jnp.where(which == i, stacked[i], out)
-    return out
+def pick(stacked, chosen):
+    weights = chosen.astype(stacked.dtype).reshape((-1,) + (1,) * (stacked.ndim - 1))
+    return jnp.sum(stacked * weights, axis=0)
 
 
 def slot_table(owners, slot_rank, slab_number, capacity):
@@ -308,15 +306,17 @@
         flat_priors = jnp.where(part == r, lines[:, r * width : (r + 1) * width], flat_priors)
     priors = flat_priors.reshape(BATCHES, -1, width)
 
-    first, second = batch_order[0], batch_order[1]
+    turns = batch_order[:, None] == jnp.arange(BATCHES, dtype=jnp.int32)[None, :]
+    first, second = turns[0], turns[1]
     y0 = pick(priors, first)
     home0 = pick(obs_home, first)
     home1 = pick(obs_home, second)
     stats0 = obs_statistics(y0, pick(obs_value, first), pick(obs_var, first), members)
     y1 = update_pool(pick(priors, second), home1, *stats0, home0, nblocks, decays)
     stats1 = obs_statistics(y1, pick(obs_value, second), pick(obs_var, second), members)
-    which = jnp.arange(BATCHES, dtype=jnp.int32)[:, None, None]
-    recorded = jnp.where(which == first, y0[None], y1[None])
+    recorded = jnp.sum(
+        jnp.stack([y0, y1])[:, None] * turns.astype(jnp.float32)[:, :, None, None], axis=0
+    )
 
     col_blocks = ((slab_index * sub_count + sub_index) * cols_dev + jnp.arange(
         cols_dev, dtype=jnp.int32
@@ -348,7 +348,7 @@
             rows[:, width + members],
             rows[:, width : width + members],
             rows[:, width + members + 1].astype(jnp.int32),
-            pick(near_valid, batch_id),
+            pick(near_valid.astype(jnp.int32), batch_id) > 0,
             nblocks,
             decays,
         )

time: 68.3 us -> 67.2 us (0.984)
  between operations: 2.5 us -> 1.2 us
    select_n x5 -> x0, other arithmetic: 1.54 us -> none  [the longest x1 0.82 us: per_device(): recorded = jnp.where(which == first, y0[None], y1[None])]
    reduce_sum x0 -> x5, other arithmetic: none -> 1.27 us  [the longest x1 0.85 us: per_device(): jnp.sum(jnp.stack([y0, y1])[:, None] * turns.astype(jnp.float32)[:, :, No...]
    reduce_sum x1 -> x2, other arithmetic: 0.12 us -> 0.9 us  [obs_statistics(): centre = jnp.mean(whole_obs, axis=1, keepdims=True)]
where the time goes in v12:
time: 67.2 us; the launch traced here: 66.9 us
  Pallas kernels  42.8 us (64%)
  local copies, waits for them, and re-layouts  10.6 us (16%)
  other arithmetic  7.99 us (12%)
  matrix products  4.39 us (7%)
  between operations  1.2 us (2%)
    pallas_call x1, Pallas kernels, gather_slots(): pl.pallas_call(functools.partial(gather_kernel, n_row), out_shape=jax.Sha...  42.8 us
    gather x1, local copies, waits for them, and re-layouts, per_device(): jnp.take(gathered.reshape(sub_count * slab_count, q_rows * width), (row_o...  3.52 us
    dot_general x2, matrix products, update_state(): jnp.einsum('blck,km->blmc', crossed * weights[:, None], increments, preci...  2.65 us

profile of v12, /device:TPU:1, one launch (start us, length us, event | category | flops | bytes accessed | tf_op | source)
XLA Modules:
  0.0 66.9 jit_solution(5532228144667708626)
XLA Ops:
  0.6 0.9 %copy.77 = s32[2,2,128]{1,2,0:T(8,128)S(1)} copy(s32[2,2,128]{2,1,0:T(2,128)} %bitcast.107) | data formatting | bytes 4096 | tf_op jit(solution)/shard_map/eq | solution.py:278
  1.5 0.4 fusion.26
  2.0 0.1 add_add_fusion
  2.2 0.2 fusion.27
  2.5 0.1 select_reduce_fusion.1
  2.6 0.1 reshape.1575
  2.7 0.7 %gather_fusion.2 = s32[16]{0:T(128)S(1)} fusion(s32[2,256]{1,0:T(2,128)S(1)} %copy-done, s32[16]{0:T(128)S(1)} %reshape.1575), kind=kCustom, calls=%fused_computation.4 | custom fusion | bytes 256 | tf_op jit(solution)/shard_map/jit(take_along_axis)/gather | solution.py:284
  3.4 0.1 reduce_sum.269
  3.5 0.2 iota_compare_fusion.1
  3.6 0.1 reduce_or.21
  3.9 0.1 rem.185
  4.0 0.6 gather_fusion
  4.6 0.7 %select_reduce_fusion = f32[16,2,80]{2,1,0:T(2,128)S(1)} fusion(f32[16,2,80,128]{3,2,1,0:T(8,128)S(1)} %gather_fusion, pred[16]{0:T(512)(128)(4,1)S(1)} %get-tuple-element.61, pred[16,128]{1,0:T(8,128)(4,1)S(1)} %fusion.62), kind=kLoop, calls=%fused_computation.9 | loop fusion | flops 980480 | bytes 1323024 | tf_op jit(solution)/shard_map/reduce_sum | solution.py:291
  5.3 0.7 %reshape_reshape.6.picked_ref = f32[4,640]{1,0:T(4,128)} reshape(f32[16,2,80]{2,1,0:T(2,128)S(1)} %select_reduce_fusion) | data formatting | bytes 20480 | tf_op jit(solution)/shard_map/reshape;reshape | solution.py:257
  6.0 42.8 %shard_map.86 = f32[4,4,2,16,640]{4,3,2,1,0:T(8,128)} custom-call(f32[4,640]{1,0:T(4,128)} %reshape_reshape.6.picked_ref), custom_call_target="tpu_custom_call" | custom-call | tf_op jit(solution)/shard_map/pallas_call | solution.py:240
  48.9 3.5 %gather_fusion.1 = f32[512,640]{1,0:T(8,128)S(1)} fusion(f32[512,640]{1,0:T(8,128)} %bitcast.92, s32[1024]{0:T(1024)S(1)} %pad_clamp_fusion.2), kind=kCustom, calls=%fused_computation.3 | custom fusion | bytes 2623488 | tf_op jit(solution)/shard_map/jit(_take)/gather | solution.py:298
  52.5 0.2 broadcast_select_fusion
  52.7 0.5 copy-done.6
  53.2 0.1 multiply_reduce_fusion.9
  53.4 0.9 %multiply_reduce_fusion.2 = (f32[512]{0:T(512)S(1)}, f32[512,160]{1,0:T(8,128)S(1)}) fusion(f32[512]{0:T(512)S(1)} %bitcast.115, f32[512,640]{1,0:T(8,128)S(1)} %broadcast_select_fusion, pred[512]{0:T(512)(128)(4,1)S(1)} %get-tuple-element.41, pred[512]{0:T(512)(128)(4,1)S(1)} %get-tuple-element.40, pred[512]{0:T(512)(128)(4,1)S(1)} %get-tuple-element.30), kind=kLoop, calls=%fused_computation.29 | loop fusion | flops 409088 | bytes 1644032 | tf_op jit(solution)/shard_map/reduce_sum | solution.py:46
  54.3 0.2 multiply_reduce_fusion.1
  54.4 0.1 copy.80
  54.7 0.1 copy.88
  54.9 0.1 multiply_reduce_fusion.10
  55.0 0.6 fusion.20
  55.7 0.4 convolution_multiply_fusion
  56.1 0.4 fusion.79
  56.5 0.1 copy.95
  56.7 0.2 copy.96
  56.9 0.8 %multiply_reduce_fusion = f32[2,256,160]{1,2,0:T(8,128)} fusion(f32[2,2]{1,0:T(2,128)S(1)} %get-tuple-element.52, f32[2,256,160]{1,2,0:T(8,128)S(1)} %copy.96), kind=kLoop, calls=%fused_computation.19 | loop fusion | flops 245760 | bytes 655376 | tf_op jit(solution)/shard_map/reduce_sum | solution.py:317
  57.7 0.1 copy.81
  57.9 0.1 copy.82
  58.0 0.1 copy.83
  58.2 0.1 copy.84
  58.3 0.2 pad_maximum_fusion.1
  58.6 0.2 fusion.35
  58.8 0.2 and_reduce_fusion
  59.0 0.1 select_reduce_fusion.2
  59.1 0.1 reduce_sum.284
  59.2 0.6 gather_fusion.3
  59.8 0.2 fusion.61
  60.1 0.1 copy.90
  60.2 0.1 copy.89
  60.3 0.2 multiply_reduce_fusion.4
  60.5 0.2 multiply_add_fusion
  60.7 0.1 copy.91
  60.9 0.1 copy.92
  61.0 0.2 pad_maximum_fusion.2
  61.2 0.1 reduce_sum.297
  61.3 0.6 gather_fusion.4
  62.0 0.2 fusion.59
  62.2 0.1 fusion.51
  62.3 0.2 fusion.58
  62.5 0.1 gt.23
  62.6 0.1 fusion.37
  62.7 0.2 fusion.60
  62.8 0.1 gt.21
  63.0 0.1 reshape.1535
  63.1 0.1 reduce_sum.285
  63.2 0.4 fusion.6
  63.7 0.8 %fusion.82 = (f32[2,15,128]{2,1,0:T(8,128)S(1)}, f32[2,15,80,128]{3,2,1,0:T(8,128)S(1)}) fusion(f32[2,15,80,128]{3,2,1,0:T(8,128)S(1)} %copy-done.1, f32[2,15,128,24]{2,3,1,0:T(8,128)S(1)} %fusion.6, f32[24,242]{1,0:T(8,128)S(1)} %broadcast_select_fusion.2), kind=kOutput, calls=%fused_computation.244 | convolution fusion | flops 44847360 | bytes 2853888 | tf_op jit(solution)/shard_map/blck,km->blmc/dot_general | solution.py:77
  64.5 0.1 reshape.1538
  64.6 0.5 fusion.9
  65.1 1.8 %fusion = f32[2,15,80,128]{3,2,1,0:T(8,128)} fusion(f32[2,15,80,128]{3,2,1,0:T(8,128)S(1)} %get-tuple-element.64, f32[2,15,128,24]{2,3,1,0:T(8,128)S(1)} %fusion.9, f32[24,242]{1,0:T(8,128)S(1)} %broadcast_select_fusion.1), kind=kOutput, calls=%fused_computation.6 | convolution fusion | flops 44544000 | bytes 2838528 | tf_op jit(solution)/shard_map/blck,km->blmc/dot_general | solution.py:77
  (72 shorter events, 1.3 us)
Async XLA Ops:
  0.6 1.6 %copy-start.2 = (s32[2,256,1]{1,2,0:T(1,128)S(1)}, s32[2,256,1]{1,2,0:T(1,128)}, u32[]{:S(2)}) copy-start(s32[2,256,1]{1,2,0:T(1,128)} %param.12) | copy-start | bytes 6148
  0.6 2.1 %copy-start = (s32[2,256]{1,0:T(2,128)S(1)}, s32[2,256]{1,0:T(2,128)}, u32[]{:S(2)}) copy-start(s32[2,256]{1,0:T(2,128)} %param.13) | copy-start | bytes 6148
  2.0 2.0 %copy-start.1 = (f32[2,15,80,128]{3,2,1,0:T(8,128)S(1)}, f32[2,15,80,128]{3,2,1,0:T(8,128)}, u32[]{:S(2)}) copy-start(f32[2,15,80,128]{3,2,1,0:T(8,128)} %param.9) | copy-start | bytes 3686404
  52.5 0.7 copy-start.6
  52.5 0.7 %copy-start.3 = (f32[2,256]{1,0:T(2,128)S(1)}, f32[2,256]{1,0:T(2,128)}, u32[]{:S(2)}) copy-start(f32[2,256]{1,0:T(2,128)} %param.11) | copy-start | bytes 6148
  52.5 0.7 %copy-start.4 = (f32[2,256]{1,0:T(2,128)S(1)}, f32[2,256]{1,0:T(2,128)}, u32[]{:S(2)}) copy-start(f32[2,256]{1,0:T(2,128)} %param.10) | copy-start | bytes 6148
  54.2 0.7 %copy-start.5 = (s32[2,256]{1,0:T(2,128)S(1)}, s32[2,256]{1,0:T(2,128)}, u32[]{:S(2)}) copy-start(s32[2,256]{1,0:T(2,128)} %param.14) | copy-start | bytes 6148

commit v13 on v12

--- a/solution.py
+++ b/solution.py
@@ -83,7 +83,7 @@
     return jnp.sum(stacked * weights, axis=0)
 
 
-def slot_table(owners, slot_rank, slab_number, capacity):
+def slot_table(owners, slot_rank, slab_number, capacity, columns):
     obs_count = owners.shape[1]
     matches = (owners == slab_number)[:, None, :] & (
         slot_rank[:, None, :] == jnp.arange(capacity, dtype=jnp.int32)[None, :, None]
@@ -92,7 +92,8 @@
         jnp.where(matches, jnp.arange(obs_count, dtype=jnp.int32)[None, None, :], 0), axis=2
     )
     slot_valid = jnp.any(matches, axis=2)
-    return (slot_obs, slot_valid)
+    slot_column = jnp.sum(jnp.where(matches, columns[:, None, :], 0), axis=2)
+    return (slot_obs, slot_valid, slot_column)
 
 
 def gather_kernel(n_row, picked_ref, out_ref, part_ref, sem0, send0, sem_a, send_a, sem_b, send_b, sem_c, send_c):
@@ -275,13 +276,10 @@
     assert 2 * span_broad + 1 <= cols_slab // BLK and slab_count >= 3
     owners = obs_owner[:, :, 0]
     obs_home = jnp.mod((owners * cols_slab + obs_column) // BLK + home_block, nblocks)
-    onehot = (owners[:, :, None] == jnp.arange(slab_count, dtype=jnp.int32)[None, None, :]).astype(
-        jnp.int32
-    )
-    running = jnp.cumsum(onehot, axis=1) - 1
-    slot_rank = jnp.sum(onehot * running, axis=2)
-    slot_obs, slot_valid = slot_table(owners, slot_rank, slab_index, capacity)
-    slot_column = jnp.take_along_axis(obs_column, slot_obs, axis=1)
+    order = jnp.arange(owners.shape[1], dtype=jnp.int32)
+    earlier = (owners[:, None, :] == owners[:, :, None]) & (order[None, :] < order[:, None])[None]
+    slot_rank = jnp.sum(earlier.astype(jnp.int32), axis=2)
+    slot_obs, slot_valid, slot_column = slot_table(owners, slot_rank, slab_index, capacity, obs_column)
     slot_level = slot_obs % levels_count
     holder = slot_column // cols_dev
     local_col = slot_column % cols_dev

time: 67.2 us -> 68.3 us (1.016)
  other arithmetic: 7.99 us -> 8.78 us
    gather x1, local copies, waits for them, and re-layouts: 0.63 us -> 1.92 us  [per_device(): levels = jnp.take(ensemble, slot_level.reshape(-1), axis=1)]
    eq x1 -> x0, local copies, waits for them, and re-layouts: 0.86 us -> none  [per_device(): owners[:, :, None] == jnp.arange(slab_count, dtype=jnp.int32)[None, None, :]]
    gather x2 -> x0, local copies, waits for them, and re-layouts: 0.78 us -> none  [per_device(): slot_column = jnp.take_along_axis(obs_column, slot_obs, axis=1)]
    reduce_sum x2, other arithmetic: 0.39 us -> 1.08 us  [the longest x1 0.83 us: slot_table(): slot_column = jnp.sum(jnp.where(matches, columns[:, None, :], 0), axis=2)]
    unnamed x18, local copies, waits for them, and re-layouts: 0.58 us -> 1.26 us
    eq x1, other arithmetic: 0.01 us -> 0.69 us  [slot_table(): owners == slab_number]
where the time goes in v13:
time: 68.3 us; the launch traced here: 68 us
  Pallas kernels  42.8 us (63%)
  local copies, waits for them, and re-layouts  10.9 us (16%)
  other arithmetic  8.78 us (13%)
  matrix products  4.35 us (6%)
  between operations  1.15 us (2%)
    pallas_call x1, Pallas kernels, gather_slots(): pl.pallas_call(functools.partial(gather_kernel, n_row), out_shape=jax.Sha...  42.8 us
    gather x1, local copies, waits for them, and re-layouts, per_device(): jnp.take(gathered.reshape(sub_count * slab_count, q_rows * width), (row_o...  3.52 us
    dot_general x2, matrix products, update_state(): jnp.einsum('blck,km->blmc', crossed * weights[:, None], increments, preci...  2.6 us
    gather x1, local copies, waits for them, and re-layouts, per_device(): levels = jnp.take(ensemble, slot_level.reshape(-1), axis=1)  1.92 us

profile of v13, /device:TPU:1, one launch (start us, length us, event | category | flops | bytes accessed | tf_op | source)
XLA Modules:
  0.0 68.0 jit_solution(4682578940561339442)
XLA Ops:
  0.6 0.7 %broadcast_compare_fusion.3 = pred[2,256]{1,0:T(4,128)(4,1)S(1)} fusion(s32[]{:T(128)S(6)} %axis_index.23, s32[2,256,1]{1,2,0:T(1,128)} %param.12), kind=kLoop, calls=%fused_computation.211 | loop fusion | flops 512 | bytes 2564 | tf_op jit(solution)/shard_map/eq | solution.py:88
  1.3 0.7 %copy.111 = s32[2,256,1]{1,0,2:T(2,128)S(1)} copy(s32[2,256,1]{1,2,0:T(1,128)} %param.12) | data formatting | bytes 4096
  2.0 0.2 convert_reduce_fusion
  2.3 0.8 %select_reduce_fusion.2 = (s32[2,8]{1,0:T(2,128)S(1)}, s32[2,8]{1,0:T(2,128)S(1)}) fusion(s32[2,256]{1,0:T(2,128)} %param.13, s32[2,256]{1,0:T(2,128)S(1)} %convert_reduce_fusion, pred[2,256]{1,0:T(4,128)(4,1)S(1)} %broadcast_compare_fusion.3), kind=kLoop, calls=%fused_computation.82 | loop fusion | flops 24544 | bytes 4736 | tf_op jit(solution)/shard_map/reduce_sum | solution.py:95
  3.1 0.1 reduce_sum.276
  3.2 0.2 iota_compare_fusion.1
  3.4 0.1 reduce_or.21
  3.5 0.1 fusion.58
  3.6 0.1 rem.186
  3.7 1.9 %gather_fusion = f32[16,2,80,128]{3,2,1,0:T(8,128)S(1)} fusion(f32[2,15,80,128]{3,2,1,0:T(8,128)} %param.9, s32[1024]{0:T(1024)S(1)} %pad_clamp_fusion.3), kind=kCustom, calls=%fused_computation.2 | custom fusion | bytes 2621504 | tf_op jit(solution)/shard_map/jit(_take)/gather | solution.py:286
  5.6 0.1 rem.184
  5.7 0.7 %select_reduce_fusion = f32[16,2,80]{2,1,0:T(2,128)S(1)} fusion(f32[16,2,80,128]{3,2,1,0:T(8,128)S(1)} %gather_fusion, pred[16]{0:T(512)(128)(4,1)S(1)} %compare_and_fusion.2, pred[16,128]{1,0:T(8,128)(4,1)S(1)} %fusion.58), kind=kLoop, calls=%fused_computation.8 | loop fusion | flops 980480 | bytes 1323024 | tf_op jit(solution)/shard_map/reduce_sum | solution.py:289
  6.4 0.7 %reshape_reshape.6.picked_ref = f32[4,640]{1,0:T(4,128)} reshape(f32[16,2,80]{2,1,0:T(2,128)S(1)} %select_reduce_fusion) | data formatting | bytes 20480 | tf_op jit(solution)/shard_map/reshape;reshape | solution.py:258
  7.1 42.8 %shard_map.86 = f32[4,4,2,16,640]{4,3,2,1,0:T(8,128)} custom-call(f32[4,640]{1,0:T(4,128)} %reshape_reshape.6.picked_ref), custom_call_target="tpu_custom_call" | custom-call | tf_op jit(solution)/shard_map/pallas_call | solution.py:241
  50.0 3.5 %gather_fusion.1 = f32[512,640]{1,0:T(8,128)S(1)} fusion(f32[512,640]{1,0:T(8,128)} %bitcast.79, s32[1024]{0:T(1024)S(1)} %pad_clamp_fusion.2), kind=kCustom, calls=%fused_computation.3 | custom fusion | bytes 2623488 | tf_op jit(solution)/shard_map/jit(_take)/gather | solution.py:296
  53.6 0.2 broadcast_select_fusion
  53.8 0.5 copy-done.6
  54.3 0.1 multiply_reduce_fusion.9
  54.4 0.9 %multiply_reduce_fusion.2 = (f32[512]{0:T(512)S(1)}, f32[512,160]{1,0:T(8,128)S(1)}) fusion(f32[512]{0:T(512)S(1)} %bitcast.101, f32[512,640]{1,0:T(8,128)S(1)} %broadcast_select_fusion, pred[512]{0:T(512)(128)(4,1)S(1)} %get-tuple-element.41, pred[512]{0:T(512)(128)(4,1)S(1)} %get-tuple-element.40, pred[512]{0:T(512)(128)(4,1)S(1)} %get-tuple-element.32), kind=kLoop, calls=%fused_computation.28 | loop fusion | flops 409088 | bytes 1644032 | tf_op jit(solution)/shard_map/reduce_sum | solution.py:46
  55.3 0.2 multiply_reduce_fusion.1
  55.5 0.1 copy.69
  55.8 0.1 copy.77
  56.0 0.1 multiply_reduce_fusion.10
  56.1 0.6 fusion.20
  56.8 0.4 convolution_multiply_fusion
  57.2 0.4 fusion.72
  57.6 0.1 copy.84
  57.8 0.2 copy.85
  58.0 0.8 %multiply_reduce_fusion = f32[2,256,160]{1,2,0:T(8,128)} fusion(f32[2,2]{1,0:T(2,128)S(1)} %get-tuple-element.52, f32[2,256,160]{1,2,0:T(8,128)S(1)} %copy.85), kind=kLoop, calls=%fused_computation.18 | loop fusion | flops 245760 | bytes 655376 | tf_op jit(solution)/shard_map/reduce_sum | solution.py:315
  58.8 0.1 copy.70
  59.0 0.1 copy.71
  59.1 0.1 copy.72
  59.3 0.1 copy.73
  59.4 0.2 pad_maximum_fusion.1
  59.7 0.2 fusion.31
  59.9 0.2 and_reduce_fusion
  60.1 0.1 select_reduce_fusion.3
  60.2 0.1 reduce_sum.291
  60.3 0.6 gather_fusion.2
  60.9 0.2 fusion.57
  61.2 0.1 copy.79
  61.3 0.1 copy.78
  61.4 0.2 multiply_reduce_fusion.4
  61.6 0.2 multiply_add_fusion
  61.8 0.1 copy.80
  62.0 0.1 copy.81
  62.1 0.2 pad_maximum_fusion.2
  62.3 0.1 reduce_sum.304
  62.4 0.6 gather_fusion.3
  63.1 0.2 fusion.55
  63.3 0.1 fusion.47
  63.4 0.2 fusion.54
  63.6 0.1 gt.23
  63.7 0.1 fusion.33
  63.8 0.2 fusion.56
  64.0 0.1 gt.21
  64.0 0.1 fusion.32
  64.1 0.1 reshape.1509
  64.2 0.1 reduce_sum.292
  64.3 0.4 fusion.6
  64.8 0.8 %fusion.75 = (f32[2,15,128]{2,1,0:T(8,128)S(1)}, f32[2,15,80,128]{3,2,1,0:T(8,128)S(1)}) fusion(f32[2,15,80,128]{3,2,1,0:T(8,128)S(1)} %copy-done, f32[2,15,128,24]{2,3,1,0:T(8,128)S(1)} %fusion.6, f32[24,242]{1,0:T(8,128)S(1)} %broadcast_select_fusion.2), kind=kOutput, calls=%fused_computation.231 | convolution fusion | flops 44847360 | bytes 2853888 | tf_op jit(solution)/shard_map/blck,km->blmc/dot_general | solution.py:77
  65.6 0.1 reshape.1512
  65.7 0.4 fusion.9
  66.2 1.8 %fusion = f32[2,15,80,128]{3,2,1,0:T(8,128)} fusion(f32[2,15,80,128]{3,2,1,0:T(8,128)S(1)} %get-tuple-element.63, f32[2,15,128,24]{2,3,1,0:T(8,128)S(1)} %fusion.9, f32[24,242]{1,0:T(8,128)S(1)} %broadcast_select_fusion.1), kind=kOutput, calls=%fused_computation.5 | convolution fusion | flops 44544000 | bytes 2838528 | tf_op jit(solution)/shard_map/blck,km->blmc/dot_general | solution.py:77
  (65 shorter events, 1.0 us)
Async XLA Ops:
  5.7 44.3 %copy-start.1 = (s32[2,256,1]{1,2,0:T(1,128)S(1)}, s32[2,256,1]{1,2,0:T(1,128)}, u32[]{:S(2)}) copy-start(s32[2,256,1]{1,2,0:T(1,128)} %param.12) | copy-start | bytes 6148
  53.6 0.7 copy-start.6
  53.6 0.7 %copy-start.3 = (f32[2,256]{1,0:T(2,128)S(1)}, f32[2,256]{1,0:T(2,128)}, u32[]{:S(2)}) copy-start(f32[2,256]{1,0:T(2,128)} %param.11) | copy-start | bytes 6148
  53.6 0.7 %copy-start.4 = (f32[2,256]{1,0:T(2,128)S(1)}, f32[2,256]{1,0:T(2,128)}, u32[]{:S(2)}) copy-start(f32[2,256]{1,0:T(2,128)} %param.10) | copy-start | bytes 6148
  55.3 0.7 %copy-start.2 = (s32[2,256]{1,0:T(2,128)S(1)}, s32[2,256]{1,0:T(2,128)}, u32[]{:S(2)}) copy-start(s32[2,256]{1,0:T(2,128)} %param.13) | copy-start | bytes 6148
  55.3 0.7 %copy-start.5 = (s32[2,256]{1,0:T(2,128)S(1)}, s32[2,256]{1,0:T(2,128)}, u32[]{:S(2)}) copy-start(s32[2,256]{1,0:T(2,128)} %param.14) | copy-start | bytes 6148
  61.2 3.1 %copy-start = (f32[2,15,80,128]{3,2,1,0:T(8,128)S(1)}, f32[2,15,80,128]{3,2,1,0:T(8,128)}, u32[]{:S(2)}) copy-start(f32[2,15,80,128]{3,2,1,0:T(8,128)} %param.9) | copy-start | bytes 3686404

commit v14 on v13

--- a/solution.py
+++ b/solution.py
@@ -276,9 +276,11 @@
     assert 2 * span_broad + 1 <= cols_slab // BLK and slab_count >= 3
     owners = obs_owner[:, :, 0]
     obs_home = jnp.mod((owners * cols_slab + obs_column) // BLK + home_block, nblocks)
-    order = jnp.arange(owners.shape[1], dtype=jnp.int32)
-    earlier = (owners[:, None, :] == owners[:, :, None]) & (order[None, :] < order[:, None])[None]
-    slot_rank = jnp.sum(earlier.astype(jnp.int32), axis=2)
+    onehot = (owners[:, :, None] == jnp.arange(slab_count, dtype=jnp.int32)[None, None, :]).astype(
+        jnp.int32
+    )
+    running = jnp.cumsum(onehot, axis=1) - 1
+    slot_rank = jnp.sum(onehot * running, axis=2)
     slot_obs, slot_valid, slot_column = slot_table(owners, slot_rank, slab_index, capacity, obs_column)
     slot_level = slot_obs % levels_count
     holder = slot_column // cols_dev

time: 68.3 us -> 66.4 us (0.972)
  local copies, waits for them, and re-layouts: 10.9 us -> 9.9 us
  other arithmetic: 8.78 us -> 7.98 us
    gather x1, local copies, waits for them, and re-layouts: 1.92 us -> 0.63 us  [per_device(): levels = jnp.take(ensemble, slot_level.reshape(-1), axis=1)]
    eq x0 -> x1, local copies, waits for them, and re-layouts: none -> 0.91 us  [per_device(): owners[:, :, None] == jnp.arange(slab_count, dtype=jnp.int32)[None, None, :]]
    reduce_sum x1, other arithmetic: 0.83 us -> 0.15 us  [slot_table(): slot_column = jnp.sum(jnp.where(matches, columns[:, None, :], 0), axis=2)]
    unnamed x18, local copies, waits for them, and re-layouts: 1.26 us -> 0.57 us
    eq x1, other arithmetic: 0.69 us -> 0.01 us  [slot_table(): owners == slab_number]
where the time goes in v14:
time: 66.4 us; the launch traced here: 66.2 us
  Pallas kernels  42.8 us (64%)
  local copies, waits for them, and re-layouts  9.9 us (15%)
  other arithmetic  7.98 us (12%)
  matrix products  4.34 us (7%)
  between operations  1.21 us (2%)
    pallas_call x1, Pallas kernels, gather_slots(): pl.pallas_call(functools.partial(gather_kernel, n_row), out_shape=jax.Sha...  42.8 us
    gather x1, local copies, waits for them, and re-layouts, per_device(): jnp.take(gathered.reshape(sub_count * slab_count, q_rows * width), (row_o...  3.52 us
    dot_general x2, matrix products, update_state(): jnp.einsum('blck,km->blmc', crossed * weights[:, None], increments, preci...  2.6 us

profile of v14, /device:TPU:1, one launch (start us, length us, event | category | flops | bytes accessed | tf_op | source)
XLA Modules:
  0.0 66.2 jit_solution(16598026841373814399)
XLA Ops:
  0.7 0.9 %copy.77 = s32[2,2,128]{1,2,0:T(8,128)S(1)} copy(s32[2,2,128]{2,1,0:T(2,128)} %bitcast.103) | data formatting | bytes 4096 | tf_op jit(solution)/shard_map/eq | solution.py:279
  1.6 0.4 fusion.26
  2.1 0.1 add_add_fusion
  2.3 0.2 fusion.27
  2.5 0.1 select_reduce_fusion.2
  2.7 0.1 reduce_sum.276
  2.8 0.2 iota_compare_fusion.1
  2.9 0.1 reduce_or.21
  3.1 0.1 rem.186
  3.2 0.6 gather_fusion
  3.9 0.1 rem.184
  4.0 0.7 %select_reduce_fusion = f32[16,2,80]{2,1,0:T(2,128)S(1)} fusion(f32[16,2,80,128]{3,2,1,0:T(8,128)S(1)} %gather_fusion, pred[16]{0:T(512)(128)(4,1)S(1)} %compare_and_fusion.2, pred[16,128]{1,0:T(8,128)(4,1)S(1)} %fusion.62), kind=kLoop, calls=%fused_computation.8 | loop fusion | flops 980480 | bytes 1323024 | tf_op jit(solution)/shard_map/reduce_sum | solution.py:291
  4.7 0.7 %reshape_reshape.6.picked_ref = f32[4,640]{1,0:T(4,128)} reshape(f32[16,2,80]{2,1,0:T(2,128)S(1)} %select_reduce_fusion) | data formatting | bytes 20480 | tf_op jit(solution)/shard_map/reshape;reshape | solution.py:258
  5.4 42.8 %shard_map.86 = f32[4,4,2,16,640]{4,3,2,1,0:T(8,128)} custom-call(f32[4,640]{1,0:T(4,128)} %reshape_reshape.6.picked_ref), custom_call_target="tpu_custom_call" | custom-call | tf_op jit(solution)/shard_map/pallas_call | solution.py:241
  48.3 3.5 %gather_fusion.1 = f32[512,640]{1,0:T(8,128)S(1)} fusion(f32[512,640]{1,0:T(8,128)} %bitcast.88, s32[1024]{0:T(1024)S(1)} %pad_clamp_fusion.2), kind=kCustom, calls=%fused_computation.3 | custom fusion | bytes 2623488 | tf_op jit(solution)/shard_map/jit(_take)/gather | solution.py:298
  51.9 0.2 broadcast_select_fusion
  52.0 0.5 copy-done.6
  52.6 0.1 multiply_reduce_fusion.9
  52.7 0.9 %multiply_reduce_fusion.2 = (f32[512]{0:T(512)S(1)}, f32[512,160]{1,0:T(8,128)S(1)}) fusion(f32[512]{0:T(512)S(1)} %bitcast.111, f32[512,640]{1,0:T(8,128)S(1)} %broadcast_select_fusion, pred[512]{0:T(512)(128)(4,1)S(1)} %get-tuple-element.41, pred[512]{0:T(512)(128)(4,1)S(1)} %get-tuple-element.40, pred[512]{0:T(512)(128)(4,1)S(1)} %get-tuple-element.32), kind=kLoop, calls=%fused_computation.28 | loop fusion | flops 409088 | bytes 1644032 | tf_op jit(solution)/shard_map/reduce_sum | solution.py:46
  53.6 0.2 multiply_reduce_fusion.1
  53.8 0.1 copy.80
  54.0 0.1 copy.88
  54.3 0.1 multiply_reduce_fusion.10
  54.4 0.6 fusion.20
  55.0 0.4 convolution_multiply_fusion
  55.5 0.4 fusion.76
  55.9 0.1 copy.95
  56.1 0.2 copy.96
  56.2 0.8 %multiply_reduce_fusion = f32[2,256,160]{1,2,0:T(8,128)} fusion(f32[2,2]{1,0:T(2,128)S(1)} %get-tuple-element.52, f32[2,256,160]{1,2,0:T(8,128)S(1)} %copy.96), kind=kLoop, calls=%fused_computation.18 | loop fusion | flops 245760 | bytes 655376 | tf_op jit(solution)/shard_map/reduce_sum | solution.py:317
  57.1 0.1 copy.81
  57.3 0.1 copy.82
  57.4 0.1 copy.83
  57.5 0.1 copy.84
  57.7 0.2 pad_maximum_fusion.1
  57.9 0.2 fusion.35
  58.1 0.2 and_reduce_fusion
  58.3 0.1 select_reduce_fusion.3
  58.4 0.1 reduce_sum.291
  58.5 0.6 gather_fusion.2
  59.2 0.2 fusion.61
  59.4 0.1 copy.90
  59.5 0.1 copy.89
  59.6 0.2 multiply_reduce_fusion.4
  59.9 0.2 multiply_add_fusion
  60.1 0.1 copy.91
  60.2 0.1 copy.92
  60.4 0.2 pad_maximum_fusion.2
  60.5 0.1 reduce_sum.304
  60.6 0.6 gather_fusion.3
  61.3 0.2 fusion.59
  61.5 0.1 fusion.51
  61.7 0.2 fusion.58
  61.8 0.1 gt.23
  61.9 0.1 fusion.37
  62.0 0.2 fusion.60
  62.2 0.1 gt.21
  62.3 0.1 fusion.36
  62.4 0.1 reshape.1510
  62.5 0.1 reduce_sum.292
  62.6 0.4 fusion.6
  63.0 0.8 %fusion.79 = (f32[2,15,128]{2,1,0:T(8,128)S(1)}, f32[2,15,80,128]{3,2,1,0:T(8,128)S(1)}) fusion(f32[2,15,80,128]{3,2,1,0:T(8,128)S(1)} %copy-done, f32[2,15,128,24]{2,3,1,0:T(8,128)S(1)} %fusion.6, f32[24,242]{1,0:T(8,128)S(1)} %broadcast_select_fusion.2), kind=kOutput, calls=%fused_computation.238 | convolution fusion | flops 44847360 | bytes 2853888 | tf_op jit(solution)/shard_map/blck,km->blmc/dot_general | solution.py:77
  63.8 0.1 reshape.1513
  63.9 0.4 fusion.9
  64.4 1.8 %fusion = f32[2,15,80,128]{3,2,1,0:T(8,128)} fusion(f32[2,15,80,128]{3,2,1,0:T(8,128)S(1)} %get-tuple-element.63, f32[2,15,128,24]{2,3,1,0:T(8,128)S(1)} %fusion.9, f32[24,242]{1,0:T(8,128)S(1)} %broadcast_select_fusion.1), kind=kOutput, calls=%fused_computation.5 | convolution fusion | flops 44544000 | bytes 2838528 | tf_op jit(solution)/shard_map/blck,km->blmc/dot_general | solution.py:77
  (71 shorter events, 1.2 us)
Async XLA Ops:
  0.6 1.6 %copy-start.1 = (s32[2,256,1]{1,2,0:T(1,128)S(1)}, s32[2,256,1]{1,2,0:T(1,128)}, u32[]{:S(2)}) copy-start(s32[2,256,1]{1,2,0:T(1,128)} %param.12) | copy-start | bytes 6148
  0.6 1.9 %copy-start.2 = (s32[2,256]{1,0:T(2,128)S(1)}, s32[2,256]{1,0:T(2,128)}, u32[]{:S(2)}) copy-start(s32[2,256]{1,0:T(2,128)} %param.13) | copy-start | bytes 6148
  0.6 2.6 %copy-start = (f32[2,15,80,128]{3,2,1,0:T(8,128)S(1)}, f32[2,15,80,128]{3,2,1,0:T(8,128)}, u32[]{:S(2)}) copy-start(f32[2,15,80,128]{3,2,1,0:T(8,128)} %param.9) | copy-start | bytes 3686404
  51.8 0.7 copy-start.6
  51.9 0.7 %copy-start.3 = (f32[2,256]{1,0:T(2,128)S(1)}, f32[2,256]{1,0:T(2,128)}, u32[]{:S(2)}) copy-start(f32[2,256]{1,0:T(2,128)} %param.11) | copy-start | bytes 6148
  51.9 0.7 %copy-start.4 = (f32[2,256]{1,0:T(2,128)S(1)}, f32[2,256]{1,0:T(2,128)}, u32[]{:S(2)}) copy-start(f32[2,256]{1,0:T(2,128)} %param.10) | copy-start | bytes 6148
  53.6 0.7 %copy-start.5 = (s32[2,256]{1,0:T(2,128)S(1)}, s32[2,256]{1,0:T(2,128)}, u32[]{:S(2)}) copy-start(s32[2,256]{1,0:T(2,128)} %param.14) | copy-start | bytes 6148

commit v15 on v14

--- a/solution.py
+++ b/solution.py
@@ -285,7 +285,7 @@
     slot_level = slot_obs % levels_count
     holder = slot_column // cols_dev
     local_col = slot_column % cols_dev
-    levels = jnp.take(ensemble, slot_level.reshape(-1), axis=1)
+    levels = ensemble.at[:, slot_level.reshape(-1)].get(mode="promise_in_bounds")
     retain = (slot_valid & (holder == sub_index)).reshape(-1)
     chosen = (jnp.arange(cols_dev, dtype=jnp.int32)[None, :] == local_col.reshape(-1, 1)) & retain[:, None]
     picked = jnp.sum(jnp.where(chosen[None, :, None, :], levels, 0.0), axis=3)
@@ -295,11 +295,9 @@
     q_rows = BATCHES * capacity // sub_count
     width = BANDS * members
     row_of = jnp.arange(BATCHES, dtype=jnp.int32)[:, None] * capacity + slot_rank
-    lines = jnp.take(
-        gathered.reshape(sub_count * slab_count, q_rows * width),
-        ((row_of // q_rows) * slab_count + owners).reshape(-1),
-        axis=0,
-    )
+    lines = gathered.reshape(sub_count * slab_count, q_rows * width).at[
+        ((row_of // q_rows) * slab_count + owners).reshape(-1)
+    ].get(mode="promise_in_bounds")
     part = (row_of % q_rows).reshape(-1, 1)
     flat_priors = lines[:, :width]
     for r in range(1, q_rows):
@@ -340,7 +338,7 @@
             ],
             axis=1,
         )
-        rows = jnp.take(table, pick(near_obs, batch_id), axis=0)
+        rows = table.at[pick(near_obs, batch_id)].get(mode="promise_in_bounds")
         ensemble = update_state(
             ensemble,
             col_blocks,

time: 66.4 us -> 65.4 us (0.985)
  no operation moved by 1% of the time
where the time goes in v15:
time: 65.4 us; the launch traced here: 65.2 us
  Pallas kernels  42.8 us (65%)
  local copies, waits for them, and re-layouts  9.37 us (14%)
  other arithmetic  7.53 us (12%)
  matrix products  4.34 us (7%)
  between operations  1.19 us (2%)
    pallas_call x1, Pallas kernels, gather_slots(): pl.pallas_call(functools.partial(gather_kernel, n_row), out_shape=jax.Sha...  42.8 us
    gather x1, local copies, waits for them, and re-layouts, per_device(): lines = gathered.reshape(sub_count * slab_count, q_rows * width).at[(row_...  3.53 us
    dot_general x2, matrix products, update_state(): jnp.einsum('blck,km->blmc', crossed * weights[:, None], increments, preci...  2.6 us

profile of v15, /device:TPU:1, one launch (start us, length us, event | category | flops | bytes accessed | tf_op | source)
XLA Modules:
  0.0 65.2 jit_solution(14937072479093132087)
XLA Ops:
  0.7 0.9 %copy.76 = s32[2,2,128]{1,2,0:T(8,128)S(1)} copy(s32[2,2,128]{2,1,0:T(2,128)} %bitcast.106) | data formatting | bytes 4096 | tf_op jit(solution)/shard_map/eq | solution.py:279
  1.6 0.4 fusion.26
  2.1 0.1 add_add_fusion
  2.3 0.2 fusion.27
  2.5 0.1 select_reduce_fusion.2
  2.7 0.1 reduce_sum.276
  2.8 0.2 iota_compare_fusion.1
  2.9 0.1 reduce_or.21
  3.0 0.1 fusion.62
  3.1 0.1 rem.177
  3.2 0.6 gather_fusion
  3.9 0.6 select_reduce_fusion
  4.5 0.7 %reshape_reshape.6.picked_ref = f32[4,640]{1,0:T(4,128)} reshape(f32[16,2,80]{2,1,0:T(2,128)S(1)} %select_reduce_fusion) | data formatting | bytes 20480 | tf_op jit(solution)/shard_map/reshape;reshape | solution.py:258
  5.2 42.8 %shard_map.86 = f32[4,4,2,16,640]{4,3,2,1,0:T(8,128)} custom-call(f32[4,640]{1,0:T(4,128)} %reshape_reshape.6.picked_ref), custom_call_target="tpu_custom_call" | custom-call | tf_op jit(solution)/shard_map/pallas_call | solution.py:241
  48.1 3.5 %gather_fusion.1 = f32[512,640]{1,0:T(8,128)S(1)} fusion(f32[512,640]{1,0:T(8,128)} %bitcast.91, s32[1024]{0:T(1024)S(1)} %pad_clamp_fusion.2), kind=kCustom, calls=%fused_computation.1 | custom fusion | bytes 2623488 | tf_op jit(solution)/shard_map/gather | solution.py:300
  51.7 0.1 fusion.75
  51.8 0.1 multiply_reduce_fusion.9
  51.9 0.9 %multiply_reduce_fusion.2 = (f32[512]{0:T(512)S(1)}, f32[512,160]{1,0:T(8,128)S(1)}) fusion(f32[512]{0:T(512)S(1)} %bitcast.113, f32[512,640]{1,0:T(8,128)S(1)} %gather_fusion.1, pred[512]{0:T(512)(128)(4,1)S(1)} %get-tuple-element.40, pred[512]{0:T(512)(128)(4,1)S(1)} %get-tuple-element.39, pred[512]{0:T(512)(128)(4,1)S(1)} %get-tuple-element.31), kind=kLoop, calls=%fused_computation.27 | loop fusion | flops 409088 | bytes 1644032 | tf_op jit(solution)/shard_map/reduce_sum | solution.py:46
  52.8 0.2 multiply_reduce_fusion.1
  53.0 0.1 copy.78
  53.2 0.1 copy.86
  53.5 0.1 multiply_reduce_fusion.10
  53.6 0.6 fusion.20
  54.2 0.4 convolution_multiply_fusion
  54.7 0.4 fusion.76
  55.1 0.1 copy.94
  55.3 0.2 copy.95
  55.4 0.8 %multiply_reduce_fusion = f32[2,256,160]{1,2,0:T(8,128)} fusion(f32[2,2]{1,0:T(2,128)S(1)} %get-tuple-element.50, f32[2,256,160]{1,2,0:T(8,128)S(1)} %copy.95), kind=kLoop, calls=%fused_computation.18 | loop fusion | flops 245760 | bytes 655376 | tf_op jit(solution)/shard_map/reduce_sum | solution.py:315
  56.3 0.1 copy.79
  56.5 0.1 copy.80
  56.6 0.1 copy.81
  56.7 0.1 copy.82
  56.9 0.2 pad_maximum_fusion.1
  57.1 0.1 broadcast_compare_fusion
  57.1 0.2 fusion.35
  57.3 0.2 and_reduce_fusion
  57.5 0.1 select_reduce_fusion.3
  57.6 0.1 reduce_sum.291
  57.7 0.6 gather_fusion.2
  58.3 0.2 fusion.61
  58.5 0.1 copy.88
  58.7 0.1 copy.87
  58.8 0.2 multiply_reduce_fusion.4
  59.0 0.2 multiply_add_fusion
  59.2 0.1 copy.89
  59.3 0.1 copy.90
  59.5 0.2 pad_maximum_fusion.2
  59.6 0.1 reduce_sum.304
  59.7 0.6 gather_fusion.3
  60.3 0.2 fusion.59
  60.5 0.1 fusion.51
  60.7 0.2 fusion.58
  60.9 0.1 gt.23
  60.9 0.1 fusion.37
  61.0 0.2 fusion.60
  61.2 0.1 gt.21
  61.3 0.1 fusion.36
  61.4 0.1 reshape.1545
  61.5 0.1 reduce_sum.292
  61.6 0.4 fusion.6
  62.0 0.8 %fusion.79 = (f32[2,15,128]{2,1,0:T(8,128)S(1)}, f32[2,15,80,128]{3,2,1,0:T(8,128)S(1)}) fusion(f32[2,15,80,128]{3,2,1,0:T(8,128)S(1)} %copy-done, f32[2,15,128,24]{2,3,1,0:T(8,128)S(1)} %fusion.6, f32[24,242]{1,0:T(8,128)S(1)} %gather_fusion.2), kind=kOutput, calls=%fused_computation.224 | convolution fusion | flops 44847360 | bytes 2853888 | tf_op jit(solution)/shard_map/blck,km->blmc/dot_general | solution.py:77
  62.9 0.1 reshape.1548
  63.0 0.4 fusion.9
  63.4 1.8 %fusion = f32[2,15,80,128]{3,2,1,0:T(8,128)} fusion(f32[2,15,80,128]{3,2,1,0:T(8,128)S(1)} %get-tuple-element.61, f32[2,15,128,24]{2,3,1,0:T(8,128)S(1)} %fusion.9, f32[24,242]{1,0:T(8,128)S(1)} %gather_fusion.3), kind=kOutput, calls=%fused_computation.5 | convolution fusion | flops 44544000 | bytes 2838528 | tf_op jit(solution)/shard_map/blck,km->blmc/dot_general | solution.py:77
  (64 shorter events, 0.8 us)
Async XLA Ops:
  0.6 1.6 %copy-start.1 = (s32[2,256,1]{1,2,0:T(1,128)S(1)}, s32[2,256,1]{1,2,0:T(1,128)}, u32[]{:S(2)}) copy-start(s32[2,256,1]{1,2,0:T(1,128)} %param.10) | copy-start | bytes 6148
  0.6 1.9 %copy-start.2 = (s32[2,256]{1,0:T(2,128)S(1)}, s32[2,256]{1,0:T(2,128)}, u32[]{:S(2)}) copy-start(s32[2,256]{1,0:T(2,128)} %param.11) | copy-start | bytes 6148
  0.6 2.6 %copy-start = (f32[2,15,80,128]{3,2,1,0:T(8,128)S(1)}, f32[2,15,80,128]{3,2,1,0:T(8,128)}, u32[]{:S(2)}) copy-start(f32[2,15,80,128]{3,2,1,0:T(8,128)} %param.7) | copy-start | bytes 3686404
  48.1 3.6 %copy-start.6 = (s32[2]{0:T(128)S(1)}, s32[2]{0:T(128)}, u32[]{:S(2)}) copy-start(s32[2]{0:T(128)} %param.13) | copy-start | bytes 28
  48.1 3.7 %copy-start.3 = (f32[2,256]{1,0:T(2,128)S(1)}, f32[2,256]{1,0:T(2,128)}, u32[]{:S(2)}) copy-start(f32[2,256]{1,0:T(2,128)} %param.9) | copy-start | bytes 6148
  48.1 3.6 %copy-start.4 = (f32[2,256]{1,0:T(2,128)S(1)}, f32[2,256]{1,0:T(2,128)}, u32[]{:S(2)}) copy-start(f32[2,256]{1,0:T(2,128)} %param.8) | copy-start | bytes 6148
  52.8 0.7 %copy-start.5 = (s32[2,256]{1,0:T(2,128)S(1)}, s32[2,256]{1,0:T(2,128)}, u32[]{:S(2)}) copy-start(s32[2,256]{1,0:T(2,128)} %param.12) | copy-start | bytes 6148

commit v16 on v15

--- a/solution.py
+++ b/solution.py
@@ -295,22 +295,26 @@
     q_rows = BATCHES * capacity // sub_count
     width = BANDS * members
     row_of = jnp.arange(BATCHES, dtype=jnp.int32)[:, None] * capacity + slot_rank
+    turns = batch_order[:, None] == jnp.arange(BATCHES, dtype=jnp.int32)[None, :]
+    first, second = turns[0], turns[1]
+    line_of = (row_of // q_rows) * slab_count + owners
+    part_of = row_of % q_rows
+    turn_line = jnp.stack([pick(line_of, turns[t]) for t in range(BATCHES)])
+    turn_part = jnp.stack([pick(part_of, turns[t]) for t in range(BATCHES)])
     lines = gathered.reshape(sub_count * slab_count, q_rows * width).at[
-        ((row_of // q_rows) * slab_count + owners).reshape(-1)
+        turn_line.reshape(-1)
     ].get(mode="promise_in_bounds")
-    part = (row_of % q_rows).reshape(-1, 1)
+    part = turn_part.reshape(-1, 1)
     flat_priors = lines[:, :width]
     for r in range(1, q_rows):
         flat_priors = jnp.where(part == r, lines[:, r * width : (r + 1) * width], flat_priors)
-    priors = flat_priors.reshape(BATCHES, -1, width)
-
-    turns = batch_order[:, None] == jnp.arange(BATCHES, dtype=jnp.int32)[None, :]
-    first, second = turns[0], turns[1]
-    y0 = pick(priors, first)
+    turn_priors = flat_priors.reshape(BATCHES, -1, width)
+
+    y0 = turn_priors[0]
     home0 = pick(obs_home, first)
     home1 = pick(obs_home, second)
     stats0 = obs_statistics(y0, pick(obs_value, first), pick(obs_var, first), members)
-    y1 = update_pool(pick(priors, second), home1, *stats0, home0, nblocks, decays)
+    y1 = update_pool(turn_priors[1], home1, *stats0, home0, nblocks, decays)
     stats1 = obs_statistics(y1, pick(obs_value, second), pick(obs_var, second), members)
     recorded = jnp.sum(
         jnp.stack([y0, y1])[:, None] * turns.astype(jnp.float32)[:, :, None, None], axis=0

time: 65.4 us -> 65.3 us (level)
    reduce_sum x2 -> x0, other arithmetic: 0.88 us -> none  [obs_statistics(): centre = jnp.mean(whole_obs, axis=1, keepdims=True)]
    select_n x1 -> x2, other arithmetic: 0.02 us -> 0.68 us  [the longest x1 0.67 us: per_device(): jnp.where(part == r, lines[:, r * width:(r + 1) * width], flat_priors)]
where the time goes in v16:
time: 65.3 us; the launch traced here: 65 us
  Pallas kernels  42.8 us (66%)
  local copies, waits for them, and re-layouts  9.65 us (15%)
  other arithmetic  7.07 us (11%)
  matrix products  4.34 us (7%)
  between operations  1.21 us (2%)
    pallas_call x1, Pallas kernels, gather_slots(): pl.pallas_call(functools.partial(gather_kernel, n_row), out_shape=jax.Sha...  42.8 us
    gather x1, local copies, waits for them, and re-layouts, per_device(): lines = gathered.reshape(sub_count * slab_count, q_rows * width).at[turn_...  3.52 us
    dot_general x2, matrix products, update_state(): jnp.einsum('blck,km->blmc', crossed * weights[:, None], increments, preci...  2.6 us

profile of v16, /device:TPU:1, one launch (start us, length us, event | category | flops | bytes accessed | tf_op | source)
XLA Modules:
  0.0 65.0 jit_solution(15403605561040002789)
XLA Ops:
  0.7 0.9 %copy.78 = s32[2,2,128]{1,2,0:T(8,128)S(1)} copy(s32[2,2,128]{2,1,0:T(2,128)} %bitcast.103) | data formatting | bytes 4096 | tf_op jit(solution)/shard_map/eq | solution.py:279
  1.6 0.4 fusion.26
  2.1 0.1 add_add_fusion
  2.3 0.2 fusion.27
  2.5 0.1 multiply_add_fusion.2
  2.7 0.1 multiply_reduce_fusion.12
  2.9 0.1 select_reduce_fusion.2
  3.0 0.1 reduce_sum.289
  3.1 0.2 iota_compare_fusion.1
  3.3 0.1 reduce_or.21
  3.4 0.1 fusion.62
  3.5 0.1 rem.159
  3.6 0.6 gather_fusion
  4.2 0.6 select_reduce_fusion
  4.9 0.7 %reshape_reshape.6.picked_ref = f32[4,640]{1,0:T(4,128)} reshape(f32[16,2,80]{2,1,0:T(2,128)S(1)} %select_reduce_fusion) | data formatting | bytes 20480 | tf_op jit(solution)/shard_map/reshape;reshape | solution.py:258
  5.6 42.8 %shard_map.86 = f32[4,4,2,16,640]{4,3,2,1,0:T(8,128)} custom-call(f32[4,640]{1,0:T(4,128)} %reshape_reshape.6.picked_ref), custom_call_target="tpu_custom_call" | custom-call | tf_op jit(solution)/shard_map/pallas_call | solution.py:241
  48.3 3.5 %gather_fusion.1 = f32[512,640]{1,0:T(8,128)S(1)} fusion(f32[512,640]{1,0:T(8,128)} %bitcast.90, s32[1024]{0:T(1024)S(1)} %pad_clamp_fusion.2), kind=kCustom, calls=%fused_computation.1 | custom fusion | bytes 2623488 | tf_op jit(solution)/shard_map/gather | solution.py:306
  51.9 0.7 %fusion.16 = f32[512,160]{1,0:T(8,128)S(1)} fusion(f32[512,640]{1,0:T(8,128)S(1)} %gather_fusion.1, pred[512]{0:T(512)(128)(4,1)S(1)} %eq.192, pred[512]{0:T(512)(128)(4,1)S(1)} %eq.190, pred[512]{0:T(512)(128)(4,1)S(1)} %eq.178), kind=kLoop, calls=%fused_computation.23 | loop fusion | flops 245760 | bytes 1639936 | tf_op jit(solution)/shard_map/jit(_where)/select_n | solution.py:310
  52.6 0.1 copy.80
  52.8 0.1 copy.81
  53.0 0.1 slice_bitcast_fusion.5
  53.1 0.3 copy-done.3
  53.5 0.1 multiply_reduce_fusion.6
  53.6 0.1 copy.88
  53.8 0.6 fusion.20
  54.4 0.4 convolution_multiply_fusion
  54.9 0.4 fusion.75
  55.3 0.1 copy.96
  55.5 0.2 copy.97
  55.6 0.8 %multiply_reduce_fusion = f32[2,256,160]{1,2,0:T(8,128)} fusion(f32[2,2]{1,0:T(2,128)S(1)} %get-tuple-element.58, f32[2,256,160]{1,2,0:T(8,128)S(1)} %copy.97), kind=kLoop, calls=%fused_computation.18 | loop fusion | flops 245760 | bytes 655376 | tf_op jit(solution)/shard_map/reduce_sum | solution.py:319
  56.5 0.1 copy.82
  56.6 0.1 copy.83
  56.7 0.1 copy.84
  56.9 0.2 pad_maximum_fusion.1
  57.1 0.1 broadcast_compare_fusion
  57.1 0.2 fusion.35
  57.3 0.2 and_reduce_fusion
  57.5 0.1 select_reduce_fusion.3
  57.6 0.1 reduce_sum.303
  57.7 0.6 gather_fusion.2
  58.3 0.1 copy.90
  58.5 0.1 copy.89
  58.6 0.2 multiply_reduce_fusion.1
  58.8 0.2 multiply_add_fusion
  59.0 0.1 copy.91
  59.1 0.1 copy.92
  59.3 0.2 pad_maximum_fusion.2
  59.5 0.1 reduce_sum.315
  59.6 0.6 gather_fusion.3
  60.2 0.2 fusion.59
  60.4 0.1 fusion.51
  60.5 0.2 fusion.58
  60.7 0.1 gt.23
  60.8 0.1 fusion.37
  60.9 0.2 fusion.60
  61.0 0.1 gt.21
  61.1 0.1 fusion.36
  61.2 0.1 reshape.1454
  61.3 0.1 reduce_sum.304
  61.4 0.4 fusion.6
  61.9 0.8 %fusion.77 = (f32[2,15,128]{2,1,0:T(8,128)S(1)}, f32[2,15,80,128]{3,2,1,0:T(8,128)S(1)}) fusion(f32[2,15,80,128]{3,2,1,0:T(8,128)S(1)} %copy-done, f32[2,15,128,24]{2,3,1,0:T(8,128)S(1)} %fusion.6, f32[24,242]{1,0:T(8,128)S(1)} %gather_fusion.2), kind=kOutput, calls=%fused_computation.227 | convolution fusion | flops 44847360 | bytes 2853888 | tf_op jit(solution)/shard_map/blck,km->blmc/dot_general | solution.py:77
  62.7 0.1 reshape.1456
  62.8 0.4 fusion.9
  63.2 1.8 %fusion = f32[2,15,80,128]{3,2,1,0:T(8,128)} fusion(f32[2,15,80,128]{3,2,1,0:T(8,128)S(1)} %get-tuple-element.68, f32[2,15,128,24]{2,3,1,0:T(8,128)S(1)} %fusion.9, f32[24,242]{1,0:T(8,128)S(1)} %gather_fusion.3), kind=kOutput, calls=%fused_computation.5 | convolution fusion | flops 44544000 | bytes 2838528 | tf_op jit(solution)/shard_map/blck,km->blmc/dot_general | solution.py:77
  (63 shorter events, 0.7 us)
Async XLA Ops:
  0.6 1.6 %copy-start.1 = (s32[2,256,1]{1,2,0:T(1,128)S(1)}, s32[2,256,1]{1,2,0:T(1,128)}, u32[]{:S(2)}) copy-start(s32[2,256,1]{1,2,0:T(1,128)} %param.10) | copy-start | bytes 6148
  0.6 1.9 %copy-start.2 = (s32[2,256]{1,0:T(2,128)S(1)}, s32[2,256]{1,0:T(2,128)}, u32[]{:S(2)}) copy-start(s32[2,256]{1,0:T(2,128)} %param.11) | copy-start | bytes 6148
  0.7 1.9 %copy-start.5 = (s32[2,256]{1,0:T(2,128)S(1)}, s32[2,256]{1,0:T(2,128)}, u32[]{:S(2)}) copy-start(s32[2,256]{1,0:T(2,128)} %param.12) | copy-start | bytes 6148
  0.7 2.0 %copy-start.6 = (s32[2]{0:T(128)S(1)}, s32[2]{0:T(128)}, u32[]{:S(2)}) copy-start(s32[2]{0:T(128)} %param.13) | copy-start | bytes 28
  0.7 2.9 %copy-start = (f32[2,15,80,128]{3,2,1,0:T(8,128)S(1)}, f32[2,15,80,128]{3,2,1,0:T(8,128)}, u32[]{:S(2)}) copy-start(f32[2,15,80,128]{3,2,1,0:T(8,128)} %param.7) | copy-start | bytes 3686404
  52.8 0.7 %copy-start.3 = (f32[2,256]{1,0:T(2,128)S(1)}, f32[2,256]{1,0:T(2,128)}, u32[]{:S(2)}) copy-start(f32[2,256]{1,0:T(2,128)} %param.9) | copy-start | bytes 6148
  52.8 0.7 %copy-start.4 = (f32[2,256]{1,0:T(2,128)S(1)}, f32[2,256]{1,0:T(2,128)}, u32[]{:S(2)}) copy-start(f32[2,256]{1,0:T(2,128)} %param.8) | copy-start | bytes 6148

commit v17 on v16

--- a/solution.py
+++ b/solution.py
@@ -316,9 +316,7 @@
     stats0 = obs_statistics(y0, pick(obs_value, first), pick(obs_var, first), members)
     y1 = update_pool(turn_priors[1], home1, *stats0, home0, nblocks, decays)
     stats1 = obs_statistics(y1, pick(obs_value, second), pick(obs_var, second), members)
-    recorded = jnp.sum(
-        jnp.stack([y0, y1])[:, None] * turns.astype(jnp.float32)[:, :, None, None], axis=0
-    )
+    recorded = jnp.where(first[:, None, None], y0[None], y1[None])
 
     col_blocks = ((slab_index * sub_count + sub_index) * cols_dev + jnp.arange(
         cols_dev, dtype=jnp.int32

time: 65.3 us -> 64.9 us (level)
    reduce_sum x1 -> x0, other arithmetic: 0.85 us -> none  [per_device(): jnp.sum(jnp.stack([y0, y1])[:, None] * turns.astype(jnp.float32)[:, :, No...]
    select_n x0 -> x1, other arithmetic: none -> 0.82 us  [per_device(): recorded = jnp.where(first[:, None, None], y0[None], y1[None])]
where the time goes in v17:
time: 64.9 us; the launch traced here: 64.6 us
  Pallas kernels  42.8 us (66%)
  local copies, waits for them, and re-layouts  9.35 us (14%)
  other arithmetic  7 us (11%)
  matrix products  4.34 us (7%)
  between operations  1.19 us (2%)
    pallas_call x1, Pallas kernels, gather_slots(): pl.pallas_call(functools.partial(gather_kernel, n_row), out_shape=jax.Sha...  42.8 us
    gather x1, local copies, waits for them, and re-layouts, per_device(): lines = gathered.reshape(sub_count * slab_count, q_rows * width).at[turn_...  3.52 us
    dot_general x2, matrix products, update_state(): jnp.einsum('blck,km->blmc', crossed * weights[:, None], increments, preci...  2.59 us

profile of v17, /device:TPU:1, one launch (start us, length us, event | category | flops | bytes accessed | tf_op | source)
XLA Modules:
  0.0 64.6 jit_solution(12271029584543208328)
XLA Ops:
  0.7 0.9 %copy.77 = s32[2,2,128]{1,2,0:T(8,128)S(1)} copy(s32[2,2,128]{2,1,0:T(2,128)} %bitcast.103) | data formatting | bytes 4096 | tf_op jit(solution)/shard_map/eq | solution.py:279
  1.6 0.4 fusion.26
  2.1 0.1 add_add_fusion
  2.3 0.2 fusion.27
  2.5 0.1 multiply_add_fusion.2
  2.6 0.1 iota_compare_fusion.3
  2.7 0.1 multiply_reduce_fusion.11
  2.9 0.1 select_reduce_fusion.2
  3.0 0.1 reduce_sum.280
  3.1 0.2 iota_compare_fusion.1
  3.3 0.1 reduce_or.21
  3.4 0.1 fusion.62
  3.5 0.1 rem.159
  3.6 0.6 gather_fusion
  4.2 0.6 select_reduce_fusion
  4.9 0.7 %reshape_reshape.6.picked_ref = f32[4,640]{1,0:T(4,128)} reshape(f32[16,2,80]{2,1,0:T(2,128)S(1)} %select_reduce_fusion) | data formatting | bytes 20480 | tf_op jit(solution)/shard_map/reshape;reshape | solution.py:258
  5.6 42.8 %shard_map.86 = f32[4,4,2,16,640]{4,3,2,1,0:T(8,128)} custom-call(f32[4,640]{1,0:T(4,128)} %reshape_reshape.6.picked_ref), custom_call_target="tpu_custom_call" | custom-call | tf_op jit(solution)/shard_map/pallas_call | solution.py:241
  48.3 3.5 %gather_fusion.1 = f32[512,640]{1,0:T(8,128)S(1)} fusion(f32[512,640]{1,0:T(8,128)} %bitcast.90, s32[1024]{0:T(1024)S(1)} %pad_clamp_fusion.2), kind=kCustom, calls=%fused_computation.1 | custom fusion | bytes 2623488 | tf_op jit(solution)/shard_map/gather | solution.py:306
  51.9 0.7 %fusion.16 = f32[512,160]{1,0:T(8,128)S(1)} fusion(f32[512,640]{1,0:T(8,128)S(1)} %gather_fusion.1, pred[512]{0:T(512)(128)(4,1)S(1)} %eq.188, pred[512]{0:T(512)(128)(4,1)S(1)} %eq.186, pred[512]{0:T(512)(128)(4,1)S(1)} %eq.174), kind=kLoop, calls=%fused_computation.22 | loop fusion | flops 245760 | bytes 1639936 | tf_op jit(solution)/shard_map/jit(_where)/select_n | solution.py:310
  52.6 0.1 copy.79
  52.8 0.1 copy.80
  53.0 0.1 fusion.76
  53.1 0.3 copy-done.3
  53.4 0.0 copy-done.4
  53.5 0.1 multiply_reduce_fusion.5
  53.6 0.1 copy.87
  53.8 0.6 %fusion.20 = (f32[1,256,256]{2,1,0:T(8,128)S(1)}, f32[1,256,256]{2,1,0:T(8,128)S(1)}) fusion(s32[256]{0:T(256)S(1)} %get-tuple-element.21, s32[256]{0:T(256)S(1)} %get-tuple-element.22), kind=kLoop, calls=%fused_computation.33 | loop fusion | flops 4128768 | bytes 526336 | tf_op jit(solution)/shard_map/jit(_where)/select_n | solution.py:40
  54.4 0.4 convolution_multiply_fusion
  54.9 0.4 fusion.74
  55.3 0.8 %broadcast_select_fusion = f32[2,256,160]{1,2,0:T(8,128)} fusion(f32[256,160]{0,1:T(8,128)S(1)} %bitcast.91, f32[256,160]{0,1:T(8,128)S(1)} %copy.79, pred[2]{0:T(512)(128)(4,1)S(1)} %get-tuple-element.57), kind=kLoop, calls=%fused_computation.51 | loop fusion | flops 81920 | bytes 655362 | tf_op jit(solution)/shard_map/jit(_where)/select_n | solution.py:319
  56.1 0.1 copy.81
  56.2 0.1 copy.82
  56.3 0.1 copy.83
  56.5 0.2 pad_maximum_fusion
  56.7 0.1 broadcast_compare_fusion
  56.7 0.2 fusion.35
  56.9 0.2 and_reduce_fusion
  57.1 0.1 select_reduce_fusion.3
  57.2 0.1 reduce_sum.294
  57.3 0.6 gather_fusion.2
  57.9 0.1 copy.89
  58.1 0.1 copy.88
  58.2 0.2 multiply_reduce_fusion
  58.4 0.2 multiply_add_fusion
  58.6 0.1 copy.90
  58.8 0.1 copy.91
  58.9 0.2 pad_maximum_fusion.1
  59.1 0.1 reduce_sum.306
  59.2 0.6 gather_fusion.3
  59.8 0.2 fusion.59
  60.0 0.1 fusion.51
  60.1 0.2 fusion.58
  60.3 0.1 gt.23
  60.4 0.1 fusion.37
  60.5 0.2 fusion.60
  60.6 0.1 gt.21
  60.7 0.1 fusion.36
  60.8 0.1 reshape.1432
  60.9 0.1 reduce_sum.295
  61.0 0.5 fusion.6
  61.5 0.8 %fusion.77 = (f32[2,15,128]{2,1,0:T(8,128)S(1)}, f32[2,15,80,128]{3,2,1,0:T(8,128)S(1)}) fusion(f32[2,15,80,128]{3,2,1,0:T(8,128)S(1)} %copy-done, f32[2,15,128,24]{2,3,1,0:T(8,128)S(1)} %fusion.6, f32[24,242]{1,0:T(8,128)S(1)} %gather_fusion.2), kind=kOutput, calls=%fused_computation.224 | convolution fusion | flops 44847360 | bytes 2853888 | tf_op jit(solution)/shard_map/blck,km->blmc/dot_general | solution.py:77
  62.3 0.1 reshape.1434
  62.4 0.5 fusion.9
  62.8 1.8 %fusion = f32[2,15,80,128]{3,2,1,0:T(8,128)} fusion(f32[2,15,80,128]{3,2,1,0:T(8,128)S(1)} %get-tuple-element.66, f32[2,15,128,24]{2,3,1,0:T(8,128)S(1)} %fusion.9, f32[24,242]{1,0:T(8,128)S(1)} %gather_fusion.3), kind=kOutput, calls=%fused_computation.5 | convolution fusion | flops 44544000 | bytes 2838528 | tf_op jit(solution)/shard_map/blck,km->blmc/dot_general | solution.py:77
  (60 shorter events, 0.6 us)
Async XLA Ops:
  0.6 1.6 %copy-start.1 = (s32[2,256,1]{1,2,0:T(1,128)S(1)}, s32[2,256,1]{1,2,0:T(1,128)}, u32[]{:S(2)}) copy-start(s32[2,256,1]{1,2,0:T(1,128)} %param.10) | copy-start | bytes 6148
  0.6 1.9 %copy-start.2 = (s32[2,256]{1,0:T(2,128)S(1)}, s32[2,256]{1,0:T(2,128)}, u32[]{:S(2)}) copy-start(s32[2,256]{1,0:T(2,128)} %param.11) | copy-start | bytes 6148
  0.7 1.9 %copy-start.5 = (s32[2,256]{1,0:T(2,128)S(1)}, s32[2,256]{1,0:T(2,128)}, u32[]{:S(2)}) copy-start(s32[2,256]{1,0:T(2,128)} %param.12) | copy-start | bytes 6148
  0.7 2.0 %copy-start.6 = (s32[2]{0:T(128)S(1)}, s32[2]{0:T(128)}, u32[]{:S(2)}) copy-start(s32[2]{0:T(128)} %param.13) | copy-start | bytes 28
  0.7 2.9 %copy-start = (f32[2,15,80,128]{3,2,1,0:T(8,128)S(1)}, f32[2,15,80,128]{3,2,1,0:T(8,128)}, u32[]{:S(2)}) copy-start(f32[2,15,80,128]{3,2,1,0:T(8,128)} %param.7) | copy-start | bytes 3686404
  52.8 0.7 %copy-start.3 = (f32[2,256]{1,0:T(2,128)S(1)}, f32[2,256]{1,0:T(2,128)}, u32[]{:S(2)}) copy-start(f32[2,256]{1,0:T(2,128)} %param.9) | copy-start | bytes 6148
  52.8 0.7 %copy-start.4 = (f32[2,256]{1,0:T(2,128)S(1)}, f32[2,256]{1,0:T(2,128)}, u32[]{:S(2)}) copy-start(f32[2,256]{1,0:T(2,128)} %param.8) | copy-start | bytes 6148
